TPU v7x, 512 devices: a whole 4x8x8 slice. The times are simulated.
512 devices in a mesh: comp: 8 (over y), pts: 64 (over x, z, core).
Axes of the slice: x: 4, y: 8, z: 8, core: 2. Of those that a mesh axis runs over, the one named last changes fastest.
Arguments:
- spectrum: float32 [1296, 65536], P('comp', 'pts'), may hold values from 0.05 to 2
- courant: float32 [1296], P('comp'), may hold values from -0.9 to 0.9
- growth: float32 [1296], replicated, may hold values from 0 to 0.4
- quad_a: bfloat16 [640, 1296], replicated, may hold values from -0.15625 to 0.15625
- quad_b: bfloat16 [640, 1296], replicated, may hold values from -0.15625 to 0.15625
- sea_mask: int32 [65536], P('pts'), may hold values 0 or 1
- nest_counts: int32 [64], replicated, may hold values from 1 to 192, 6144 in all
- nest_offsets: int32 [6144], replicated, may hold values from 0 to 1023
Outputs:
- final_spectrum: float32 [1296, 65536], P('comp', 'pts')
- nest_boundary: float32 [1296, 6144], P('comp', 'pts')
Inputs may be any that keep to these rules, and one draw needn't show every extreme that they name: nest_counts sum to 6144; the entries of block o are the consecutive entries after those of blocks before it; some block supplies exactly 192.
All inputs are finite; a program needn't handle non-finite values. No bound on the sum of `sea_mask` on one device may be relied on, other than what follows from the above.
Results may differ from a plain program's by a relative error of at most 0.0028.
Values sent between devices are 32-bit elements; how exact they have to be, the bound alone decides.
No kernel may reach another device: no remote copies, remote signals or barrier semaphores. Data moves between devices by JAX's collectives and lax.ppermute only.
A program may use at most 64 MiB of HBM per device.

v0:
```python
import jax
import jax.numpy as jnp
from jax import lax
from jax.sharding import PartitionSpec as P

STEPS = 2


dissipation = 0.5


def with_halo(array, sides, width):
    for axis, dim in sides:
        count, length = (lax.axis_size(axis), array.shape[dim])
        up = [(i, (i + 1) % count) for i in range(count - 1)]
        down = [(j, i) for i, j in up]
        last = lax.slice_in_dim(array, length - width, length, axis=dim)
        first = lax.slice_in_dim(array, 0, width, axis=dim)
        before = lax.ppermute(last, axis, up)
        after = lax.ppermute(first, axis, down)
        array = jnp.concatenate([before, array, after], axis=dim)
    return array


def propagate(field, courant, sea):
    padded = with_halo(field, (("pts", 1),), 1)
    upwind = jnp.where(courant[:, None] > 0, padded[:, :-2], padded[:, 2:])
    speed = jnp.abs(courant)[:, None]
    return ((1.0 - speed) * field + speed * upwind) * sea[None, :]


def source(moved, quad_a, quad_b, growth):
    rounded = moved.astype(jnp.bfloat16)
    left = jnp.dot(quad_a, rounded, preferred_element_type=jnp.float32)
    right = jnp.dot(quad_b, rounded, preferred_element_type=jnp.float32)
    pairs = (left * right).astype(jnp.bfloat16)
    transfer = lax.dot_general(
        quad_a, pairs, (((0,), (0,)), ((), ())), preferred_element_type=jnp.float32
    )
    spread = jnp.sqrt(jnp.mean(moved * moved, axis=0) + 1e-06)
    return (moved + growth[:, None] * moved + transfer) / (1.0 + dissipation * spread)[None, :]


def entry_of(index_b, first_count, boundary):
    first = (index_b + first_count) % boundary
    second = index_b - boundary // 2
    return jnp.where(index_b < boundary // 2, first, second)


def per_device(spectrum, courant, growth, quad_a, quad_b, sea_mask, nest_counts, nest_offsets):
    sea = sea_mask.astype(jnp.float32)
    field = spectrum
    for step in range(STEPS):
        moved = propagate(field, courant, sea)
        whole = lax.all_to_all(moved, "comp", split_axis=1, concat_axis=0, tiled=True)
        updated = source(whole, quad_a, quad_b, growth)
        field = lax.all_to_all(updated, "comp", split_axis=0, concat_axis=1, tiled=True)
    block = lax.axis_index("pts")
    boundary = nest_offsets.shape[0]
    ends = jnp.cumsum(nest_counts)
    index_b = jnp.arange(boundary, dtype=jnp.int32)
    entries = entry_of(index_b, ends[0], boundary)
    owner = jnp.sum((ends[None, :] <= entries[:, None]).astype(jnp.int32), axis=1)
    offsets = jnp.take(nest_offsets, entries)
    picked = jnp.take(field, offsets, axis=1) * (owner == block).astype(jnp.float32)[None, :]
    nest = lax.psum_scatter(picked, "pts", scatter_dimension=1, tiled=True)
    return (field, nest)


def solution(mesh):
    return jax.shard_map(
        per_device,
        mesh=mesh,
        in_specs=(P("comp", "pts"), P("comp"), P(), P(), P(), P("pts"), P(), P()),
        out_specs=(P("comp", "pts"), P("comp", "pts")),
        check_vma=False,
    )
```

profile of v0, /device:TPU:1, one launch (start us, length us, event | category | flops | bytes accessed | tf_op | source)
XLA Modules:
  0.0 350.6 jit_solution(4576457664623271180)
XLA Ops:
  7.2 0.0 copy-start
  7.2 1.1 fusion.27
  8.3 5.4 %collective-permute-start = (f32[162,1]{1,0:T(8,128)S(1)}, f32[162,1]{1,0:T(8,128)S(1)}, u32[]{:S(2)}, u32[]{:S(2)}) collective-permute-start(f32[162,1]{1,0:T(8,128)S(1)} %get-tuple-element.12), channel_id=1, source_target_pairs={{0,1},{1,2},{2,3},{3,4},{4,5},{5,6},{6,7},{7,8},{8,9},{9,10},{10,1... | collective-permute-start | bytes 1952 | tf_op jit(solution)/shard_map/ppermute | solution.py:19
  13.7 4.7 %collective-permute-start.1 = (f32[162,1]{1,0:T(8,128)S(1)}, f32[162,1]{1,0:T(8,128)S(1)}, u32[]{:S(2)}, u32[]{:S(2)}) collective-permute-start(f32[162,1]{1,0:T(8,128)S(1)} %get-tuple-element.13), channel_id=1, source_target_pairs={{1,0},{2,1},{3,2},{4,3},{5,4},{6,5},{7,6},{8,7},{9,8},{10,9},{11,1... | collective-permute-start | bytes 1952 | tf_op jit(solution)/shard_map/ppermute | solution.py:20
  18.4 0.7 broadcast_subtract_fusion
  19.1 0.7 broadcast_compare_fusion
  19.8 0.7 convert_element_type.27
  20.4 0.0 collective-permute-done
  20.4 0.0 collective-permute-done.1
  20.4 2.2 fusion.13
  22.7 0.1 copy.37
  22.9 0.1 copy.30
  23.0 25.1 %all_to_all.76 = f32[162,8,128]{2,0,1:T(8,128)S(1)} all-to-all(f32[162,8,128]{2,0,1:T(8,128)S(1)} %copy.30), channel_id=1, replica_groups=mesh['comp'=8,'pts'=64] {'comp'}, dimensions={1} | all-to-all | bytes 1327104 | tf_op jit(solution)/shard_map/all_to_all | solution.py:55
  48.1 0.0 copy-start.3
  48.1 0.2 multiply_reduce_fusion.1
  48.3 0.0 copy-done
  48.4 0.5 fusion.20
  48.9 0.0 copy-done.3
  48.9 2.6 fusion.3
  51.6 23.3 %all_to_all.77 = f32[8,162,128]{2,1,0:T(8,128)S(1)} all-to-all(f32[8,162,128]{2,1,0:T(8,128)S(1)} %all_to_all.60), channel_id=1, replica_groups=mesh['comp'=8,'pts'=64] {'comp'}, dimensions={0} | all-to-all | bytes 1327104 | tf_op jit(solution)/shard_map/all_to_all | solution.py:57
  74.8 0.1 copy.31
  75.0 0.1 copy.38
  75.1 0.1 fusion.26
  75.2 5.4 %collective-permute-start.2 = (f32[162,1]{1,0:T(8,128)S(1)}, f32[162,1]{1,0:T(8,128)S(1)}, u32[]{:S(2)}, u32[]{:S(2)}) collective-permute-start(f32[162,1]{1,0:T(8,128)S(1)} %get-tuple-element.10), channel_id=1, source_target_pairs={{0,1},{1,2},{2,3},{3,4},{4,5},{5,6},{6,7},{7,8},{8,9},{9,10},{10,1... | collective-permute-start | bytes 1952 | tf_op jit(solution)/shard_map/ppermute | solution.py:19
  80.6 1.9 collective-permute-start.3
  82.5 0.0 collective-permute-done.2
  82.5 3.9 %collective-permute-done.3 = f32[162,1]{1,0:T(8,128)S(1)} collective-permute-done((f32[162,1]{1,0:T(8,128)S(1)}, f32[162,1]{1,0:T(8,128)S(1)}, u32[]{:S(2)}, u32[]{:S(2)}) %collective-permute-start.3) | collective-permute-done | bytes 680 | tf_op jit(solution)/shard_map/ppermute | solution.py:20
  86.4 0.5 fusion.9
  87.0 0.1 copy.39
  87.1 0.0 copy-start.2
  87.2 0.0 copy-start.1
  87.2 1.0 copy.32
  88.1 3.5 %all-to-all-start.2 = ((f32[162,8,128]{2,0,1:T(8,128)}), f32[162,8,128]{2,0,1:T(8,128)S(1)}, u32[]{:S(2)}, u32[]{:S(2)}) async-start(f32[162,8,128]{2,0,1:T(8,128)} %copy.32), calls=%async_computation.2 | async-start | bytes 1376256 | tf_op jit(solution)/shard_map/all_to_all | solution.py:55
  91.7 0.0 copy-done.2
  91.7 0.1 copy.34
  91.8 0.1 reduce-window.4
  91.9 0.5 slice.47
  92.4 0.7 compare_select_fusion.1
  93.1 0.0 copy-done.1
  93.2 34.3 %gather_fusion = s32[6144]{0:T(1024)S(1)} fusion(s32[6144]{0:T(1024)S(1)} %copy-done.1, s32[6144]{0:T(1024)S(1)} %broadcast_clamp_fusion.1), kind=kCustom, calls=%fused_computation | custom fusion | bytes 73728 | tf_op jit(solution)/shard_map/jit(_take)/gather | solution.py:64
  127.4 0.0 all-to-all-done.2
  127.5 0.5 fusion.16
  128.0 0.2 multiply_reduce_fusion
  128.2 2.6 fusion.1
  130.8 0.9 all_to_all.68
  131.7 6.6 %all-to-all-start.3 = ((f32[8,162,128]{2,1,0:T(8,128)}), f32[8,162,128]{2,1,0:T(8,128)S(1)}, u32[]{:S(2)}, u32[]{:S(2)}) async-start(f32[8,162,128]{2,1,0:T(8,128)} %all_to_all.68), calls=%async_computation.3 | async-start | bytes 1376256 | tf_op jit(solution)/shard_map/all_to_all | solution.py:57
  138.3 0.0 reduce-scatter.2.cloned.1.call-start
  138.3 0.7 compare_select_fusion
  139.1 0.1 reduce.2
  139.2 0.7 fusion.22
  139.9 0.3 convert_reduce_fusion
  140.2 0.7 compare_convert_fusion
  140.8 17.3 %all-to-all-done.3 = f32[8,162,128]{2,1,0:T(8,128)S(1)} async-done(((f32[8,162,128]{2,1,0:T(8,128)}), f32[8,162,128]{2,1,0:T(8,128)S(1)}, u32[]{:S(2)}, u32[]{:S(2)}) %all-to-all-start.3) | async-done | bytes 663584 | tf_op jit(solution)/shard_map/all_to_all | solution.py:57
  158.1 0.3 copy.33
  158.4 23.7 %gather_fusion.1 = f32[6144,162]{1,0:T(8,128)} fusion(f32[162,1024]{0,1:T(8,128)S(1)} %bitcast.41, s32[6144]{0:T(1024)S(1)} %broadcast_clamp_fusion), kind=kCustom, calls=%fused_computation.1 | custom fusion | bytes 7987200 | tf_op jit(solution)/shard_map/jit(_take)/gather | solution.py:65
  182.2 7.6 %multiply_bitcast_fusion = f32[162,6144]{0,1:T(8,128)} fusion(f32[6144,162]{1,0:T(8,128)} %gather_fusion.1, f32[6144]{0:T(1024)S(1)} %get-tuple-element.16, pred[6144]{0:T(1024)(128)(4,1)S(1)} %get-tuple-element.17), kind=kLoop, calls=%fused_computation.2 | loop fusion | flops 1990656 | bytes 7993344 | tf_op jit(solution)/shard_map/mul | solution.py:65
  189.7 0.0 reduce-scatter.2.cloned.1.call-update
  189.8 1.2 copy.35
  190.9 151.2 %reduce-scatter.2.cloned.1.call-done = f32[162,96]{0,1:T(8,128)} async-done(((f32[162,6144]{0,1:T(8,128)}), f32[162,96]{0,1:T(8,128)}) %reduce-scatter.2.cloned.1.call-update) | async-done | bytes 62224 | tf_op jit(solution)/shard_map/reduce_scatter | solution.py:66
  342.1 1.6 copy.36
  (10 shorter events, 0.3 us)
Async XLA Ops:
  7.2 41.2 %copy-start = (bf16[640,1296]{0,1:T(8,128)(2,1)S(1)}, bf16[640,1296]{0,1:T(8,128)(2,1)}, u32[]{:S(2)}) copy-start(bf16[640,1296]{0,1:T(8,128)(2,1)} %param.11) | copy-start | bytes 4976644
  8.3 12.1 %collective-permute-start = (f32[162,1]{1,0:T(8,128)S(1)}, f32[162,1]{1,0:T(8,128)S(1)}, u32[]{:S(2)}, u32[]{:S(2)}) collective-permute-start(f32[162,1]{1,0:T(8,128)S(1)} %get-tuple-element.12), channel_id=1, source_target_pairs={{0,1},{1,2},{2,3},{3,4},{4,5},{5,6},{6,7},{7,8},{8,9},{9,10},{10,1... | collective-permute-start | bytes 1952 | tf_op jit(solution)/shard_map/ppermute | solution.py:19
  13.7 6.7 %collective-permute-start.1 = (f32[162,1]{1,0:T(8,128)S(1)}, f32[162,1]{1,0:T(8,128)S(1)}, u32[]{:S(2)}, u32[]{:S(2)}) collective-permute-start(f32[162,1]{1,0:T(8,128)S(1)} %get-tuple-element.13), channel_id=1, source_target_pairs={{1,0},{2,1},{3,2},{4,3},{5,4},{6,5},{7,6},{8,7},{9,8},{10,9},{11,1... | collective-permute-start | bytes 1952 | tf_op jit(solution)/shard_map/ppermute | solution.py:20
  48.1 0.7 copy-start.3
  75.2 7.3 %collective-permute-start.2 = (f32[162,1]{1,0:T(8,128)S(1)}, f32[162,1]{1,0:T(8,128)S(1)}, u32[]{:S(2)}, u32[]{:S(2)}) collective-permute-start(f32[162,1]{1,0:T(8,128)S(1)} %get-tuple-element.10), channel_id=1, source_target_pairs={{0,1},{1,2},{2,3},{3,4},{4,5},{5,6},{6,7},{7,8},{8,9},{9,10},{10,1... | collective-permute-start | bytes 1952 | tf_op jit(solution)/shard_map/ppermute | solution.py:19
  80.6 5.8 %collective-permute-start.3 = (f32[162,1]{1,0:T(8,128)S(1)}, f32[162,1]{1,0:T(8,128)S(1)}, u32[]{:S(2)}, u32[]{:S(2)}) collective-permute-start(f32[162,1]{1,0:T(8,128)S(1)} %get-tuple-element.11), channel_id=1, source_target_pairs={{1,0},{2,1},{3,2},{4,3},{5,4},{6,5},{7,6},{8,7},{9,8},{10,9},{11,1... | collective-permute-start | bytes 1952 | tf_op jit(solution)/shard_map/ppermute | solution.py:20
  87.1 4.5 %copy-start.2 = (s32[64]{0:T(128)S(1)}, s32[64]{0:T(128)}, u32[]{:S(2)}) copy-start(s32[64]{0:T(128)} %param.14) | copy-start | bytes 772
  87.2 6.0 %copy-start.1 = (s32[6144]{0:T(1024)S(1)}, s32[6144]{0:T(1024)}, u32[]{:S(2)}) copy-start(s32[6144]{0:T(1024)} %param.15) | copy-start | bytes 73732
  88.1 39.3 %all-to-all-start.2 = ((f32[162,8,128]{2,0,1:T(8,128)}), f32[162,8,128]{2,0,1:T(8,128)S(1)}, u32[]{:S(2)}, u32[]{:S(2)}) async-start(f32[162,8,128]{2,0,1:T(8,128)} %copy.32), calls=%async_computation.2 | async-start | bytes 1376256 | tf_op jit(solution)/shard_map/all_to_all | solution.py:55
  131.7 26.4 %all-to-all-start.3 = ((f32[8,162,128]{2,1,0:T(8,128)}), f32[8,162,128]{2,1,0:T(8,128)S(1)}, u32[]{:S(2)}, u32[]{:S(2)}) async-start(f32[8,162,128]{2,1,0:T(8,128)} %all_to_all.68), calls=%async_computation.3 | async-start | bytes 1376256 | tf_op jit(solution)/shard_map/all_to_all | solution.py:57
  138.3 203.8 %reduce-scatter.2.cloned.1.call-start = ((), (), s32[]{:S(2)}) async-start(), calls=%async_computation.5 | async-start | bytes 6389760 | tf_op jit(solution)/shard_map/reduce_scatter | solution.py:66
Sparse Core Ops, SparseCore 0:
  189.9 152.1 reduce-scatter.1
where the time goes:
time: 356 us; the launch traced here: 351 us
  waiting for transfers between devices  172 us (48%)
  local copies, waits for them, and re-layouts  65.8 us (18%)
  blocking collectives  48.3 us (14%)
  starting transfers between devices  27.5 us (8%)
  other arithmetic  16.1 us (5%)
  between operations  14.3 us (4%)
  matrix products  6.24 us (2%)
    reduce_scatter x1, waiting for transfers between devices, per_device(): nest = lax.psum_scatter(picked, 'pts', scatter_dimension=1, tiled=True)  151 us
    gather x1, local copies, waits for them, and re-layouts, per_device(): offsets = jnp.take(nest_offsets, entries)  34.3 us
    all_to_all x1, blocking collectives, per_device(): lax.all_to_all(moved, 'comp', split_axis=1, concat_axis=0, tiled=True)  25.1 us
    gather x1, local copies, waits for them, and re-layouts, per_device(): jnp.take(field, offsets, axis=1)  23.7 us
    all_to_all x1, blocking collectives, per_device(): lax.all_to_all(updated, 'comp', split_axis=0, concat_axis=1, tiled=True)  23.3 us
    all_to_all x1, waiting for transfers between devices, per_device(): lax.all_to_all(updated, 'comp', split_axis=0, concat_axis=1, tiled=True)  17.3 us
    ppermute x2, starting transfers between devices, with_halo(): before = lax.ppermute(last, axis, up)  10.7 us
    mul x1, other arithmetic, per_device(): jnp.take(field, offsets, axis=1)  7.59 us
  transfers between devices with their start and end apart: 7, of which 3 were waited for; matrix products, arithmetic and copies ran while one was open for 12% of the time, Pallas kernels for 0%

commit v1 on v0

v1 whole, which is shorter than its diff:
```python
import functools

import jax
import jax.numpy as jnp
from jax import lax
from jax.experimental import pallas as pl
from jax.experimental.pallas import tpu as pltpu
from jax.sharding import PartitionSpec as P

STEPS = 2
LANES = 128
NB_BLOCK = 192
DISSIPATION = 0.5

F32 = jnp.float32
BF16 = jnp.bfloat16
VMEM = pl.BlockSpec(memory_space=pltpu.VMEM)
SMEM = pl.BlockSpec(memory_space=pltpu.SMEM)


def call(body, out_shape, n_in, smem=(), cost=None, scratch=()):
    specs = [SMEM if i in smem else VMEM for i in range(n_in)]
    outs = VMEM if not isinstance(out_shape, (tuple, list)) else tuple(VMEM for _ in out_shape)
    flops, bytes_accessed = cost or (1_000_000, 1_000_000)
    return pl.pallas_call(
        body,
        out_shape=out_shape,
        in_specs=specs,
        out_specs=outs,
        scratch_shapes=list(scratch),
        cost_estimate=pl.CostEstimate(flops=flops, bytes_accessed=bytes_accessed, transcendentals=0),
    )


def iota(shape, axis):
    return lax.broadcasted_iota(jnp.int32, shape, axis)


def split3(value):
    high = value.astype(BF16)
    rest = value - high.astype(F32)
    middle = rest.astype(BF16)
    low = (rest - middle.astype(F32)).astype(BF16)
    return high, middle, low


def exact_dot(value, chosen, dims):
    high, middle, low = (lax.dot_general(term, chosen, (dims, ((), ())), preferred_element_type=F32) for term in split3(value))
    return (high + middle) + low


def exact_pick(chosen, value):
    high, middle, low = (lax.dot_general(chosen, term, (((1,), (0,)), ((), ())), preferred_element_type=F32) for term in split3(value))
    return (high + middle) + low


def edges_body(field_ref, sea_ref, up_ref, down_ref):
    comps, points = field_ref.shape
    padded = up_ref.shape[1]
    for ref, start, order in ((up_ref, points - LANES, (LANES - 1, LANES - 2)), (down_ref, 0, (0, 1))):
        tile = field_ref[:, start:start + LANES]
        tile = jnp.concatenate([tile, jnp.zeros((padded - comps, LANES), F32)], axis=0)
        turned = tile.T
        for row, lane in enumerate(order):
            ref[row:row + 1, :] = turned[lane:lane + 1, :]
        sea = sea_ref[0:1, start + order[0]:start + order[0] + 1].astype(F32)
        ref[2:3, :] = jnp.broadcast_to(sea, (1, padded))
        ref[3:8, :] = jnp.zeros((5, padded), F32)


def pack_body(field_ref, sea_ref, courant_ref, before_ref, after_ref, out_ref):
    comps, points = field_ref.shape
    chunks = points // LANES
    padded = before_ref.shape[1]
    rows = jnp.concatenate(
        [before_ref[0:3, :], after_ref[0:3, :], jnp.concatenate([courant_ref[...], jnp.zeros((1, padded - comps), F32)], axis=1), jnp.zeros((1, padded), F32)],
        axis=0,
    )
    columns = rows.T[:comps, :]

    def wide(at):
        return jnp.broadcast_to(columns[:, at:at + 1], (comps, LANES))

    near_before, far_before, sea_before = wide(0), wide(1), wide(2)
    near_after, far_after, sea_after = wide(3), wide(4), wide(5)
    courant = wide(6)
    speed = jnp.abs(courant)
    stay = 1.0 - speed
    forward = courant > 0
    lane = iota((comps, LANES), 1)

    tiles = [field_ref[:, k * LANES:(k + 1) * LANES] for k in range(chunks)]
    moved = []
    for k in range(chunks):
        left_edge = near_before if k == 0 else jnp.broadcast_to(tiles[k - 1][:, LANES - 1:LANES], (comps, LANES))
        right_edge = near_after if k == chunks - 1 else jnp.broadcast_to(tiles[k + 1][:, 0:1], (comps, LANES))
        left = jnp.where(lane == 0, left_edge, pltpu.roll(tiles[k], 1, 1))
        right = jnp.where(lane == LANES - 1, right_edge, pltpu.roll(tiles[k], LANES - 1, 1))
        sea = sea_ref[0:1, k * LANES:(k + 1) * LANES].astype(F32)
        value = (stay * tiles[k] + speed * jnp.where(forward, left, right)) * sea
        out_ref[k, 0:comps, :] = value
        moved.append(value)

    first = jnp.broadcast_to(tiles[0][:, 0:1], (comps, LANES))
    last = jnp.broadcast_to(tiles[chunks - 1][:, LANES - 1:LANES], (comps, LANES))
    moved_before = (stay * near_before + speed * jnp.where(forward, far_before, first)) * sea_before
    moved_after = (stay * near_after + speed * jnp.where(forward, last, far_after)) * sea_after
    ghosts = courant
    for k in range(chunks):
        low = moved_before if k == 0 else jnp.broadcast_to(moved[k - 1][:, LANES - 1:LANES], (comps, LANES))
        high = moved_after if k == chunks - 1 else jnp.broadcast_to(moved[k + 1][:, 0:1], (comps, LANES))
        ghosts = jnp.where(lane == k, low, jnp.where(lane == chunks + k, high, ghosts))
    turned = jnp.concatenate([ghosts, jnp.zeros((padded - comps, LANES), F32)], axis=0).T
    for k in range(chunks):
        for at, source in ((0, k), (2, chunks + k), (4, 2 * chunks)):
            out_ref[k, comps + at:comps + at + 1, :] = turned[source:source + 1, 0:LANES]
            out_ref[k, comps + at + 1:comps + at + 2, :] = turned[source:source + 1, LANES:2 * LANES]


def steps_body(where_ref, slab_ref, a_ref, b_ref, turned_a_ref, growth_ref, sea_ref, out_ref, moved_ref, courant_ref, gain_ref, result_ref):
    groups, _, _ = slab_ref.shape
    comps = out_ref.shape[1]
    total = moved_ref.shape[0]
    lane = iota((comps, LANES), 1)
    for g in range(groups):
        start = g * comps
        moved_ref[start:start + comps, 0:LANES] = slab_ref[g, 0:comps, :]
        extra = slab_ref[g, comps:comps + 6, :]
        rows = jnp.concatenate([extra, jnp.zeros((2, LANES), F32)], axis=0)
        columns = rows.T
        tall = [jnp.concatenate([columns[:, 2 * i:2 * i + 1], columns[:comps - LANES, 2 * i + 1:2 * i + 2]], axis=0) for i in range(3)]
        low, high, courant = (jnp.broadcast_to(t, (comps, LANES)) for t in tall)
        moved_ref[start:start + comps, LANES:2 * LANES] = jnp.where(lane == 0, high, jnp.where(lane == LANES - 1, low, 0.0))
        courant_ref[start:start + comps, :] = courant
    growth = growth_ref[...]
    width = growth.shape[1]
    gain_ref[...] = jnp.broadcast_to(jnp.broadcast_to(growth, (8, width)).T[:, 0:1], (total, LANES))

    def source(moved, gain):
        rounded = moved.astype(BF16)
        left = jnp.dot(a_ref[...], rounded, preferred_element_type=F32)
        right = jnp.dot(b_ref[...], rounded, preferred_element_type=F32)
        pairs = (left * right).astype(BF16)
        transfer = jnp.dot(turned_a_ref[...], pairs, preferred_element_type=F32)
        mean = jnp.sum(moved * moved, axis=0, keepdims=True) / total
        spread = jnp.sqrt(mean + 1e-06)
        scale = 1.0 / (1.0 + DISSIPATION * spread)
        return (moved + gain * moved + transfer) * scale

    gain = gain_ref[...]
    moved = moved_ref[...]
    field = source(moved, jnp.concatenate([gain, gain], axis=1))
    left = pltpu.roll(field, 1, 1)[:, 0:LANES]
    right = pltpu.roll(field, 2 * LANES - 1, 1)[:, 0:LANES]
    courant = courant_ref[...]
    speed = jnp.abs(courant)
    sea = sea_ref[pl.ds(where_ref[0], 1), :].astype(F32)
    moved = ((1.0 - speed) * field[:, 0:LANES] + speed * jnp.where(courant > 0, left, right)) * sea
    result_ref[...] = source(moved, gain)
    for g in range(groups):
        out_ref[g, :, :] = result_ref[g * comps:(g + 1) * comps, :]


def gather_body(where_ref, counts_ref, slab_ref, offsets_ref, final_ref, out_ref):
    chunks, comps, _ = slab_ref.shape
    n = counts_ref.shape[0]
    slots = NB_BLOCK // n
    block = where_ref[1]
    start = jnp.int32(0)
    for s in range(n):
        start = start + jnp.where(s < block, counts_ref[s], 0)
    count = counts_ref[block]
    row = lax.div(start, jnp.int32(n))
    shift = lax.rem(start, jnp.int32(n))
    lines = [offsets_ref[pl.ds(row + t, 1), :] for t in range(slots + 1)]
    at = iota((1, n), 1)
    wraps = at < shift
    base = jnp.where(wraps, at - shift + n, at - shift)
    wanted = [jnp.where(base + n * t < count, jnp.where(wraps, lines[t + 1], lines[t]), -1) for t in range(slots)]
    wanted = jnp.concatenate(wanted, axis=1)
    point = iota((LANES, slots * n), 0)
    picked = jnp.zeros((comps, slots * n), F32)
    for k in range(chunks):
        tile = slab_ref[k, :, :]
        final_ref[:, k * LANES:(k + 1) * LANES] = tile
        chosen = (point + k * LANES == wanted).astype(F32).astype(BF16)
        picked = picked + exact_dot(tile, chosen, ((1,), (0,)))
    rest = comps - LANES
    side = 2 * LANES
    picked = jnp.concatenate([picked, jnp.zeros((comps, side - slots * n), F32)], axis=1)
    picked = jnp.concatenate([picked, jnp.zeros((side - comps, side), F32)], axis=0)
    turned = picked.T
    tail = jnp.zeros((n, LANES), F32)
    for t in range(slots):
        out_ref[t, :, :] = turned[t * n:(t + 1) * n, 0:LANES]
        part = turned[t * n:(t + 1) * n, LANES:2 * LANES]
        tail = tail + (part if t == 0 else pltpu.roll(part, t * rest, 1))
    out_ref[slots, :, :] = tail


def relay_body(where_ref, counts_ref, column_ref, in_ref, out_ref, *, rest):
    n = counts_ref.shape[0]
    slots = NB_BLOCK // n
    share = in_ref.shape[0] - 1
    me = where_ref[1]
    column = column_ref[...]
    source_row = iota((n, n), 0)
    source_lane = iota((n, n), 1)
    wide = jnp.broadcast_to(column, (n, n))
    starts = jnp.sum(jnp.where(source_row < source_lane, wide, 0), axis=0, keepdims=True)
    counts = jnp.sum(jnp.where(source_row == source_lane, wide, 0), axis=0, keepdims=True)
    span = NB_BLOCK // 2
    window = jnp.where(source_row < n // 2, span * source_row + counts[:, 0:1], span * (source_row - n // 2))
    base = lax.rem(me - starts + 128 * n, jnp.int32(n))
    lane = iota((n, LANES), 1)
    heads = [jnp.zeros((n, LANES), F32) for _ in range(2)]
    tail = jnp.zeros((n, LANES), F32)
    for t in range(slots):
        position = base + n * t
        valid = position < counts
        inside = starts + position - window
        hit = jnp.logical_and(jnp.logical_and(inside >= 0, inside < span), valid)
        head = in_ref[t, :, :]
        part = in_ref[share, :, :]
        part = part if t == 0 else pltpu.roll(part, LANES - t * rest, 1)
        part = jnp.where(lane < rest, part, 0.0)
        for u in range(2):
            in_half = jnp.logical_and(hit, (inside < n) if u == 0 else (inside >= n))
            chosen = in_half.astype(F32).astype(BF16)
            heads[u] = heads[u] + exact_pick(chosen, head)
            tail = tail + exact_pick(chosen, part if u == 0 else pltpu.roll(part, u * rest, 1))
    for u in range(2):
        out_ref[u, :, :] = heads[u]
    out_ref[2, :, :] = tail


def settle_body(where_ref, counts_ref, in_ref, out_ref):
    comps, span = out_ref.shape
    n = in_ref.shape[1]
    rest = comps - LANES
    block = where_ref[1]
    device = iota((n, LANES), 0)
    at = iota((n, LANES), 1)
    window = jnp.where(block < n // 2, span * block + counts_ref[0], span * (block - n // 2))
    target = lax.rem(device - window + 256 * n, jnp.int32(n))
    total = None
    for u in range(2):
        chosen = (at == target + n * u).astype(F32).astype(BF16)
        tail = in_ref[2, :, :]
        tail = tail if u == 0 else pltpu.roll(tail, LANES - u * rest, 1)
        both = jnp.concatenate([in_ref[u, :, :], tail], axis=1).T
        value = exact_dot(both, chosen, ((1,), (0,)))
        total = value if total is None else total + value
    out_ref[...] = total[0:comps, 0:span]


def per_device(spectrum, courant, growth, quad_a, quad_b, sea_mask, nest_counts, nest_offsets):
    comps, points = spectrum.shape
    total = growth.shape[0]
    groups = lax.axis_size("comp")
    n = lax.axis_size("pts")
    chunks = points // LANES
    padded = 2 * LANES
    slab_rows = comps + 6
    sea_row = sea_mask.reshape(1, points)
    sea_tiles = sea_mask.reshape(chunks, LANES)
    where = jnp.stack([lax.axis_index("comp"), lax.axis_index("pts")]).astype(jnp.int32)
    edge = jax.ShapeDtypeStruct((8, padded), F32)

    up, down = call(edges_body, (edge, edge), 2)(spectrum, sea_row)
    before = lax.ppermute(up, "pts", [(i, i + 1) for i in range(n - 1)])
    after = lax.ppermute(down, "pts", [(i + 1, i) for i in range(n - 1)])
    slabs = call(pack_body, jax.ShapeDtypeStruct((chunks, slab_rows, LANES), F32), 5)(
        spectrum, sea_row, courant.reshape(1, comps), before, after
    )
    slabs = lax.all_to_all(slabs, "comp", split_axis=0, concat_axis=0, tiled=True)

    turned_a = quad_a.T
    result = call(
        steps_body,
        jax.ShapeDtypeStruct((groups, comps, LANES), F32),
        7,
        smem=(0,),
        scratch=(
            pltpu.VMEM((total, 2 * LANES), F32),
            pltpu.VMEM((total, LANES), F32),
            pltpu.VMEM((total, LANES), F32),
            pltpu.VMEM((total, LANES), F32),
        ),
    )(where, slabs, quad_a, quad_b, turned_a, growth.reshape(1, total), sea_tiles)
    result = lax.all_to_all(result, "comp", split_axis=0, concat_axis=0, tiled=True)

    slots = NB_BLOCK // n
    lines = jnp.pad(nest_offsets, (0, 4 * n)).reshape(-1, n)
    field, sent = call(
        gather_body,
        (jax.ShapeDtypeStruct((comps, points), F32), jax.ShapeDtypeStruct((slots + 1, n, LANES), F32)),
        4,
        smem=(0, 1),
    )(where, nest_counts, result, lines)
    sent = lax.all_to_all(sent.transpose(1, 0, 2), "pts", split_axis=0, concat_axis=0, tiled=True)
    sent = call(
        functools.partial(relay_body, rest=comps - LANES),
        jax.ShapeDtypeStruct((3, n, LANES), F32),
        4,
        smem=(0, 1),
    )(where, nest_counts, nest_counts.reshape(n, 1), sent.transpose(1, 0, 2))
    sent = lax.all_to_all(sent.transpose(1, 0, 2), "pts", split_axis=0, concat_axis=0, tiled=True)
    nest = call(settle_body, jax.ShapeDtypeStruct((comps, NB_BLOCK // 2), F32), 3, smem=(0, 1))(
        where, nest_counts, sent.transpose(1, 0, 2)
    )
    return (field, nest)


def solution(mesh):
    return jax.shard_map(
        per_device,
        mesh=mesh,
        in_specs=(P("comp", "pts"), P("comp"), P(), P(), P(), P("pts"), P(), P()),
        out_specs=(P("comp", "pts"), P("comp", "pts")),
        check_vma=False,
    )
```

time: 356 us -> 131 us (0.37); the launches traced: 351 us -> 131 us
  waiting for transfers between devices: 172 us -> 44.3 us
  local copies, waits for them, and re-layouts: 65.8 us -> 14.3 us
  blocking collectives: 48.3 us -> 15 us
  Pallas kernels: 0 us -> 21.7 us
  other arithmetic: 16.1 us -> 0.58 us
  between operations: 14.3 us -> 0.73 us
  starting transfers between devices: 27.5 us -> 34.1 us
  matrix products: 6.24 us -> 0 us
    reduce_scatter x1 -> x0, waiting for transfers between devices: 151 us -> none  [per_device(): nest = lax.psum_scatter(picked, 'pts', scatter_dimension=1, tiled=True)]
    gather x2 -> x0, local copies, waits for them, and re-layouts: 58 us -> none  [the longest x1 34.3 us: per_device(): offsets = jnp.take(nest_offsets, entries)]
    all_to_all x2 -> x1, blocking collectives: 48.3 us -> 15 us  [per_device(): lax.all_to_all(sent.transpose(1, 0, 2), 'pts', split_axis=0, concat_axis=...]
    all_to_all x2 -> x3, waiting for transfers between devices: 17.3 us -> 43.3 us  [the longest x1 20.7 us: per_device(): lax.all_to_all(result, 'comp', split_axis=0, concat_axis=0, tiled=True)]
    pallas_call x0 -> x6, Pallas kernels: none -> 21.7 us  [the longest x1 9.47 us: per_device(): call(steps_body, jax.ShapeDtypeStruct((groups, comps, LANES), F32), 7, sm...]
    all_to_all x2 -> x3, starting transfers between devices: 10.1 us -> 24 us  [the longest x1 14 us: per_device(): lax.all_to_all(sent.transpose(1, 0, 2), 'pts', split_axis=0, concat_axis=...]
    mul x3 -> x0, other arithmetic: 10.4 us -> none  [the longest x1 7.59 us: per_device(): jnp.take(field, offsets, axis=1)]
    ppermute x4 -> x2, starting transfers between devices: 17.3 us -> 10 us  [the longest x1 5.37 us: per_device(): before = lax.ppermute(up, 'pts', [(i, i + 1) for i in range(n - 1)])]
  transfers between devices with their start and end apart: 7 -> 5, of which waited for: 3 -> 4; matrix products, arithmetic and copies ran while one was open for 12% -> 7% of each run, Pallas kernels for 0% -> 0%
where the time goes in v1:
time: 131 us
  waiting for transfers between devices  44.3 us (34%)
  starting transfers between devices  34.1 us (26%)
  Pallas kernels  21.7 us (17%)
  blocking collectives  15 us (11%)
  local copies, waits for them, and re-layouts  14.3 us (11%)
    all_to_all x1, waiting for transfers between devices, per_device(): lax.all_to_all(result, 'comp', split_axis=0, concat_axis=0, tiled=True)  20.7 us
    all_to_all x1, blocking collectives, per_device(): lax.all_to_all(sent.transpose(1, 0, 2), 'pts', split_axis=0, concat_axis=...  15 us
    all_to_all x1, starting transfers between devices, per_device(): lax.all_to_all(sent.transpose(1, 0, 2), 'pts', split_axis=0, concat_axis=...  14 us
    all_to_all x1, waiting for transfers between devices, per_device(): lax.all_to_all(slabs, 'comp', split_axis=0, concat_axis=0, tiled=True)  13 us
    all_to_all x1, waiting for transfers between devices, per_device(): lax.all_to_all(sent.transpose(1, 0, 2), 'pts', split_axis=0, concat_axis=...  9.62 us
    pallas_call x1, Pallas kernels, per_device(): call(steps_body, jax.ShapeDtypeStruct((groups, comps, LANES), F32), 7, sm...  9.47 us
    unnamed x18, local copies, waits for them, and re-layouts  8.41 us
    all_to_all x1, starting transfers between devices, per_device(): lax.all_to_all(slabs, 'comp', split_axis=0, concat_axis=0, tiled=True)  6.32 us
  transfers between devices with their start and end apart: 5, of which 4 were waited for; matrix products, arithmetic and copies ran while one was open for 7% of the time, Pallas kernels for 0%

profile of v1, /device:TPU:1, one launch (start us, length us, event | category | flops | bytes accessed | tf_op | source)
XLA Modules:
  0.0 130.8 jit_solution(13060575789248985469)
XLA Ops:
  0.6 0.0 copy-start
  0.6 2.0 %shard_map.95 = (f32[8,256]{1,0:T(8,128)}, f32[8,256]{1,0:T(8,128)}) custom-call(f32[162,1024]{1,0:T(8,128)} %field_ref.3, s32[1,1024]{1,0:T(1,128)} %bitcast.20), custom_call_target="tpu_custom_call" | custom-call | flops 1000000 | bytes 1000000 | tf_op jit(solution)/shard_map/pallas_call | solution.py:270
  2.6 5.4 %collective-permute-start = (f32[8,256]{1,0:T(8,128)}, f32[8,256]{1,0:T(8,128)S(1)}, u32[]{:S(2)}, u32[]{:S(2)}) collective-permute-start(f32[8,256]{1,0:T(8,128)} %get-tuple-element.6), channel_id=1, source_target_pairs={{0,1},{1,2},{2,3},{3,4},{4,5},{5,6},{6,7},{7,8},{8,9},{9,10},{10,1... | collective-permute-start | bytes 24584 | tf_op jit(solution)/shard_map/ppermute | solution.py:271
  8.0 4.7 %collective-permute-start.1 = (f32[8,256]{1,0:T(8,128)}, f32[8,256]{1,0:T(8,128)S(1)}, u32[]{:S(2)}, u32[]{:S(2)}) collective-permute-start(f32[8,256]{1,0:T(8,128)} %get-tuple-element.7), channel_id=1, source_target_pairs={{1,0},{2,1},{3,2},{4,3},{5,4},{6,5},{7,6},{8,7},{9,8},{10,9},{11,1... | collective-permute-start | bytes 24584 | tf_op jit(solution)/shard_map/ppermute | solution.py:272
  12.6 0.0 collective-permute-done.before_ref
  12.7 0.0 copy-start.4
  12.7 1.0 collective-permute-done.1.after_ref
  13.7 0.0 copy-start.5
  13.7 0.0 copy-done.4
  13.7 0.6 copy-done.5
  14.3 3.5 %shard_map.96 = f32[8,168,128]{2,1,0:T(8,128)} custom-call(f32[162,1024]{1,0:T(8,128)} %field_ref.3, s32[1,1024]{1,0:T(1,128)} %bitcast.21, f32[1,162]{1,0:T(1,128)} %bitcast.24, f32[8,256]{1,0:T(8,128)} %copy-done.4, f32[8,256]{1,0:T(8,128)} %copy-done.5), custom_call_target="tpu_custom_call" | custom-call | flops 1000000 | bytes 1000000 | tf_op jit(solution)/shard_map/pallas_call | solution.py:273
  17.8 6.3 %all-to-all-start = ((f32[8,168,128]{2,1,0:T(8,128)}), f32[8,168,128]{2,1,0:T(8,128)S(1)}, u32[]{:S(2)}, u32[]{:S(2)}) async-start(f32[8,168,128]{2,1,0:T(8,128)} %shard_map.96), calls=%async_computation | async-start | bytes 1376256 | tf_op jit(solution)/shard_map/all_to_all | solution.py:276
  24.1 0.0 copy-done
  24.1 2.4 %copy.16.a_ref = bf16[640,1296]{1,0:T(8,128)(2,1)} copy(bf16[640,1296]{0,1:T(8,128)(2,1)S(1)} %copy-done) | data formatting | bytes 3317760 | tf_op args[3]
  26.5 0.0 copy-start.6
  26.5 3.7 %copy.17.b_ref = bf16[640,1296]{1,0:T(8,128)(2,1)} copy(bf16[640,1296]{0,1:T(8,128)(2,1)} %param.12) | data formatting | bytes 3317760 | tf_op args[4]
  30.2 0.0 copy-done.6
  30.2 0.6 reshape.24.growth_ref
  30.8 0.6 pad_add_fusion.where_ref
  31.3 13.0 %all-to-all-done.slab_ref = f32[8,168,128]{2,1,0:T(8,128)S(1)} async-done(((f32[8,168,128]{2,1,0:T(8,128)}), f32[8,168,128]{2,1,0:T(8,128)S(1)}, u32[]{:S(2)}, u32[]{:S(2)}) %all-to-all-start) | async-done | bytes 688160 | tf_op jit(solution)/shard_map/all_to_all | solution.py:276
  44.4 0.0 copy-start.2
  44.4 0.8 copy-done.2
  45.2 0.0 copy-start.3
  45.2 9.5 %shard_map.97 = f32[8,162,128]{2,1,0:T(8,128)} custom-call(s32[2]{0:T(128)} %pad_add_fusion.where_ref, f32[8,168,128]{2,1,0:T(8,128)} %copy-done.2, bf16[640,1296]{1,0:T(8,128)(2,1)} %copy.16.a_ref, bf16[640,1296]{1,0:T(8,128)(2,1)} %copy.17.b_ref, bf16[1296,640]{1,0:T(8,128)(2,1)} %bitcast.15, f32[1,1296]{1,0:T(1,128)} %reshape.24.growth_ref, s32[8,128]{1,0:T(8,128)} %bitcast.22), custom_call_target="tpu_custom_call" | custom-call | flops 1000000 | bytes 1000000 | tf_op jit(solution)/shard_map/pallas_call | solution.py:279
  54.7 0.0 copy-start.7
  54.7 3.7 %all-to-all-start.1 = ((f32[8,162,128]{2,1,0:T(8,128)}), f32[8,162,128]{2,1,0:T(8,128)S(1)}, u32[]{:S(2)}, u32[]{:S(2)}) async-start(f32[8,162,128]{2,1,0:T(8,128)} %shard_map.97), calls=%async_computation.1 | async-start | bytes 1376256 | tf_op jit(solution)/shard_map/all_to_all | solution.py:291
  58.4 0.0 copy-done.3
  58.4 0.7 reshape.26.offsets_ref
  59.1 20.7 %all-to-all-done.1.slab_ref = f32[8,162,128]{2,1,0:T(8,128)S(1)} async-done(((f32[8,162,128]{2,1,0:T(8,128)}), f32[8,162,128]{2,1,0:T(8,128)S(1)}, u32[]{:S(2)}, u32[]{:S(2)}) %all-to-all-start.1) | async-done | bytes 663584 | tf_op jit(solution)/shard_map/all_to_all | solution.py:291
  79.8 0.0 copy-start.1
  79.8 0.9 copy-done.1
  80.7 2.8 %shard_map.98 = (f32[162,1024]{1,0:T(8,128)}, f32[4,64,128]{2,1,0:T(8,128)}) custom-call(s32[2]{0:T(128)} %pad_add_fusion.where_ref, s32[64]{0:T(128)} %counts_ref.5, f32[8,162,128]{2,1,0:T(8,128)} %copy-done.1, s32[100,64]{1,0:T(8,128)} %reshape.26.offsets_ref), custom_call_target="tpu_custom_call" | custom-call | flops 1000000 | bytes 1000000 | tf_op jit(solution)/shard_map/pallas_call | solution.py:295
  83.5 1.6 %copy.18 = f32[64,4,128]{2,1,0:T(4,128)} copy(f32[64,4,128]{2,0,1:T(8,128)} %bitcast.19) | data formatting | bytes 262144 | tf_op jit(solution)/shard_map/transpose | solution.py:301
  85.1 14.0 %all-to-all-start.2 = ((f32[64,4,128]{2,1,0:T(4,128)}), f32[64,4,128]{2,1,0:T(4,128)S(1)}, u32[]{:S(2)}, u32[]{:S(2)}) async-start(f32[64,4,128]{2,1,0:T(4,128)} %copy.18), calls=%async_computation.2 | async-start | bytes 262144 | tf_op jit(solution)/shard_map/all_to_all | solution.py:301
  99.2 0.0 copy-done.7
  99.2 0.7 copy.20.column_ref
  99.9 9.6 %all-to-all-done.2 = f32[64,4,128]{2,1,0:T(4,128)S(1)} async-done(((f32[64,4,128]{2,1,0:T(4,128)}), f32[64,4,128]{2,1,0:T(4,128)S(1)}, u32[]{:S(2)}, u32[]{:S(2)}) %all-to-all-start.2) | async-done | bytes 131104 | tf_op jit(solution)/shard_map/all_to_all | solution.py:301
  109.5 0.7 copy.25
  110.2 2.1 %shard_map.99 = f32[3,64,128]{2,1,0:T(8,128)} custom-call(s32[2]{0:T(128)} %pad_add_fusion.where_ref, s32[64]{0:T(128)} %counts_ref.5, s32[64,1]{1,0:T(8,128)} %copy.20.column_ref, f32[4,64,128]{2,1,0:T(8,128)} %bitcast.16), custom_call_target="tpu_custom_call" | custom-call | flops 1000000 | bytes 1000000 | tf_op jit(solution)/shard_map/pallas_call | solution.py:302
  112.2 1.0 copy.21
  113.2 15.0 %all_to_all.20 = f32[64,3,128]{2,1,0:T(4,128)S(1)} all-to-all(f32[64,3,128]{2,1,0:T(4,128)S(1)} %copy.21), channel_id=1, replica_groups=mesh['comp'=8,'pts'=64] {'pts'}, dimensions={0} | all-to-all | bytes 196608 | tf_op jit(solution)/shard_map/all_to_all | solution.py:308
  128.2 0.7 copy.26
  128.9 1.9 %shard_map.100 = f32[162,96]{1,0:T(8,128)} custom-call(s32[2]{0:T(128)} %pad_add_fusion.where_ref, s32[64]{0:T(128)} %counts_ref.5, f32[3,64,128]{2,1,0:T(8,128)} %bitcast.18), custom_call_target="tpu_custom_call" | custom-call | flops 1000000 | bytes 1000000 | tf_op jit(solution)/shard_map/pallas_call | solution.py:309
  (1 shorter events, 0.0 us)
Async XLA Ops:
  0.6 23.5 %copy-start = (bf16[640,1296]{0,1:T(8,128)(2,1)S(1)}, bf16[640,1296]{0,1:T(8,128)(2,1)}, u32[]{:S(2)}) copy-start(bf16[640,1296]{0,1:T(8,128)(2,1)} %param.11) | copy-start | bytes 4976644
  2.6 10.0 %collective-permute-start = (f32[8,256]{1,0:T(8,128)}, f32[8,256]{1,0:T(8,128)S(1)}, u32[]{:S(2)}, u32[]{:S(2)}) collective-permute-start(f32[8,256]{1,0:T(8,128)} %get-tuple-element.6), channel_id=1, source_target_pairs={{0,1},{1,2},{2,3},{3,4},{4,5},{5,6},{6,7},{7,8},{8,9},{9,10},{10,1... | collective-permute-start | bytes 24584 | tf_op jit(solution)/shard_map/ppermute | solution.py:271
  8.0 5.7 %collective-permute-start.1 = (f32[8,256]{1,0:T(8,128)}, f32[8,256]{1,0:T(8,128)S(1)}, u32[]{:S(2)}, u32[]{:S(2)}) collective-permute-start(f32[8,256]{1,0:T(8,128)} %get-tuple-element.7), channel_id=1, source_target_pairs={{1,0},{2,1},{3,2},{4,3},{5,4},{6,5},{7,6},{8,7},{9,8},{10,9},{11,1... | collective-permute-start | bytes 24584 | tf_op jit(solution)/shard_map/ppermute | solution.py:272
  12.7 1.0 copy-start.4
  13.7 0.6 copy-start.5
  17.8 26.6 %all-to-all-start = ((f32[8,168,128]{2,1,0:T(8,128)}), f32[8,168,128]{2,1,0:T(8,128)S(1)}, u32[]{:S(2)}, u32[]{:S(2)}) async-start(f32[8,168,128]{2,1,0:T(8,128)} %shard_map.96), calls=%async_computation | async-start | bytes 1376256 | tf_op jit(solution)/shard_map/all_to_all | solution.py:276
  26.5 3.7 %copy-start.6 = (f32[1296]{0:T(1024)S(1)}, f32[1296]{0:T(1024)}, u32[]{:S(2)}) copy-start(f32[1296]{0:T(1024)} %param.10) | copy-start | bytes 15556
  44.4 0.8 copy-start.2
  45.2 13.2 %copy-start.3 = (s32[6144]{0:T(1024)S(1)}, s32[6144]{0:T(1024)}, u32[]{:S(2)}) copy-start(s32[6144]{0:T(1024)} %param.15) | copy-start | bytes 73732
  54.7 44.4 %copy-start.7 = (s32[64]{0:T(128)S(1)}, s32[64]{0:T(128)}, u32[]{:S(2)}) copy-start(s32[64]{0:T(128)} %counts_ref.5) | copy-start | bytes 772
  54.7 25.1 %all-to-all-start.1 = ((f32[8,162,128]{2,1,0:T(8,128)}), f32[8,162,128]{2,1,0:T(8,128)S(1)}, u32[]{:S(2)}, u32[]{:S(2)}) async-start(f32[8,162,128]{2,1,0:T(8,128)} %shard_map.97), calls=%async_computation.1 | async-start | bytes 1376256 | tf_op jit(solution)/shard_map/all_to_all | solution.py:291
  79.8 0.9 copy-start.1
  85.1 24.4 %all-to-all-start.2 = ((f32[64,4,128]{2,1,0:T(4,128)}), f32[64,4,128]{2,1,0:T(4,128)S(1)}, u32[]{:S(2)}, u32[]{:S(2)}) async-start(f32[64,4,128]{2,1,0:T(4,128)} %copy.18), calls=%async_computation.2 | async-start | bytes 262144 | tf_op jit(solution)/shard_map/all_to_all | solution.py:301

commit v2 on v1

--- a/solution.py
+++ b/solution.py
@@ -10,6 +10,7 @@
 STEPS = 2
 LANES = 128
 NB_BLOCK = 192
+SLAB = 4
 DISSIPATION = 0.5
 
 F32 = jnp.float32
@@ -18,7 +19,7 @@
 SMEM = pl.BlockSpec(memory_space=pltpu.SMEM)
 
 
-def call(body, out_shape, n_in, smem=(), cost=None, scratch=()):
+def call(body, out_shape, n_in, smem=(), cost=None, scratch=(), vmem=8):
     specs = [SMEM if i in smem else VMEM for i in range(n_in)]
     outs = VMEM if not isinstance(out_shape, (tuple, list)) else tuple(VMEM for _ in out_shape)
     flops, bytes_accessed = cost or (1_000_000, 1_000_000)
@@ -28,6 +29,7 @@
         in_specs=specs,
         out_specs=outs,
         scratch_shapes=list(scratch),
+        compiler_params=pltpu.CompilerParams(vmem_limit_bytes=vmem << 20),
         cost_estimate=pl.CostEstimate(flops=flops, bytes_accessed=bytes_accessed, transcendentals=0),
     )
 
@@ -90,12 +92,12 @@
     lane = iota((comps, LANES), 1)
 
     tiles = [field_ref[:, k * LANES:(k + 1) * LANES] for k in range(chunks)]
+    ups = [pltpu.roll(tile, 1, 1) for tile in tiles]
+    downs = [pltpu.roll(tile, LANES - 1, 1) for tile in tiles]
     moved = []
     for k in range(chunks):
-        left_edge = near_before if k == 0 else jnp.broadcast_to(tiles[k - 1][:, LANES - 1:LANES], (comps, LANES))
-        right_edge = near_after if k == chunks - 1 else jnp.broadcast_to(tiles[k + 1][:, 0:1], (comps, LANES))
-        left = jnp.where(lane == 0, left_edge, pltpu.roll(tiles[k], 1, 1))
-        right = jnp.where(lane == LANES - 1, right_edge, pltpu.roll(tiles[k], LANES - 1, 1))
+        left = jnp.where(lane == 0, near_before if k == 0 else ups[k - 1], ups[k])
+        right = jnp.where(lane == LANES - 1, near_after if k == chunks - 1 else downs[k + 1], downs[k])
         sea = sea_ref[0:1, k * LANES:(k + 1) * LANES].astype(F32)
         value = (stay * tiles[k] + speed * jnp.where(forward, left, right)) * sea
         out_ref[k, 0:comps, :] = value
@@ -107,8 +109,8 @@
     moved_after = (stay * near_after + speed * jnp.where(forward, last, far_after)) * sea_after
     ghosts = courant
     for k in range(chunks):
-        low = moved_before if k == 0 else jnp.broadcast_to(moved[k - 1][:, LANES - 1:LANES], (comps, LANES))
-        high = moved_after if k == chunks - 1 else jnp.broadcast_to(moved[k + 1][:, 0:1], (comps, LANES))
+        low = moved_before if k == 0 else pltpu.roll(moved[k - 1], k + 1, 1)
+        high = moved_after if k == chunks - 1 else pltpu.roll(moved[k + 1], chunks + k, 1)
         ghosts = jnp.where(lane == k, low, jnp.where(lane == chunks + k, high, ghosts))
     turned = jnp.concatenate([ghosts, jnp.zeros((padded - comps, LANES), F32)], axis=0).T
     for k in range(chunks):
@@ -161,9 +163,10 @@
         out_ref[g, :, :] = result_ref[g * comps:(g + 1) * comps, :]
 
 
-def gather_body(where_ref, counts_ref, slab_ref, offsets_ref, final_ref, out_ref):
+def gather_body(where_ref, counts_ref, slab_ref, offsets_ref, out_ref):
     chunks, comps, _ = slab_ref.shape
     n = counts_ref.shape[0]
+    rows = SLAB * n
     slots = NB_BLOCK // n
     block = where_ref[1]
     start = jnp.int32(0)
@@ -173,85 +176,94 @@
     row = lax.div(start, jnp.int32(n))
     shift = lax.rem(start, jnp.int32(n))
     lines = [offsets_ref[pl.ds(row + t, 1), :] for t in range(slots + 1)]
-    at = iota((1, n), 1)
+    lane = iota((1, rows), 1)
+    at = lane // SLAB
+    slot = lane % SLAB
     wraps = at < shift
     base = jnp.where(wraps, at - shift + n, at - shift)
-    wanted = [jnp.where(base + n * t < count, jnp.where(wraps, lines[t + 1], lines[t]), -1) for t in range(slots)]
-    wanted = jnp.concatenate(wanted, axis=1)
-    point = iota((LANES, slots * n), 0)
-    picked = jnp.zeros((comps, slots * n), F32)
+    wanted = jnp.full((1, rows), -1, jnp.int32)
+    for t in range(slots):
+        mine = jnp.logical_and(slot == t, base + n * t < count)
+        wanted = jnp.where(mine, jnp.where(wraps, lines[t + 1], lines[t]), wanted)
+    point = iota((LANES, rows), 0)
+    picked = jnp.zeros((comps, rows), F32)
     for k in range(chunks):
-        tile = slab_ref[k, :, :]
-        final_ref[:, k * LANES:(k + 1) * LANES] = tile
         chosen = (point + k * LANES == wanted).astype(F32).astype(BF16)
-        picked = picked + exact_dot(tile, chosen, ((1,), (0,)))
-    rest = comps - LANES
+        picked = picked + exact_dot(slab_ref[k, :, :], chosen, ((1,), (0,)))
     side = 2 * LANES
-    picked = jnp.concatenate([picked, jnp.zeros((comps, side - slots * n), F32)], axis=1)
-    picked = jnp.concatenate([picked, jnp.zeros((side - comps, side), F32)], axis=0)
-    turned = picked.T
-    tail = jnp.zeros((n, LANES), F32)
+    turned = jnp.concatenate([picked, jnp.zeros((side - comps, rows), F32)], axis=0).T
+    out_ref[...] = fold(turned, slots, comps - LANES)
+
+
+def fold(turned, slots, rest):
+    rows = turned.shape[0]
+    slot = iota((rows, LANES), 0) % SLAB
+    lane = iota((rows, LANES), 1)
+    main = turned[:, 0:LANES]
+    side = turned[:, LANES:2 * LANES]
+    out = jnp.where(slot < slots, main, 0.0)
     for t in range(slots):
-        out_ref[t, :, :] = turned[t * n:(t + 1) * n, 0:LANES]
-        part = turned[t * n:(t + 1) * n, LANES:2 * LANES]
-        tail = tail + (part if t == 0 else pltpu.roll(part, t * rest, 1))
-    out_ref[slots, :, :] = tail
-
-
-def relay_body(where_ref, counts_ref, column_ref, in_ref, out_ref, *, rest):
-    n = counts_ref.shape[0]
+        part = pltpu.roll(side, slots - t, 0)
+        part = part if t == 0 else pltpu.roll(part, t * rest, 1)
+        inside = jnp.logical_and(lane >= t * rest, lane < (t + 1) * rest)
+        out = jnp.where(jnp.logical_and(slot == slots, inside), part, out)
+    return out
+
+
+def unfold(value, slots, rest):
+    rows = value.shape[0]
+    slot = iota((rows, LANES), 0) % SLAB
+    lane = iota((rows, LANES), 1)
+    side = jnp.zeros((rows, LANES), F32)
+    for t in range(slots):
+        part = pltpu.roll(value, rows - (slots - t), 0)
+        part = part if t == 0 else pltpu.roll(part, LANES - t * rest, 1)
+        side = jnp.where(jnp.logical_and(slot == t, lane < rest), part, side)
+    return jnp.concatenate([jnp.where(slot < slots, value, 0.0), side], axis=1)
+
+
+def relay_body(where_ref, column_ref, in_ref, out_ref, *, rest):
+    rows = in_ref.shape[0]
+    n = rows // SLAB
     slots = NB_BLOCK // n
-    share = in_ref.shape[0] - 1
     me = where_ref[1]
-    column = column_ref[...]
-    source_row = iota((n, n), 0)
-    source_lane = iota((n, n), 1)
-    wide = jnp.broadcast_to(column, (n, n))
-    starts = jnp.sum(jnp.where(source_row < source_lane, wide, 0), axis=0, keepdims=True)
-    counts = jnp.sum(jnp.where(source_row == source_lane, wide, 0), axis=0, keepdims=True)
+    row = iota((rows, rows), 0)
+    lane = iota((rows, rows), 1)
+    wide = jnp.broadcast_to(column_ref[...], (n, rows))
+    source = iota((n, rows), 0)
+    target = iota((n, rows), 1) // SLAB
+    starts = jnp.sum(jnp.where(source < target, wide, 0), axis=0, keepdims=True)
+    counts = jnp.sum(jnp.where(source == target, wide, 0), axis=0, keepdims=True)
     span = NB_BLOCK // 2
-    window = jnp.where(source_row < n // 2, span * source_row + counts[:, 0:1], span * (source_row - n // 2))
-    base = lax.rem(me - starts + 128 * n, jnp.int32(n))
-    lane = iota((n, LANES), 1)
-    heads = [jnp.zeros((n, LANES), F32) for _ in range(2)]
-    tail = jnp.zeros((n, LANES), F32)
-    for t in range(slots):
-        position = base + n * t
-        valid = position < counts
-        inside = starts + position - window
-        hit = jnp.logical_and(jnp.logical_and(inside >= 0, inside < span), valid)
-        head = in_ref[t, :, :]
-        part = in_ref[share, :, :]
-        part = part if t == 0 else pltpu.roll(part, LANES - t * rest, 1)
-        part = jnp.where(lane < rest, part, 0.0)
-        for u in range(2):
-            in_half = jnp.logical_and(hit, (inside < n) if u == 0 else (inside >= n))
-            chosen = in_half.astype(F32).astype(BF16)
-            heads[u] = heads[u] + exact_pick(chosen, head)
-            tail = tail + exact_pick(chosen, part if u == 0 else pltpu.roll(part, u * rest, 1))
-    for u in range(2):
-        out_ref[u, :, :] = heads[u]
-    out_ref[2, :, :] = tail
+    slot = iota((1, rows), 1) % SLAB
+    position = lax.rem(me - starts + 128 * n, jnp.int32(n)) + n * slot
+    valid = jnp.logical_and(position < counts, slot < slots)
+    entry = jnp.where(valid, starts + position, -(1 << 20))
+    place = iota((rows, 1), 0)
+    half = place % SLAB
+    place = place // SLAB
+    window = jnp.where(place < n // 2, span * place + counts[:, 0:1], span * (place - n // 2)) + n * half
+    size = jnp.where(half == 0, n, jnp.where(half == 1, span - n, 0))
+    inside = entry - window
+    chosen = jnp.logical_and(inside >= 0, inside < size).astype(F32).astype(BF16)
+    value = exact_pick(chosen, unfold(in_ref[...], slots, rest))
+    out_ref[...] = fold(value, 2, rest)
 
 
 def settle_body(where_ref, counts_ref, in_ref, out_ref):
     comps, span = out_ref.shape
-    n = in_ref.shape[1]
-    rest = comps - LANES
+    rows = in_ref.shape[0]
+    n = rows // SLAB
     block = where_ref[1]
-    device = iota((n, LANES), 0)
-    at = iota((n, LANES), 1)
+    row = iota((rows, LANES), 0)
+    device = row // SLAB
+    half = row % SLAB
+    at = iota((rows, LANES), 1)
     window = jnp.where(block < n // 2, span * block + counts_ref[0], span * (block - n // 2))
-    target = lax.rem(device - window + 256 * n, jnp.int32(n))
-    total = None
-    for u in range(2):
-        chosen = (at == target + n * u).astype(F32).astype(BF16)
-        tail = in_ref[2, :, :]
-        tail = tail if u == 0 else pltpu.roll(tail, LANES - u * rest, 1)
-        both = jnp.concatenate([in_ref[u, :, :], tail], axis=1).T
-        value = exact_dot(both, chosen, ((1,), (0,)))
-        total = value if total is None else total + value
-    out_ref[...] = total[0:comps, 0:span]
+    target = lax.rem(device - window + 256 * n, jnp.int32(n)) + n * half
+    chosen = jnp.logical_and(at == target, half < 2).astype(F32).astype(BF16)
+    value = exact_dot(unfold(in_ref[...], 2, comps - LANES).T, chosen, ((1,), (0,)))
+    out_ref[...] = value[0:comps, 0:span]
 
 
 def per_device(spectrum, courant, growth, quad_a, quad_b, sea_mask, nest_counts, nest_offsets):
@@ -287,28 +299,18 @@
             pltpu.VMEM((total, LANES), F32),
             pltpu.VMEM((total, LANES), F32),
         ),
+        vmem=28,
     )(where, slabs, quad_a, quad_b, turned_a, growth.reshape(1, total), sea_tiles)
     result = lax.all_to_all(result, "comp", split_axis=0, concat_axis=0, tiled=True)
 
-    slots = NB_BLOCK // n
-    lines = jnp.pad(nest_offsets, (0, 4 * n)).reshape(-1, n)
-    field, sent = call(
-        gather_body,
-        (jax.ShapeDtypeStruct((comps, points), F32), jax.ShapeDtypeStruct((slots + 1, n, LANES), F32)),
-        4,
-        smem=(0, 1),
-    )(where, nest_counts, result, lines)
-    sent = lax.all_to_all(sent.transpose(1, 0, 2), "pts", split_axis=0, concat_axis=0, tiled=True)
-    sent = call(
-        functools.partial(relay_body, rest=comps - LANES),
-        jax.ShapeDtypeStruct((3, n, LANES), F32),
-        4,
-        smem=(0, 1),
-    )(where, nest_counts, nest_counts.reshape(n, 1), sent.transpose(1, 0, 2))
-    sent = lax.all_to_all(sent.transpose(1, 0, 2), "pts", split_axis=0, concat_axis=0, tiled=True)
-    nest = call(settle_body, jax.ShapeDtypeStruct((comps, NB_BLOCK // 2), F32), 3, smem=(0, 1))(
-        where, nest_counts, sent.transpose(1, 0, 2)
-    )
+    lines = jnp.repeat(jnp.pad(nest_offsets, (0, 4 * n)).reshape(-1, n), SLAB, axis=1)
+    slab = jax.ShapeDtypeStruct((SLAB * n, LANES), F32)
+    sent = call(gather_body, slab, 4, smem=(0, 1))(where, nest_counts, result, lines)
+    sent = lax.all_to_all(sent, "pts", split_axis=0, concat_axis=0, tiled=True)
+    field = result.transpose(1, 0, 2).reshape(comps, points)
+    sent = call(functools.partial(relay_body, rest=comps - LANES), slab, 3, smem=(0,))(where, nest_counts.reshape(n, 1), sent)
+    sent = lax.all_to_all(sent, "pts", split_axis=0, concat_axis=0, tiled=True)
+    nest = call(settle_body, jax.ShapeDtypeStruct((comps, NB_BLOCK // 2), F32), 3, smem=(0, 1))(where, nest_counts, sent)
     return (field, nest)
 
 

time: 131 us -> 124 us (0.947)
  blocking collectives: 15 us -> 0 us
  waiting for transfers between devices: 44.3 us -> 56.6 us
  Pallas kernels: 21.7 us -> 14.7 us
  starting transfers between devices: 34.1 us -> 39 us
  local copies, waits for them, and re-layouts: 14.3 us -> 12.2 us
    all_to_all x1 -> x0, blocking collectives: 15 us -> none  [per_device(): lax.all_to_all(sent.transpose(1, 0, 2), 'pts', split_axis=0, concat_axis=...]
    all_to_all x1 -> x2, waiting for transfers between devices: 9.62 us -> 19.4 us  [per_device(): sent = lax.all_to_all(sent, 'pts', split_axis=0, concat_axis=0, tiled=True)]
    all_to_all x1 -> x2, starting transfers between devices: 14 us -> 18.9 us  [per_device(): sent = lax.all_to_all(sent, 'pts', split_axis=0, concat_axis=0, tiled=True)]
    unnamed x18 -> x26, local copies, waits for them, and re-layouts: 8.41 us -> 11.7 us
    transpose x2 -> x1, local copies, waits for them, and re-layouts: 2.6 us -> 0.13 us  [per_device(): field = result.transpose(1, 0, 2).reshape(comps, points)]
    pallas_call x1, Pallas kernels: 9.47 us -> 7.08 us  [per_device(): call(steps_body, jax.ShapeDtypeStruct((groups, comps, LANES), F32), 7, sm...]
    all_to_all x1, waiting for transfers between devices: 13 us -> 15.3 us  [per_device(): lax.all_to_all(slabs, 'comp', split_axis=0, concat_axis=0, tiled=True)]
    pallas_call x1, Pallas kernels: 1.96 us -> 0.11 us  [per_device(): up, down = call(edges_body, (edge, edge), 2)(spectrum, sea_row)]
  transfers between devices with their start and end apart: 5 -> 6, of which waited for: 4 -> 5; matrix products, arithmetic and copies ran while one was open for 7% -> 5% of each run, Pallas kernels for 0% -> 0%
where the time goes in v2:
time: 124 us; the launch traced here: 123 us
  waiting for transfers between devices  56.6 us (46%)
  starting transfers between devices  39 us (31%)
  Pallas kernels  14.7 us (12%)
  local copies, waits for them, and re-layouts  12.2 us (10%)
    all_to_all x1, waiting for transfers between devices, per_device(): lax.all_to_all(result, 'comp', split_axis=0, concat_axis=0, tiled=True)  21.1 us
    all_to_all x2, waiting for transfers between devices, per_device(): sent = lax.all_to_all(sent, 'pts', split_axis=0, concat_axis=0, tiled=True)  19.4 us
    all_to_all x2, starting transfers between devices, per_device(): sent = lax.all_to_all(sent, 'pts', split_axis=0, concat_axis=0, tiled=True)  18.9 us
    all_to_all x1, waiting for transfers between devices, per_device(): lax.all_to_all(slabs, 'comp', split_axis=0, concat_axis=0, tiled=True)  15.3 us
    unnamed x26, local copies, waits for them, and re-layouts  11.7 us
    pallas_call x1, Pallas kernels, per_device(): call(steps_body, jax.ShapeDtypeStruct((groups, comps, LANES), F32), 7, sm...  7.08 us
    all_to_all x1, starting transfers between devices, per_device(): lax.all_to_all(slabs, 'comp', split_axis=0, concat_axis=0, tiled=True)  6.32 us
    ppermute x1, starting transfers between devices, per_device(): before = lax.ppermute(up, 'pts', [(i, i + 1) for i in range(n - 1)])  5.38 us
  transfers between devices with their start and end apart: 6, of which 5 were waited for; matrix products, arithmetic and copies ran while one was open for 5% of the time, Pallas kernels for 0%

profile of v2, /device:TPU:1, one launch (start us, length us, event | category | flops | bytes accessed | tf_op | source)
XLA Modules:
  0.0 123.3 jit_solution(775330488163050513)
XLA Ops:
  0.6 0.0 copy-start.1
  0.6 0.0 copy-start.2
  0.6 1.2 copy-done.2
  1.9 0.0 copy-start.4
  1.9 0.7 copy-done.4
  2.5 0.1 shard_map.95
  2.7 5.4 %collective-permute-start = (f32[8,256]{1,0:T(8,128)S(1)}, f32[8,256]{1,0:T(8,128)S(1)}, u32[]{:S(2)}, u32[]{:S(2)}) collective-permute-start(f32[8,256]{1,0:T(8,128)S(1)} %get-tuple-element.4), channel_id=1, source_target_pairs={{0,1},{1,2},{2,3},{3,4},{4,5},{5,6},{6,7},{7,8},{8,9},{9,10},{10,1... | collective-permute-start | bytes 24584 | tf_op jit(solution)/shard_map/ppermute | solution.py:283
  8.1 4.7 %collective-permute-start.1 = (f32[8,256]{1,0:T(8,128)S(1)}, f32[8,256]{1,0:T(8,128)S(1)}, u32[]{:S(2)}, u32[]{:S(2)}) collective-permute-start(f32[8,256]{1,0:T(8,128)S(1)} %get-tuple-element.5), channel_id=1, source_target_pairs={{1,0},{2,1},{3,2},{4,3},{5,4},{6,5},{7,6},{8,7},{9,8},{10,9},{11,1... | collective-permute-start | bytes 24584 | tf_op jit(solution)/shard_map/ppermute | solution.py:284
  12.7 0.0 collective-permute-done.before_ref
  12.7 0.8 collective-permute-done.1.after_ref
  13.5 0.0 copy-start.5
  13.5 0.7 copy-done.5
  14.2 0.0 copy-start.8
  14.2 0.7 copy-done.8
  14.9 2.1 %shard_map.96 = f32[8,168,128]{2,1,0:T(8,128)} custom-call(f32[162,1024]{1,0:T(8,128)S(1)} %copy-done.2, s32[1,1024]{1,0:T(1,128)S(1)} %bitcast.21, f32[1,162]{1,0:T(1,128)S(1)} %bitcast.24, f32[8,256]{1,0:T(8,128)S(1)} %collective-permute-done.before_ref, f32[8,256]{1,0:T(8,128)S(1)} %collective-permute-done.1.after_ref), custom_call_target="tpu_custom_call" | custom-call | flops 1000000 | bytes 1000000 | tf_op jit(solution)/shard_map/pallas_call | solution.py:285
  17.0 6.3 %all-to-all-start = ((f32[8,168,128]{2,1,0:T(8,128)}), f32[8,168,128]{2,1,0:T(8,128)}, u32[]{:S(2)}, u32[]{:S(2)}) async-start(f32[8,168,128]{2,1,0:T(8,128)} %shard_map.96), calls=%async_computation | async-start | bytes 1376256 | tf_op jit(solution)/shard_map/all_to_all | solution.py:288
  23.3 0.0 copy-done.1
  23.3 1.4 %copy.13.a_ref = bf16[640,1296]{1,0:T(8,128)(2,1)S(1)} copy(bf16[640,1296]{0,1:T(8,128)(2,1)S(1)} %copy-done.1) | data formatting | bytes 3317760 | tf_op args[3]
  24.7 0.0 copy-start.10
  24.7 0.0 copy-start.6
  24.7 3.6 %copy.14.b_ref = bf16[640,1296]{1,0:T(8,128)(2,1)} copy(bf16[640,1296]{0,1:T(8,128)(2,1)} %param.12) | data formatting | bytes 3317760 | tf_op args[4]
  28.3 0.0 copy-done.10
  28.4 0.1 pad_add_fusion.where_ref
  28.4 15.3 %all-to-all-done.slab_ref = f32[8,168,128]{2,1,0:T(8,128)} async-done(((f32[8,168,128]{2,1,0:T(8,128)}), f32[8,168,128]{2,1,0:T(8,128)}, u32[]{:S(2)}, u32[]{:S(2)}) %all-to-all-start) | async-done | bytes 688160 | tf_op jit(solution)/shard_map/all_to_all | solution.py:288
  43.7 0.0 copy-done.6
  43.7 0.0 copy-start
  43.7 1.5 %copy-done = bf16[640,1296]{1,0:T(8,128)(2,1)S(1)} copy-done((bf16[640,1296]{1,0:T(8,128)(2,1)S(1)}, bf16[640,1296]{1,0:T(8,128)(2,1)}, u32[]{:S(2)}) %copy-start) | copy-done | bytes 1658904
  45.2 0.0 copy-start.9
  45.2 7.1 %shard_map.97 = f32[8,162,128]{2,1,0:T(8,128)S(1)} custom-call(s32[2]{0:T(128)S(1)} %pad_add_fusion.where_ref, f32[8,168,128]{2,1,0:T(8,128)} %all-to-all-done.slab_ref, bf16[640,1296]{1,0:T(8,128)(2,1)S(1)} %copy.13.a_ref, bf16[640,1296]{1,0:T(8,128)(2,1)S(1)} %copy-done, bf16[1296,640]{1,0:T(8,128)(2,1)S(1)} %bitcast.16, ...), custom_call_target="tpu_custom_call" | custom-call | flops 1000000 | bytes 1000000 | tf_op jit(solution)/shard_map/pallas_call | solution.py:291
  52.3 0.0 copy-start.3
  52.3 0.8 copy-done.3
  53.1 0.0 copy-start.7
  53.1 3.7 %all-to-all-start.1 = ((f32[8,162,128]{2,1,0:T(8,128)}), f32[8,162,128]{2,1,0:T(8,128)S(1)}, u32[]{:S(2)}, u32[]{:S(2)}) async-start(f32[8,162,128]{2,1,0:T(8,128)} %copy-done.3), calls=%async_computation.1 | async-start | bytes 1376256 | tf_op jit(solution)/shard_map/all_to_all | solution.py:304
  56.8 0.0 copy-done.9
  56.9 0.1 reshape.38
  56.9 0.1 copy.16
  57.0 0.1 copy.17.offsets_ref
  57.2 21.1 %all-to-all-done.1.slab_ref = f32[8,162,128]{2,1,0:T(8,128)S(1)} async-done(((f32[8,162,128]{2,1,0:T(8,128)}), f32[8,162,128]{2,1,0:T(8,128)S(1)}, u32[]{:S(2)}, u32[]{:S(2)}) %all-to-all-start.1) | async-done | bytes 663584 | tf_op jit(solution)/shard_map/all_to_all | solution.py:304
  78.2 0.0 copy-done.7
  78.2 2.2 %shard_map.98 = f32[256,128]{1,0:T(8,128)} custom-call(s32[2]{0:T(128)S(1)} %pad_add_fusion.where_ref, s32[64]{0:T(128)S(1)} %copy-done.7, f32[8,162,128]{2,1,0:T(8,128)S(1)} %all-to-all-done.1.slab_ref, s32[100,256]{1,0:T(8,128)S(1)} %copy.17.offsets_ref), custom_call_target="tpu_custom_call" | custom-call | flops 1000000 | bytes 1000000 | tf_op jit(solution)/shard_map/pallas_call | solution.py:308
  80.4 14.1 %all-to-all-start.2 = ((f32[64,4,128]{2,1,0:T(4,128)}), f32[64,4,128]{2,1,0:T(4,128)S(1)}, u32[]{:S(2)}, u32[]{:S(2)}) async-start(f32[64,4,128]{2,1,0:T(4,128)} %bitcast.9), calls=%async_computation.2 | async-start | bytes 262144 | tf_op jit(solution)/shard_map/all_to_all | solution.py:309
  94.5 0.1 copy.18.column_ref
  94.6 10.2 %all-to-all-done.2 = f32[64,4,128]{2,1,0:T(4,128)S(1)} async-done(((f32[64,4,128]{2,1,0:T(4,128)}), f32[64,4,128]{2,1,0:T(4,128)S(1)}, u32[]{:S(2)}, u32[]{:S(2)}) %all-to-all-start.2) | async-done | bytes 131104 | tf_op jit(solution)/shard_map/all_to_all | solution.py:309
  104.8 1.7 %shard_map.99 = f32[256,128]{1,0:T(8,128)} custom-call(s32[2]{0:T(128)S(1)} %pad_add_fusion.where_ref, s32[64,1]{1,0:T(8,128)S(1)} %copy.18.column_ref, f32[256,128]{1,0:T(8,128)S(1)} %bitcast.19), custom_call_target="tpu_custom_call" | custom-call | flops 1000000 | bytes 1000000 | tf_op jit(solution)/shard_map/pallas_call | solution.py:311
  106.5 4.9 %all-to-all-start.3 = ((f32[64,4,128]{2,1,0:T(4,128)}), f32[64,4,128]{2,1,0:T(4,128)S(1)}, u32[]{:S(2)}, u32[]{:S(2)}) async-start(f32[64,4,128]{2,1,0:T(4,128)} %bitcast.11), calls=%async_computation.3 | async-start | bytes 262144 | tf_op jit(solution)/shard_map/all_to_all | solution.py:312
  111.4 0.1 copy.15
  111.6 1.0 copy.19
  112.6 9.2 %all-to-all-done.3 = f32[64,4,128]{2,1,0:T(4,128)S(1)} async-done(((f32[64,4,128]{2,1,0:T(4,128)}), f32[64,4,128]{2,1,0:T(4,128)S(1)}, u32[]{:S(2)}, u32[]{:S(2)}) %all-to-all-start.3) | async-done | bytes 131104 | tf_op jit(solution)/shard_map/all_to_all | solution.py:312
  121.8 1.6 %shard_map.100 = f32[162,96]{1,0:T(8,128)} custom-call(s32[2]{0:T(128)S(1)} %pad_add_fusion.where_ref, s32[64]{0:T(128)S(1)} %copy-done.7, f32[256,128]{1,0:T(8,128)S(1)} %bitcast.18), custom_call_target="tpu_custom_call" | custom-call | flops 1000000 | bytes 1000000 | tf_op jit(solution)/shard_map/pallas_call | solution.py:313
  (4 shorter events, 0.1 us)
Async XLA Ops:
  0.6 22.7 %copy-start.1 = (bf16[640,1296]{0,1:T(8,128)(2,1)S(1)}, bf16[640,1296]{0,1:T(8,128)(2,1)}, u32[]{:S(2)}) copy-start(bf16[640,1296]{0,1:T(8,128)(2,1)} %param.11) | copy-start | bytes 4976644
  0.6 1.2 copy-start.2
  1.9 0.7 copy-start.4
  2.7 10.1 %collective-permute-start = (f32[8,256]{1,0:T(8,128)S(1)}, f32[8,256]{1,0:T(8,128)S(1)}, u32[]{:S(2)}, u32[]{:S(2)}) collective-permute-start(f32[8,256]{1,0:T(8,128)S(1)} %get-tuple-element.4), channel_id=1, source_target_pairs={{0,1},{1,2},{2,3},{3,4},{4,5},{5,6},{6,7},{7,8},{8,9},{9,10},{10,1... | collective-permute-start | bytes 24584 | tf_op jit(solution)/shard_map/ppermute | solution.py:283
  8.1 5.5 %collective-permute-start.1 = (f32[8,256]{1,0:T(8,128)S(1)}, f32[8,256]{1,0:T(8,128)S(1)}, u32[]{:S(2)}, u32[]{:S(2)}) collective-permute-start(f32[8,256]{1,0:T(8,128)S(1)} %get-tuple-element.5), channel_id=1, source_target_pairs={{1,0},{2,1},{3,2},{4,3},{5,4},{6,5},{7,6},{8,7},{9,8},{10,9},{11,1... | collective-permute-start | bytes 24584 | tf_op jit(solution)/shard_map/ppermute | solution.py:284
  13.5 0.7 copy-start.5
  14.2 0.7 copy-start.8
  17.0 26.7 %all-to-all-start = ((f32[8,168,128]{2,1,0:T(8,128)}), f32[8,168,128]{2,1,0:T(8,128)}, u32[]{:S(2)}, u32[]{:S(2)}) async-start(f32[8,168,128]{2,1,0:T(8,128)} %shard_map.96), calls=%async_computation | async-start | bytes 1376256 | tf_op jit(solution)/shard_map/all_to_all | solution.py:288
  24.7 3.7 %copy-start.10 = (f32[1296]{0:T(1024)S(1)}, f32[1296]{0:T(1024)}, u32[]{:S(2)}) copy-start(f32[1296]{0:T(1024)} %param.10) | copy-start | bytes 15556
  24.7 19.0 %copy-start.6 = (s32[1024]{0:T(1024)S(1)}, s32[1024]{0:T(1024)}, u32[]{:S(2)}) copy-start(s32[1024]{0:T(1024)} %param.13) | copy-start | bytes 12292
  43.7 1.5 %copy-start = (bf16[640,1296]{1,0:T(8,128)(2,1)S(1)}, bf16[640,1296]{1,0:T(8,128)(2,1)}, u32[]{:S(2)}) copy-start(bf16[640,1296]{1,0:T(8,128)(2,1)} %copy.14.b_ref) | copy-start | bytes 4976644
  45.2 11.6 %copy-start.9 = (s32[6144]{0:T(1024)S(1)}, s32[6144]{0:T(1024)}, u32[]{:S(2)}) copy-start(s32[6144]{0:T(1024)} %param.15) | copy-start | bytes 73732
  52.3 0.9 copy-start.3
  53.1 25.1 %copy-start.7 = (s32[64]{0:T(128)S(1)}, s32[64]{0:T(128)}, u32[]{:S(2)}) copy-start(s32[64]{0:T(128)} %counts_ref.3) | copy-start | bytes 772
  53.1 25.1 %all-to-all-start.1 = ((f32[8,162,128]{2,1,0:T(8,128)}), f32[8,162,128]{2,1,0:T(8,128)S(1)}, u32[]{:S(2)}, u32[]{:S(2)}) async-start(f32[8,162,128]{2,1,0:T(8,128)} %copy-done.3), calls=%async_computation.1 | async-start | bytes 1376256 | tf_op jit(solution)/shard_map/all_to_all | solution.py:304
  80.4 24.4 %all-to-all-start.2 = ((f32[64,4,128]{2,1,0:T(4,128)}), f32[64,4,128]{2,1,0:T(4,128)S(1)}, u32[]{:S(2)}, u32[]{:S(2)}) async-start(f32[64,4,128]{2,1,0:T(4,128)} %bitcast.9), calls=%async_computation.2 | async-start | bytes 262144 | tf_op jit(solution)/shard_map/all_to_all | solution.py:309
  106.5 15.2 %all-to-all-start.3 = ((f32[64,4,128]{2,1,0:T(4,128)}), f32[64,4,128]{2,1,0:T(4,128)S(1)}, u32[]{:S(2)}, u32[]{:S(2)}) async-start(f32[64,4,128]{2,1,0:T(4,128)} %bitcast.11), calls=%async_computation.3 | async-start | bytes 262144 | tf_op jit(solution)/shard_map/all_to_all | solution.py:312

commit v3 on v2

v3 whole, which is shorter than its diff:
```python
import functools

import jax
import jax.numpy as jnp
from jax import lax
from jax.experimental import pallas as pl
from jax.experimental.pallas import tpu as pltpu
from jax.sharding import PartitionSpec as P

STEPS = 2
LANES = 128
NB_BLOCK = 192
SLAB = 4
DISSIPATION = 0.5

F32 = jnp.float32
BF16 = jnp.bfloat16
VMEM = pl.BlockSpec(memory_space=pltpu.VMEM)
HBM = pl.BlockSpec(memory_space=pltpu.HBM)


def call(body, out_shape, ins, outs=VMEM, scratch=(), vmem=8):
    return pl.pallas_call(
        body,
        out_shape=out_shape,
        in_specs=list(ins),
        out_specs=outs,
        scratch_shapes=list(scratch),
        compiler_params=pltpu.CompilerParams(vmem_limit_bytes=vmem << 20),
        cost_estimate=pl.CostEstimate(flops=1_000_000, bytes_accessed=1_000_000, transcendentals=0),
    )


def iota(shape, axis):
    return lax.broadcasted_iota(jnp.int32, shape, axis)


def split3(value):
    high = value.astype(BF16)
    rest = value - high.astype(F32)
    middle = rest.astype(BF16)
    low = (rest - middle.astype(F32)).astype(BF16)
    return high, middle, low


def exact_dot(value, chosen, dims):
    high, middle, low = (lax.dot_general(term, chosen, (dims, ((), ())), preferred_element_type=F32) for term in split3(value))
    return (high + middle) + low


def exact_pick(chosen, value):
    high, middle, low = (lax.dot_general(chosen, term, (((1,), (0,)), ((), ())), preferred_element_type=F32) for term in split3(value))
    return (high + middle) + low


def edges_body(field_ref, side_ref, up_ref, down_ref):
    comps, points = field_ref.shape
    padded = up_ref.shape[1]
    for ref, start, order in ((up_ref, points - LANES, (LANES - 1, LANES - 2)), (down_ref, 0, (0, 1))):
        tile = jnp.concatenate([field_ref[:, start:start + LANES], jnp.zeros((padded - comps, LANES), F32)], axis=0)
        turned = tile.T
        for row, lane in enumerate(order):
            ref[row:row + 1, :] = turned[lane:lane + 1, :]
        point = start + order[0]
        ref[2:3, :] = jnp.broadcast_to(side_ref[0:1, point:point + 1], (1, padded))
        ref[3:8, :] = jnp.zeros((5, padded), F32)


STEP = 40


def pack_body(field_ref, side_ref, before_ref, after_ref, out_ref, slab_ref, sems):
    comps, points = field_ref.shape
    chunks = points // LANES
    padded = before_ref.shape[1]
    whole = comps // 8 * 8
    rows = jnp.concatenate([before_ref[0:3, :], after_ref[0:3, :], side_ref[1:2, 0:padded], jnp.zeros((1, padded), F32)], axis=0)
    columns = rows.T[:comps, :]

    def wide(at):
        return jnp.broadcast_to(columns[:, at:at + 1], (comps, LANES))

    near_before, far_before, sea_before = wide(0), wide(1), wide(2)
    near_after, far_after, sea_after = wide(3), wide(4), wide(5)
    courant = wide(6)
    speed = jnp.abs(courant)
    stay = 1.0 - speed
    forward = courant > 0
    lane = iota((comps, LANES), 1)

    tiles = [field_ref[:, k * LANES:(k + 1) * LANES] for k in range(chunks)]
    ups = [pltpu.roll(tile, 1, 1) for tile in tiles]
    downs = [pltpu.roll(tile, LANES - 1, 1) for tile in tiles]
    moved = []
    copies = []
    for k in range(chunks):
        left = jnp.where(lane == 0, near_before if k == 0 else ups[k - 1], ups[k])
        right = jnp.where(lane == LANES - 1, near_after if k == chunks - 1 else downs[k + 1], downs[k])
        sea = side_ref[0:1, k * LANES:(k + 1) * LANES]
        value = (stay * tiles[k] + speed * jnp.where(forward, left, right)) * sea
        slab_ref[k, 0:comps, :] = value
        moved.append(value)

    first = jnp.broadcast_to(tiles[0][:, 0:1], (comps, LANES))
    last = jnp.broadcast_to(tiles[chunks - 1][:, LANES - 1:LANES], (comps, LANES))
    moved_before = (stay * near_before + speed * jnp.where(forward, far_before, first)) * sea_before
    moved_after = (stay * near_after + speed * jnp.where(forward, last, far_after)) * sea_after
    ghosts = courant
    for k in range(chunks):
        low = moved_before if k == 0 else pltpu.roll(moved[k - 1], k + 1, 1)
        high = moved_after if k == chunks - 1 else pltpu.roll(moved[k + 1], chunks + k, 1)
        ghosts = jnp.where(lane == k, low, jnp.where(lane == chunks + k, high, ghosts))
    turned = jnp.concatenate([ghosts, jnp.zeros((padded - comps, LANES), F32)], axis=0).T
    head = turned[0:3 * chunks, 0:LANES]
    tail = turned[0:3 * chunks, LANES:2 * LANES]
    mixed = tail[0:chunks] + pltpu.roll(tail[chunks:2 * chunks], STEP, 1) + pltpu.roll(tail[2 * chunks:3 * chunks], 2 * STEP, 1)
    for k in range(chunks):
        slab_ref[k, comps:comps + 1, :] = head[k:k + 1]
        slab_ref[k, comps + 1:comps + 2, :] = head[chunks + k:chunks + k + 1]
        slab_ref[k, comps + 2:comps + 3, :] = head[2 * chunks:2 * chunks + 1]
        slab_ref[k, comps + 3:comps + 4, :] = mixed[k:k + 1]
        slab_ref[k, comps + 4:comps + 5, :] = side_ref[0:1, k * LANES:(k + 1) * LANES]
        slab_ref[k, comps + 5:comps + 6, :] = jnp.zeros((1, LANES), F32)
        copy = pltpu.make_async_copy(slab_ref.at[k], out_ref.at[k], sems.at[k])
        copy.start()
        copies.append(copy)
    for copy in copies:
        copy.wait()


def stack_body(a_ref, b_ref, out_ref):
    half = a_ref.shape[1]
    for at, ref in ((0, a_ref), (half, b_ref)):
        for start in range(0, half, LANES):
            out_ref[at + start:at + start + LANES, :] = ref[:, start:start + LANES].T


def steps_body(packed_ref, stacked_ref, turned_ref, growth_ref, out_ref, slab_ref, both_ref, turned_a_ref, moved_ref, courant_ref, gain_ref, result_ref, sems):
    groups, rows, _ = slab_ref.shape
    comps = rows - 6
    total = moved_ref.shape[0]
    half = both_ref.shape[0] // 2
    rest = comps - LANES
    packed = pltpu.make_async_copy(packed_ref, slab_ref, sems.at[groups])
    stacked = pltpu.make_async_copy(stacked_ref, both_ref, sems.at[groups + 1])
    turned = pltpu.make_async_copy(turned_ref, turned_a_ref, sems.at[groups + 2])
    for copy in (packed, stacked, turned):
        copy.start()
    packed.wait()
    lane = iota((comps, LANES), 1)
    columns = jnp.concatenate([slab_ref[g, rows - 8:rows, :] for g in range(groups)] + [jnp.zeros((LANES - 8 * groups, LANES), F32)], axis=0).T
    for g in range(groups):
        start = g * comps
        moved_ref[start:start + comps, 0:LANES] = slab_ref[g, 0:comps, :]
        at = 8 * g + 2
        low, high, courant = (
            jnp.broadcast_to(jnp.concatenate([columns[:, at + i:at + i + 1], columns[STEP * i:STEP * i + rest, at + 3:at + 4]], axis=0), (comps, LANES))
            for i in range(3)
        )
        moved_ref[start:start + comps, LANES:2 * LANES] = jnp.where(lane == 0, low, jnp.where(lane == LANES - 1, high, 0.0))
        courant_ref[start:start + comps, :] = courant
    growth = growth_ref[...]
    width = growth.shape[1]
    gain_ref[...] = jnp.broadcast_to(jnp.broadcast_to(growth, (8, width)).T[:, 0:1], (total, LANES))

    def source(moved, gain):
        rounded = moved.astype(BF16)
        both = jnp.dot(both_ref[...], rounded, preferred_element_type=F32)
        pairs = (both[0:half] * both[half:2 * half]).astype(BF16)
        transfer = jnp.dot(turned_a_ref[...], pairs, preferred_element_type=F32)
        mean = jnp.sum(moved * moved, axis=0, keepdims=True) / total
        spread = jnp.sqrt(mean + 1e-06)
        scale = 1.0 / (1.0 + DISSIPATION * spread)
        return (moved + gain * moved + transfer) * scale

    gain = gain_ref[...]
    moved = moved_ref[...]
    stacked.wait()
    turned.wait()
    field = source(moved, jnp.concatenate([gain, gain], axis=1))
    field, ghost = field[:, 0:LANES], field[:, LANES:2 * LANES]
    lane = iota((total, LANES), 1)
    left = jnp.where(lane == 0, ghost, pltpu.roll(field, 1, 1))
    right = jnp.where(lane == LANES - 1, ghost, pltpu.roll(field, LANES - 1, 1))
    courant = courant_ref[...]
    speed = jnp.abs(courant)
    sea = slab_ref[0, rows - 2:rows - 1, :]
    moved = ((1.0 - speed) * field + speed * jnp.where(courant > 0, left, right)) * sea
    value = source(moved, gain)
    copies = []
    for g in range(groups):
        result_ref[g, :, :] = value[g * comps:(g + 1) * comps]
        copy = pltpu.make_async_copy(result_ref.at[g], out_ref.at[g], sems.at[g])
        copy.start()
        copies.append(copy)
    for copy in copies:
        copy.wait()


def gather_body(block_ref, column_ref, slab_ref, offsets_ref, out_ref):
    chunks, comps, _ = slab_ref.shape
    n = column_ref.shape[0]
    rows = SLAB * n
    slots = NB_BLOCK // n
    block = block_ref[0:1, 0:1]
    device = iota((n, 1), 0)
    start = jnp.sum(jnp.where(device < block, column_ref[...], 0), axis=0, keepdims=True)
    count = jnp.sum(jnp.where(device == block, column_ref[...], 0), axis=0, keepdims=True)
    shift = lax.rem(start, jnp.int32(n))
    lane = iota((1, rows), 1)
    at = lane // SLAB
    slot = lane % SLAB
    wraps = at < shift
    base = jnp.where(wraps, at - shift + n, at - shift)
    line = lax.div(start, jnp.int32(n)) + slot + jnp.where(wraps, 1, 0)
    table = offsets_ref[...]
    wanted = jnp.sum(jnp.where(iota(table.shape, 0) == line, table, 0), axis=0, keepdims=True)
    wanted = jnp.where(jnp.logical_and(slot < slots, base + n * slot < count), wanted, -1)
    point = iota((LANES, rows), 0)
    picked = jnp.zeros((comps, rows), F32)
    for k in range(chunks):
        chosen = (point + k * LANES == wanted).astype(F32).astype(BF16)
        picked = picked + exact_dot(slab_ref[k, :, :], chosen, ((1,), (0,)))
    side = 2 * LANES
    turned = jnp.concatenate([picked, jnp.zeros((side - comps, rows), F32)], axis=0).T
    out_ref[...] = fold(turned, slots, comps - LANES)


def fold(turned, slots, rest):
    rows = turned.shape[0]
    slot = iota((rows, LANES), 0) % SLAB
    lane = iota((rows, LANES), 1)
    main = turned[:, 0:LANES]
    side = turned[:, LANES:2 * LANES]
    out = jnp.where(slot < slots, main, 0.0)
    for t in range(slots):
        part = pltpu.roll(side, slots - t, 0)
        part = part if t == 0 else pltpu.roll(part, t * rest, 1)
        inside = jnp.logical_and(lane >= t * rest, lane < (t + 1) * rest)
        out = jnp.where(jnp.logical_and(slot == slots, inside), part, out)
    return out


def unfold(value, slots, rest):
    rows = value.shape[0]
    slot = iota((rows, LANES), 0) % SLAB
    lane = iota((rows, LANES), 1)
    side = jnp.zeros((rows, LANES), F32)
    for t in range(slots):
        part = pltpu.roll(value, rows - (slots - t), 0)
        part = part if t == 0 else pltpu.roll(part, LANES - t * rest, 1)
        side = jnp.where(jnp.logical_and(slot == t, lane < rest), part, side)
    return jnp.concatenate([jnp.where(slot < slots, value, 0.0), side], axis=1)


def relay_body(block_ref, column_ref, in_ref, out_ref, *, rest):
    rows = in_ref.shape[0]
    n = rows // SLAB
    slots = NB_BLOCK // n
    me = block_ref[0:1, 0:1]
    wide = jnp.broadcast_to(column_ref[...], (n, rows))
    source = iota((n, rows), 0)
    target = iota((n, rows), 1) // SLAB
    starts = jnp.sum(jnp.where(source < target, wide, 0), axis=0, keepdims=True)
    counts = jnp.sum(jnp.where(source == target, wide, 0), axis=0, keepdims=True)
    span = NB_BLOCK // 2
    slot = iota((1, rows), 1) % SLAB
    position = lax.rem(me - starts + 128 * n, jnp.int32(n)) + n * slot
    valid = jnp.logical_and(position < counts, slot < slots)
    entry = jnp.where(valid, starts + position, -(1 << 20))
    place = iota((rows, 1), 0)
    half = place % SLAB
    place = place // SLAB
    window = jnp.where(place < n // 2, span * place + counts[:, 0:1], span * (place - n // 2)) + n * half
    size = jnp.where(half == 0, n, jnp.where(half == 1, span - n, 0))
    inside = entry - window
    chosen = jnp.logical_and(inside >= 0, inside < size).astype(F32).astype(BF16)
    value = exact_pick(chosen, unfold(in_ref[...], slots, rest))
    out_ref[...] = fold(value, 2, rest)


def settle_body(block_ref, column_ref, in_ref, out_ref):
    comps, span = out_ref.shape
    rows = in_ref.shape[0]
    n = rows // SLAB
    block = block_ref[0:1, 0:1]
    row = iota((rows, LANES), 0)
    device = row // SLAB
    half = row % SLAB
    at = iota((rows, LANES), 1)
    window = jnp.where(block < n // 2, span * block + column_ref[0:1, 0:1], span * (block - n // 2))
    target = lax.rem(device - window + 256 * n, jnp.int32(n)) + n * half
    chosen = jnp.logical_and(at == target, half < 2).astype(F32).astype(BF16)
    value = exact_dot(unfold(in_ref[...], 2, comps - LANES).T, chosen, ((1,), (0,)))
    out_ref[...] = value[0:comps, 0:span]


def per_device(spectrum, courant, growth, quad_a, quad_b, sea_mask, nest_counts, nest_offsets):
    comps, points = spectrum.shape
    total = growth.shape[0]
    groups = lax.axis_size("comp")
    n = lax.axis_size("pts")
    chunks = points // LANES
    padded = 2 * LANES
    packed = jax.ShapeDtypeStruct((chunks, comps + 6, LANES), F32)
    edge = jax.ShapeDtypeStruct((8, padded), F32)
    slab = jax.ShapeDtypeStruct((SLAB * n, LANES), F32)

    side = jnp.concatenate([sea_mask.astype(F32), courant, jnp.zeros((points - comps,), F32)]).reshape(2, points)
    up, down = call(edges_body, (edge, edge), (VMEM, VMEM), (VMEM, VMEM))(spectrum, side)
    before = lax.ppermute(up, "pts", [(i, i + 1) for i in range(n - 1)])
    after = lax.ppermute(down, "pts", [(i + 1, i) for i in range(n - 1)])
    slabs = call(
        pack_body, packed, (VMEM,) * 4, HBM, scratch=(pltpu.VMEM(packed.shape, F32), pltpu.SemaphoreType.DMA((chunks,)))
    )(spectrum, side, before, after)
    slabs = lax.all_to_all(slabs, "comp", split_axis=0, concat_axis=0, tiled=True)

    both = call(stack_body, jax.ShapeDtypeStruct((2 * quad_a.shape[0], total), BF16), (VMEM, VMEM), vmem=16)(quad_a.T, quad_b.T)
    result = call(
        steps_body,
        jax.ShapeDtypeStruct((groups, comps, LANES), F32),
        (HBM, HBM, HBM, VMEM),
        HBM,
        scratch=(
            pltpu.VMEM(packed.shape, F32),
            pltpu.VMEM((2 * quad_a.shape[0], total), BF16),
            pltpu.VMEM((total, quad_a.shape[0]), BF16),
            pltpu.VMEM((total, 2 * LANES), F32),
            pltpu.VMEM((total, LANES), F32),
            pltpu.VMEM((total, LANES), F32),
            pltpu.VMEM((groups, comps, LANES), F32),
            pltpu.SemaphoreType.DMA((groups + 3,)),
        ),
        vmem=58,
    )(slabs, both, quad_a.T, growth.reshape(1, total))
    result = lax.all_to_all(result, "comp", split_axis=0, concat_axis=0, tiled=True)

    block = jnp.full((1, LANES), lax.axis_index("pts"), jnp.int32)
    column = nest_counts.reshape(n, 1)
    lines = jnp.repeat(jnp.pad(nest_offsets, (0, 4 * n)).reshape(-1, n), SLAB, axis=1)
    sent = call(gather_body, slab, (VMEM,) * 4)(block, column, result, lines)
    sent = lax.all_to_all(sent, "pts", split_axis=0, concat_axis=0, tiled=True)
    field = result.transpose(1, 0, 2).reshape(comps, points)
    sent = call(functools.partial(relay_body, rest=comps - LANES), slab, (VMEM,) * 3)(block, column, sent)
    sent = lax.all_to_all(sent, "pts", split_axis=0, concat_axis=0, tiled=True)
    nest = call(settle_body, jax.ShapeDtypeStruct((comps, NB_BLOCK // 2), F32), (VMEM,) * 3)(block, column, sent)
    return (field, nest)


def solution(mesh):
    return jax.shard_map(
        per_device,
        mesh=mesh,
        in_specs=(P("comp", "pts"), P("comp"), P(), P(), P(), P("pts"), P(), P()),
        out_specs=(P("comp", "pts"), P("comp", "pts")),
        check_vma=False,
    )
```

time: 124 us -> 121 us (0.976)
  blocking collectives: 0 us -> 24.2 us
  starting transfers between devices: 39 us -> 25.1 us
  waiting for transfers between devices: 56.6 us -> 48 us
  local copies, waits for them, and re-layouts: 12.2 us -> 5.8 us
  Pallas kernels: 14.7 us -> 16.2 us
    all_to_all x0 -> x1, blocking collectives: none -> 24.2 us  [per_device(): sent = lax.all_to_all(sent, 'pts', split_axis=0, concat_axis=0, tiled=True)]
    all_to_all x2 -> x1, starting transfers between devices: 18.9 us -> 4.88 us  [per_device(): sent = lax.all_to_all(sent, 'pts', split_axis=0, concat_axis=0, tiled=True)]
    all_to_all x2 -> x1, waiting for transfers between devices: 19.4 us -> 9.17 us  [per_device(): sent = lax.all_to_all(sent, 'pts', split_axis=0, concat_axis=0, tiled=True)]
    unnamed x26 -> x16, local copies, waits for them, and re-layouts: 11.7 us -> 3.91 us
    all_to_all x1, waiting for transfers between devices: 15.3 us -> 17 us  [per_device(): lax.all_to_all(slabs, 'comp', split_axis=0, concat_axis=0, tiled=True)]
    pallas_call x6 -> x7, Pallas kernels: 14.7 us -> 16.2 us  [the longest x1 9.74 us: per_device(): call(steps_body, jax.ShapeDtypeStruct((groups, comps, LANES), F32), (HBM,...]
  transfers between devices with their start and end apart: 6 -> 5, of which waited for: 5 -> 4; matrix products, arithmetic and copies ran while one was open for 5% -> 2% of each run, Pallas kernels for 0% -> 1%
where the time goes in v3:
time: 121 us
  waiting for transfers between devices  48 us (40%)
  starting transfers between devices  25.1 us (21%)
  blocking collectives  24.2 us (20%)
  Pallas kernels  16.2 us (13%)
  local copies, waits for them, and re-layouts  5.8 us (5%)
    all_to_all x1, blocking collectives, per_device(): sent = lax.all_to_all(sent, 'pts', split_axis=0, concat_axis=0, tiled=True)  24.2 us
    all_to_all x1, waiting for transfers between devices, per_device(): lax.all_to_all(result, 'comp', split_axis=0, concat_axis=0, tiled=True)  21 us
    all_to_all x1, waiting for transfers between devices, per_device(): lax.all_to_all(slabs, 'comp', split_axis=0, concat_axis=0, tiled=True)  17 us
    pallas_call x1, Pallas kernels, per_device(): call(steps_body, jax.ShapeDtypeStruct((groups, comps, LANES), F32), (HBM,...  9.74 us
    all_to_all x1, waiting for transfers between devices, per_device(): sent = lax.all_to_all(sent, 'pts', split_axis=0, concat_axis=0, tiled=True)  9.17 us
    all_to_all x1, starting transfers between devices, per_device(): lax.all_to_all(slabs, 'comp', split_axis=0, concat_axis=0, tiled=True)  6.33 us
    ppermute x1, starting transfers between devices, per_device(): before = lax.ppermute(up, 'pts', [(i, i + 1) for i in range(n - 1)])  5.65 us
    all_to_all x1, starting transfers between devices, per_device(): sent = lax.all_to_all(sent, 'pts', split_axis=0, concat_axis=0, tiled=True)  4.88 us
  transfers between devices with their start and end apart: 5, of which 4 were waited for; matrix products, arithmetic and copies ran while one was open for 2% of the time, Pallas kernels for 1%

profile of v3, /device:TPU:1, one launch (start us, length us, event | category | flops | bytes accessed | tf_op | source)
XLA Modules:
  0.0 120.7 jit_solution(17631689836740797467)
XLA Ops:
  0.6 0.7 convert_element_type.3
  1.3 0.8 concatenate.3
  2.1 0.0 copy-start.2
  2.1 1.1 copy-done.2
  3.2 0.0 copy-start.5
  3.2 0.0 copy-start.1
  3.2 0.0 copy-start.3
  3.2 0.1 shard_map.95
  3.3 5.6 %collective-permute-start = (f32[8,256]{1,0:T(8,128)S(1)}, f32[8,256]{1,0:T(8,128)S(1)}, u32[]{:S(2)}, u32[]{:S(2)}) collective-permute-start(f32[8,256]{1,0:T(8,128)S(1)} %get-tuple-element.4), channel_id=1, source_target_pairs={{0,1},{1,2},{2,3},{3,4},{4,5},{5,6},{6,7},{7,8},{8,9},{9,10},{10,1... | collective-permute-start | bytes 24584 | tf_op jit(solution)/shard_map/ppermute | solution.py:311
  9.0 4.7 %collective-permute-start.1 = (f32[8,256]{1,0:T(8,128)S(1)}, f32[8,256]{1,0:T(8,128)S(1)}, u32[]{:S(2)}, u32[]{:S(2)}) collective-permute-start(f32[8,256]{1,0:T(8,128)S(1)} %get-tuple-element.5), channel_id=1, source_target_pairs={{1,0},{2,1},{3,2},{4,3},{5,4},{6,5},{7,6},{8,7},{9,8},{10,9},{11,1... | collective-permute-start | bytes 24584 | tf_op jit(solution)/shard_map/ppermute | solution.py:312
  13.6 0.0 collective-permute-done.before_ref
  13.6 0.8 collective-permute-done.1.after_ref
  14.4 2.1 %shard_map.96 = f32[8,168,128]{2,1,0:T(8,128)} custom-call(f32[162,1024]{1,0:T(8,128)S(1)} %copy-done.2, f32[2,1024]{1,0:T(2,128)S(1)} %reshape.26.side_ref, f32[8,256]{1,0:T(8,128)S(1)} %collective-permute-done.before_ref, f32[8,256]{1,0:T(8,128)S(1)} %collective-permute-done.1.after_ref), custom_call_target="tpu_custom_call" | custom-call | flops 1000000 | bytes 1000000 | tf_op jit(solution)/shard_map/pallas_call | solution.py:313
  16.6 6.3 %all-to-all-start = ((f32[8,168,128]{2,1,0:T(8,128)}), f32[8,168,128]{2,1,0:T(8,128)}, u32[]{:S(2)}, u32[]{:S(2)}) async-start(f32[8,168,128]{2,1,0:T(8,128)} %shard_map.96), calls=%async_computation | async-start | bytes 1376256 | tf_op jit(solution)/shard_map/all_to_all | solution.py:316
  22.9 0.0 copy-done.5
  22.9 0.6 reshape.27.growth_ref
  23.5 0.0 copy-done.1
  23.5 0.0 copy-done.3
  23.5 1.0 shard_map.97.stacked_ref
  24.5 0.0 copy-start
  24.5 1.8 %copy-done = bf16[1280,1296]{1,0:T(8,128)(2,1)} copy-done((bf16[1280,1296]{1,0:T(8,128)(2,1)}, bf16[1280,1296]{1,0:T(8,128)(2,1)S(1)}, u32[]{:S(2)}) %copy-start) | copy-done | bytes 3317784
  26.3 0.0 copy-start.6
  26.3 0.0 copy-start.4
  26.3 17.0 %all-to-all-done.packed_ref = f32[8,168,128]{2,1,0:T(8,128)} async-done(((f32[8,168,128]{2,1,0:T(8,128)}), f32[8,168,128]{2,1,0:T(8,128)}, u32[]{:S(2)}, u32[]{:S(2)}) %all-to-all-start) | async-done | bytes 688160 | tf_op jit(solution)/shard_map/all_to_all | solution.py:316
  43.3 9.7 %shard_map.98 = f32[8,162,128]{2,1,0:T(8,128)} custom-call(f32[8,168,128]{2,1,0:T(8,128)} %all-to-all-done.packed_ref, bf16[1280,1296]{1,0:T(8,128)(2,1)} %copy-done, bf16[1296,640]{1,0:T(8,128)(2,1)} %bitcast.12, f32[1,1296]{1,0:T(1,128)} %reshape.27.growth_ref), custom_call_target="tpu_custom_call" | custom-call | flops 1000000 | bytes 1000000 | tf_op jit(solution)/shard_map/pallas_call | solution.py:319
  53.1 3.6 %all-to-all-start.1 = ((f32[8,162,128]{2,1,0:T(8,128)}), f32[8,162,128]{2,1,0:T(8,128)S(1)}, u32[]{:S(2)}, u32[]{:S(2)}) async-start(f32[8,162,128]{2,1,0:T(8,128)} %shard_map.98), calls=%async_computation.1 | async-start | bytes 1376256 | tf_op jit(solution)/shard_map/all_to_all | solution.py:336
  56.6 0.0 copy-done.6
  56.7 0.1 copy.18.column_ref
  56.8 0.0 copy-done.4
  56.8 0.1 reshape.30
  56.8 0.1 copy.14
  57.0 0.1 copy.16.offsets_ref
  57.1 21.0 %all-to-all-done.1.slab_ref = f32[8,162,128]{2,1,0:T(8,128)S(1)} async-done(((f32[8,162,128]{2,1,0:T(8,128)}), f32[8,162,128]{2,1,0:T(8,128)S(1)}, u32[]{:S(2)}, u32[]{:S(2)}) %all-to-all-start.1) | async-done | bytes 663584 | tf_op jit(solution)/shard_map/all_to_all | solution.py:336
  78.0 1.0 shard_map.99
  79.1 24.2 %all_to_all.32 = f32[64,4,128]{2,1,0:T(4,128)S(1)} all-to-all(f32[64,4,128]{2,1,0:T(4,128)S(1)} %bitcast.16), channel_id=1, replica_groups=mesh['comp'=8,'pts'=64] {'pts'}, dimensions={0} | all-to-all | bytes 262144 | tf_op jit(solution)/shard_map/all_to_all | solution.py:342
  103.3 1.2 shard_map.100
  104.4 4.9 %all-to-all-start.3 = ((f32[64,4,128]{2,1,0:T(4,128)}), f32[64,4,128]{2,1,0:T(4,128)S(1)}, u32[]{:S(2)}, u32[]{:S(2)}) async-start(f32[64,4,128]{2,1,0:T(4,128)} %bitcast.7), calls=%async_computation.3 | async-start | bytes 262144 | tf_op jit(solution)/shard_map/all_to_all | solution.py:345
  109.3 0.1 copy.13
  109.5 1.0 copy.19
  110.5 9.2 %all-to-all-done.3 = f32[64,4,128]{2,1,0:T(4,128)S(1)} async-done(((f32[64,4,128]{2,1,0:T(4,128)}), f32[64,4,128]{2,1,0:T(4,128)S(1)}, u32[]{:S(2)}, u32[]{:S(2)}) %all-to-all-start.3) | async-done | bytes 131104 | tf_op jit(solution)/shard_map/all_to_all | solution.py:345
  119.7 1.0 shard_map.101
  (6 shorter events, 0.1 us)
Async XLA Ops:
  2.1 1.1 copy-start.2
  3.2 19.7 %copy-start.5 = (f32[1296]{0:T(1024)S(1)}, f32[1296]{0:T(1024)}, u32[]{:S(2)}) copy-start(f32[1296]{0:T(1024)} %param.10) | copy-start | bytes 15556
  3.2 20.3 %copy-start.1 = (bf16[640,1296]{0,1:T(8,128)(2,1)S(1)}, bf16[640,1296]{0,1:T(8,128)(2,1)}, u32[]{:S(2)}) copy-start(bf16[640,1296]{0,1:T(8,128)(2,1)} %param.11) | copy-start | bytes 4976644
  3.2 20.3 %copy-start.3 = (bf16[640,1296]{0,1:T(8,128)(2,1)S(1)}, bf16[640,1296]{0,1:T(8,128)(2,1)}, u32[]{:S(2)}) copy-start(bf16[640,1296]{0,1:T(8,128)(2,1)} %param.12) | copy-start | bytes 4976644
  3.3 10.3 %collective-permute-start = (f32[8,256]{1,0:T(8,128)S(1)}, f32[8,256]{1,0:T(8,128)S(1)}, u32[]{:S(2)}, u32[]{:S(2)}) collective-permute-start(f32[8,256]{1,0:T(8,128)S(1)} %get-tuple-element.4), channel_id=1, source_target_pairs={{0,1},{1,2},{2,3},{3,4},{4,5},{5,6},{6,7},{7,8},{8,9},{9,10},{10,1... | collective-permute-start | bytes 24584 | tf_op jit(solution)/shard_map/ppermute | solution.py:311
  9.0 5.5 %collective-permute-start.1 = (f32[8,256]{1,0:T(8,128)S(1)}, f32[8,256]{1,0:T(8,128)S(1)}, u32[]{:S(2)}, u32[]{:S(2)}) collective-permute-start(f32[8,256]{1,0:T(8,128)S(1)} %get-tuple-element.5), channel_id=1, source_target_pairs={{1,0},{2,1},{3,2},{4,3},{5,4},{6,5},{7,6},{8,7},{9,8},{10,9},{11,1... | collective-permute-start | bytes 24584 | tf_op jit(solution)/shard_map/ppermute | solution.py:312
  16.6 26.8 %all-to-all-start = ((f32[8,168,128]{2,1,0:T(8,128)}), f32[8,168,128]{2,1,0:T(8,128)}, u32[]{:S(2)}, u32[]{:S(2)}) async-start(f32[8,168,128]{2,1,0:T(8,128)} %shard_map.96), calls=%async_computation | async-start | bytes 1376256 | tf_op jit(solution)/shard_map/all_to_all | solution.py:316
  24.5 1.8 %copy-start = (bf16[1280,1296]{1,0:T(8,128)(2,1)}, bf16[1280,1296]{1,0:T(8,128)(2,1)S(1)}, u32[]{:S(2)}) copy-start(bf16[1280,1296]{1,0:T(8,128)(2,1)S(1)} %shard_map.97.stacked_ref) | copy-start | bytes 9953284
  26.3 30.3 %copy-start.6 = (s32[64]{0:T(128)S(1)}, s32[64]{0:T(128)}, u32[]{:S(2)}) copy-start(s32[64]{0:T(128)} %param.14) | copy-start | bytes 772
  26.3 30.4 %copy-start.4 = (s32[6144]{0:T(1024)S(1)}, s32[6144]{0:T(1024)}, u32[]{:S(2)}) copy-start(s32[6144]{0:T(1024)} %param.15) | copy-start | bytes 73732
  53.1 25.0 %all-to-all-start.1 = ((f32[8,162,128]{2,1,0:T(8,128)}), f32[8,162,128]{2,1,0:T(8,128)S(1)}, u32[]{:S(2)}, u32[]{:S(2)}) async-start(f32[8,162,128]{2,1,0:T(8,128)} %shard_map.98), calls=%async_computation.1 | async-start | bytes 1376256 | tf_op jit(solution)/shard_map/all_to_all | solution.py:336
  104.4 15.2 %all-to-all-start.3 = ((f32[64,4,128]{2,1,0:T(4,128)}), f32[64,4,128]{2,1,0:T(4,128)S(1)}, u32[]{:S(2)}, u32[]{:S(2)}) async-start(f32[64,4,128]{2,1,0:T(4,128)} %bitcast.7), calls=%async_computation.3 | async-start | bytes 262144 | tf_op jit(solution)/shard_map/all_to_all | solution.py:345

commit v4 on v3

--- a/solution.py
+++ b/solution.py
@@ -11,6 +11,7 @@
 LANES = 128
 NB_BLOCK = 192
 SLAB = 4
+BLOCK = 336
 DISSIPATION = 0.5
 
 F32 = jnp.float32
@@ -113,10 +114,10 @@
     turned = jnp.concatenate([ghosts, jnp.zeros((padded - comps, LANES), F32)], axis=0).T
     head = turned[0:3 * chunks, 0:LANES]
     tail = turned[0:3 * chunks, LANES:2 * LANES]
-    mixed = tail[0:chunks] + pltpu.roll(tail[chunks:2 * chunks], STEP, 1) + pltpu.roll(tail[2 * chunks:3 * chunks], 2 * STEP, 1)
+    mixed = tail[chunks:2 * chunks] + pltpu.roll(tail[0:chunks], STEP, 1) + pltpu.roll(tail[2 * chunks:3 * chunks], 2 * STEP, 1)
     for k in range(chunks):
-        slab_ref[k, comps:comps + 1, :] = head[k:k + 1]
-        slab_ref[k, comps + 1:comps + 2, :] = head[chunks + k:chunks + k + 1]
+        slab_ref[k, comps:comps + 1, :] = head[chunks + k:chunks + k + 1]
+        slab_ref[k, comps + 1:comps + 2, :] = head[k:k + 1]
         slab_ref[k, comps + 2:comps + 3, :] = head[2 * chunks:2 * chunks + 1]
         slab_ref[k, comps + 3:comps + 4, :] = mixed[k:k + 1]
         slab_ref[k, comps + 4:comps + 5, :] = side_ref[0:1, k * LANES:(k + 1) * LANES]
@@ -128,69 +129,85 @@
         copy.wait()
 
 
-def stack_body(a_ref, b_ref, out_ref):
-    half = a_ref.shape[1]
+def stack_body(a_ref, b_ref, growth_ref, both_ref, turned_ref, gain_ref, *, comps):
+    total, half = a_ref.shape
+    rows = comps + 6
+    groups = total // comps
+    gap = jnp.zeros((rows - comps, half), F32)
     for at, ref in ((0, a_ref), (half, b_ref)):
+        whole = ref[...].astype(F32)
+        spread = jnp.concatenate([part for g in range(groups) for part in (whole[g * comps:(g + 1) * comps], gap)], axis=0)
+        if at == 0:
+            turned_ref[...] = spread.astype(BF16)
         for start in range(0, half, LANES):
-            out_ref[at + start:at + start + LANES, :] = ref[:, start:start + LANES].T
-
-
-def steps_body(packed_ref, stacked_ref, turned_ref, growth_ref, out_ref, slab_ref, both_ref, turned_a_ref, moved_ref, courant_ref, gain_ref, result_ref, sems):
-    groups, rows, _ = slab_ref.shape
-    comps = rows - 6
-    total = moved_ref.shape[0]
+            both_ref[at + start:at + start + LANES, :] = spread[:, start:start + LANES].T.astype(BF16)
+    growth = growth_ref[...]
+    column = jnp.broadcast_to(growth, (8, total)).T[:, 0:1]
+    for g in range(groups):
+        gain_ref[g * rows:g * rows + comps, :] = jnp.broadcast_to(column[g * comps:(g + 1) * comps], (comps, LANES))
+        gain_ref[g * rows + comps:(g + 1) * rows, :] = jnp.zeros((rows - comps, LANES), F32)
+
+
+def steps_body(
+    packed_ref, stacked_ref, turned_ref, gains_ref, out_ref, slab_ref, both_ref, turned_a_ref, gain_ref, ghost_ref, again_ref, courant_ref, sems, *, comps
+):
+    padded = slab_ref.shape[0]
+    rows = comps + 6
+    groups = padded // rows
+    total = groups * comps
     half = both_ref.shape[0] // 2
-    rest = comps - LANES
-    packed = pltpu.make_async_copy(packed_ref, slab_ref, sems.at[groups])
-    stacked = pltpu.make_async_copy(stacked_ref, both_ref, sems.at[groups + 1])
-    turned = pltpu.make_async_copy(turned_ref, turned_a_ref, sems.at[groups + 2])
-    for copy in (packed, stacked, turned):
+    loads = ((packed_ref, slab_ref), (gains_ref, gain_ref), (stacked_ref, both_ref), (turned_ref, turned_a_ref))
+    copies = [pltpu.make_async_copy(source, target, sems.at[i]) for i, (source, target) in enumerate(loads)]
+    for copy in copies:
         copy.start()
-    packed.wait()
-    lane = iota((comps, LANES), 1)
-    columns = jnp.concatenate([slab_ref[g, rows - 8:rows, :] for g in range(groups)] + [jnp.zeros((LANES - 8 * groups, LANES), F32)], axis=0).T
+    copies[0].wait()
+    lane = iota((rows - LANES, LANES), 1)
+    columns = jnp.concatenate([slab_ref[(g + 1) * rows - 8:(g + 1) * rows, :] for g in range(groups)] + [jnp.zeros((LANES - 8 * groups, LANES), F32)], axis=0).T
     for g in range(groups):
-        start = g * comps
-        moved_ref[start:start + comps, 0:LANES] = slab_ref[g, 0:comps, :]
+        start = g * rows
         at = 8 * g + 2
-        low, high, courant = (
-            jnp.broadcast_to(jnp.concatenate([columns[:, at + i:at + i + 1], columns[STEP * i:STEP * i + rest, at + 3:at + 4]], axis=0), (comps, LANES))
-            for i in range(3)
+        tail = columns[:, at + 3:at + 4]
+        high, low, courant = (jnp.broadcast_to(tail[STEP * i:STEP * (i + 1)], (STEP, LANES)) for i in range(3))
+        ghost_ref[start:start + LANES, :] = pltpu.roll(columns, LANES - at - 1, 1)
+        ghost_ref[start + LANES:start + rows, :] = jnp.where(lane == 0, low, high)
+        courant_ref[start:start + LANES, :] = jnp.broadcast_to(columns[:, at + 2:at + 3], (LANES, LANES))
+        courant_ref[start + LANES:start + rows, :] = courant
+    blocks = [slice(start, start + BLOCK) for start in range(0, padded, BLOCK)]
+
+    def pairs_and_scale(refs):
+        rounded = jnp.concatenate([ref[...].astype(BF16) for ref in refs], axis=1)
+        left = jnp.dot(both_ref[0:half, :], rounded, preferred_element_type=F32)
+        right = jnp.dot(both_ref[half:2 * half, :], rounded, preferred_element_type=F32)
+        squares = jnp.concatenate(
+            [sum(jnp.sum(jnp.square(ref[g * rows:g * rows + comps, :]), axis=0, keepdims=True) for g in range(groups)) for ref in refs], axis=1
         )
-        moved_ref[start:start + comps, LANES:2 * LANES] = jnp.where(lane == 0, low, jnp.where(lane == LANES - 1, high, 0.0))
-        courant_ref[start:start + comps, :] = courant
-    growth = growth_ref[...]
-    width = growth.shape[1]
-    gain_ref[...] = jnp.broadcast_to(jnp.broadcast_to(growth, (8, width)).T[:, 0:1], (total, LANES))
-
-    def source(moved, gain):
-        rounded = moved.astype(BF16)
-        both = jnp.dot(both_ref[...], rounded, preferred_element_type=F32)
-        pairs = (both[0:half] * both[half:2 * half]).astype(BF16)
-        transfer = jnp.dot(turned_a_ref[...], pairs, preferred_element_type=F32)
-        mean = jnp.sum(moved * moved, axis=0, keepdims=True) / total
-        spread = jnp.sqrt(mean + 1e-06)
-        scale = 1.0 / (1.0 + DISSIPATION * spread)
-        return (moved + gain * moved + transfer) * scale
-
-    gain = gain_ref[...]
-    moved = moved_ref[...]
-    stacked.wait()
-    turned.wait()
-    field = source(moved, jnp.concatenate([gain, gain], axis=1))
-    field, ghost = field[:, 0:LANES], field[:, LANES:2 * LANES]
-    lane = iota((total, LANES), 1)
-    left = jnp.where(lane == 0, ghost, pltpu.roll(field, 1, 1))
-    right = jnp.where(lane == LANES - 1, ghost, pltpu.roll(field, LANES - 1, 1))
-    courant = courant_ref[...]
-    speed = jnp.abs(courant)
-    sea = slab_ref[0, rows - 2:rows - 1, :]
-    moved = ((1.0 - speed) * field + speed * jnp.where(courant > 0, left, right)) * sea
-    value = source(moved, gain)
+        spread = jnp.sqrt(squares / total + 1e-06)
+        return (left * right).astype(BF16), 1.0 / (1.0 + DISSIPATION * spread)
+
+    for copy in copies[1:]:
+        copy.wait()
+    pairs, scale = pairs_and_scale((slab_ref, ghost_ref))
+    lane = iota((BLOCK, LANES), 1)
+    sea = slab_ref[rows - 2:rows - 1, :]
+    for block in blocks:
+        gain = gain_ref[block, :]
+        transfer = jnp.dot(turned_a_ref[block, :], pairs, preferred_element_type=F32)
+        field, ghost = (
+            (ref[block, :] + gain * ref[block, :] + transfer[:, i * LANES:(i + 1) * LANES]) * scale[:, i * LANES:(i + 1) * LANES]
+            for i, ref in enumerate((slab_ref, ghost_ref))
+        )
+        left = jnp.where(lane == 0, ghost, pltpu.roll(field, 1, 1))
+        right = jnp.where(lane == LANES - 1, ghost, pltpu.roll(field, LANES - 1, 1))
+        courant = courant_ref[block, :]
+        speed = jnp.abs(courant)
+        again_ref[block, :] = ((1.0 - speed) * field + speed * jnp.where(courant > 0, left, right)) * sea
+    pairs, scale = pairs_and_scale((again_ref,))
     copies = []
-    for g in range(groups):
-        result_ref[g, :, :] = value[g * comps:(g + 1) * comps]
-        copy = pltpu.make_async_copy(result_ref.at[g], out_ref.at[g], sems.at[g])
+    for i, block in enumerate(blocks):
+        moved = again_ref[block, :]
+        transfer = jnp.dot(turned_a_ref[block, :], pairs, preferred_element_type=F32)
+        courant_ref[block, :] = (moved + gain_ref[block, :] * moved + transfer) * scale
+        copy = pltpu.make_async_copy(courant_ref.at[block], out_ref.at[block], sems.at[len(loads) + i])
         copy.start()
         copies.append(copy)
     for copy in copies:
@@ -198,7 +215,8 @@
 
 
 def gather_body(block_ref, column_ref, slab_ref, offsets_ref, out_ref):
-    chunks, comps, _ = slab_ref.shape
+    chunks = slab_ref.shape[0]
+    comps = slab_ref.shape[1] - 6
     n = column_ref.shape[0]
     rows = SLAB * n
     slots = NB_BLOCK // n
@@ -220,7 +238,7 @@
     picked = jnp.zeros((comps, rows), F32)
     for k in range(chunks):
         chosen = (point + k * LANES == wanted).astype(F32).astype(BF16)
-        picked = picked + exact_dot(slab_ref[k, :, :], chosen, ((1,), (0,)))
+        picked = picked + exact_dot(slab_ref[k, 0:comps, :], chosen, ((1,), (0,)))
     side = 2 * LANES
     turned = jnp.concatenate([picked, jnp.zeros((side - comps, rows), F32)], axis=0).T
     out_ref[...] = fold(turned, slots, comps - LANES)
@@ -315,24 +333,34 @@
     )(spectrum, side, before, after)
     slabs = lax.all_to_all(slabs, "comp", split_axis=0, concat_axis=0, tiled=True)
 
-    both = call(stack_body, jax.ShapeDtypeStruct((2 * quad_a.shape[0], total), BF16), (VMEM, VMEM), vmem=16)(quad_a.T, quad_b.T)
+    rows = groups * (comps + 6)
+    half = quad_a.shape[0]
+    wide = jax.ShapeDtypeStruct((rows, LANES), F32)
+    both, turned_a, gain = call(
+        functools.partial(stack_body, comps=comps),
+        (jax.ShapeDtypeStruct((2 * half, rows), BF16), jax.ShapeDtypeStruct((rows, half), BF16), wide),
+        (VMEM, VMEM, VMEM),
+        (VMEM, VMEM, VMEM),
+        vmem=40,
+    )(quad_a.T, quad_b.T, growth.reshape(1, total))
     result = call(
-        steps_body,
-        jax.ShapeDtypeStruct((groups, comps, LANES), F32),
-        (HBM, HBM, HBM, VMEM),
+        functools.partial(steps_body, comps=comps),
+        wide,
+        (HBM, HBM, HBM, HBM),
         HBM,
         scratch=(
-            pltpu.VMEM(packed.shape, F32),
-            pltpu.VMEM((2 * quad_a.shape[0], total), BF16),
-            pltpu.VMEM((total, quad_a.shape[0]), BF16),
-            pltpu.VMEM((total, 2 * LANES), F32),
-            pltpu.VMEM((total, LANES), F32),
-            pltpu.VMEM((total, LANES), F32),
-            pltpu.VMEM((groups, comps, LANES), F32),
-            pltpu.SemaphoreType.DMA((groups + 3,)),
+            pltpu.VMEM((rows, LANES), F32),
+            pltpu.VMEM((2 * half, rows), BF16),
+            pltpu.VMEM((rows, half), BF16),
+            pltpu.VMEM((rows, LANES), F32),
+            pltpu.VMEM((rows, LANES), F32),
+            pltpu.VMEM((rows, LANES), F32),
+            pltpu.VMEM((rows, LANES), F32),
+            pltpu.SemaphoreType.DMA((4 + rows // BLOCK,)),
         ),
         vmem=58,
-    )(slabs, both, quad_a.T, growth.reshape(1, total))
+    )(slabs.reshape(rows, LANES), both, turned_a, gain)
+    result = result.reshape(packed.shape)
     result = lax.all_to_all(result, "comp", split_axis=0, concat_axis=0, tiled=True)
 
     block = jnp.full((1, LANES), lax.axis_index("pts"), jnp.int32)
@@ -340,7 +368,7 @@
     lines = jnp.repeat(jnp.pad(nest_offsets, (0, 4 * n)).reshape(-1, n), SLAB, axis=1)
     sent = call(gather_body, slab, (VMEM,) * 4)(block, column, result, lines)
     sent = lax.all_to_all(sent, "pts", split_axis=0, concat_axis=0, tiled=True)
-    field = result.transpose(1, 0, 2).reshape(comps, points)
+    field = result[:, 0:comps].transpose(1, 0, 2).reshape(comps, points)
     sent = call(functools.partial(relay_body, rest=comps - LANES), slab, (VMEM,) * 3)(block, column, sent)
     sent = lax.all_to_all(sent, "pts", split_axis=0, concat_axis=0, tiled=True)
     nest = call(settle_body, jax.ShapeDtypeStruct((comps, NB_BLOCK // 2), F32), (VMEM,) * 3)(block, column, sent)

time: 121 us -> 119 us (0.983)
  waiting for transfers between devices: 48 us -> 45.9 us
  Pallas kernels: 16.2 us -> 14.3 us
  local copies, waits for them, and re-layouts: 5.8 us -> 7.33 us
    unnamed x16 -> x20, local copies, waits for them, and re-layouts: 3.91 us -> 5.99 us
    all_to_all x1, waiting for transfers between devices: 17 us -> 15 us  [per_device(): lax.all_to_all(slabs, 'comp', split_axis=0, concat_axis=0, tiled=True)]
    pallas_call x2, Pallas kernels: 10.7 us -> 8.78 us  [the longest x1 7.25 us: per_device(): call(functools.partial(steps_body, comps=comps), wide, (HBM, HBM, HBM, HB...]
  transfers between devices with their start and end apart: 5 -> 5, of which waited for: 4 -> 4; matrix products, arithmetic and copies ran while one was open for 2% -> 1% of each run, Pallas kernels for 1% -> 1%
where the time goes in v4:
time: 119 us; the launch traced here: 118 us
  waiting for transfers between devices  45.9 us (39%)
  starting transfers between devices  25.1 us (21%)
  blocking collectives  24.2 us (20%)
  Pallas kernels  14.3 us (12%)
  local copies, waits for them, and re-layouts  7.33 us (6%)
    all_to_all x1, blocking collectives, per_device(): sent = lax.all_to_all(sent, 'pts', split_axis=0, concat_axis=0, tiled=True)  24.2 us
    all_to_all x1, waiting for transfers between devices, per_device(): lax.all_to_all(result, 'comp', split_axis=0, concat_axis=0, tiled=True)  21 us
    all_to_all x1, waiting for transfers between devices, per_device(): lax.all_to_all(slabs, 'comp', split_axis=0, concat_axis=0, tiled=True)  15 us
    all_to_all x1, waiting for transfers between devices, per_device(): sent = lax.all_to_all(sent, 'pts', split_axis=0, concat_axis=0, tiled=True)  9.12 us
    pallas_call x1, Pallas kernels, per_device(): call(functools.partial(steps_body, comps=comps), wide, (HBM, HBM, HBM, HB...  7.25 us
    all_to_all x1, starting transfers between devices, per_device(): lax.all_to_all(slabs, 'comp', split_axis=0, concat_axis=0, tiled=True)  6.33 us
    unnamed x20, local copies, waits for them, and re-layouts  5.99 us
    ppermute x1, starting transfers between devices, per_device(): before = lax.ppermute(up, 'pts', [(i, i + 1) for i in range(n - 1)])  5.65 us
  transfers between devices with their start and end apart: 5, of which 4 were waited for; matrix products, arithmetic and copies ran while one was open for 1% of the time, Pallas kernels for 1%

profile of v4, /device:TPU:1, one launch (start us, length us, event | category | flops | bytes accessed | tf_op | source)
XLA Modules:
  0.0 118.2 jit_solution(3759119959353266937)
XLA Ops:
  0.6 0.7 convert_element_type.3
  1.3 0.8 concatenate.3
  2.1 0.0 copy-start.1
  2.1 1.1 copy-done.1
  3.2 0.0 copy-start.7
  3.2 0.0 copy-start.3
  3.2 0.0 copy-start.4
  3.2 0.1 shard_map.95
  3.3 5.6 %collective-permute-start = (f32[8,256]{1,0:T(8,128)S(1)}, f32[8,256]{1,0:T(8,128)S(1)}, u32[]{:S(2)}, u32[]{:S(2)}) collective-permute-start(f32[8,256]{1,0:T(8,128)S(1)} %get-tuple-element.7), channel_id=1, source_target_pairs={{0,1},{1,2},{2,3},{3,4},{4,5},{5,6},{6,7},{7,8},{8,9},{9,10},{10,1... | collective-permute-start | bytes 24584 | tf_op jit(solution)/shard_map/ppermute | solution.py:329
  9.0 4.7 %collective-permute-start.1 = (f32[8,256]{1,0:T(8,128)S(1)}, f32[8,256]{1,0:T(8,128)S(1)}, u32[]{:S(2)}, u32[]{:S(2)}) collective-permute-start(f32[8,256]{1,0:T(8,128)S(1)} %get-tuple-element.8), channel_id=1, source_target_pairs={{1,0},{2,1},{3,2},{4,3},{5,4},{6,5},{7,6},{8,7},{9,8},{10,9},{11,1... | collective-permute-start | bytes 24584 | tf_op jit(solution)/shard_map/ppermute | solution.py:330
  13.6 0.0 collective-permute-done.before_ref
  13.6 0.8 collective-permute-done.1.after_ref
  14.4 2.1 %shard_map.96 = f32[8,168,128]{2,1,0:T(8,128)} custom-call(f32[162,1024]{1,0:T(8,128)S(1)} %copy-done.1, f32[2,1024]{1,0:T(2,128)S(1)} %reshape.32.side_ref, f32[8,256]{1,0:T(8,128)S(1)} %collective-permute-done.before_ref, f32[8,256]{1,0:T(8,128)S(1)} %collective-permute-done.1.after_ref), custom_call_target="tpu_custom_call" | custom-call | flops 1000000 | bytes 1000000 | tf_op jit(solution)/shard_map/pallas_call | solution.py:331
  16.6 6.3 %all-to-all-start = ((f32[8,168,128]{2,1,0:T(8,128)}), f32[8,168,128]{2,1,0:T(8,128)}, u32[]{:S(2)}, u32[]{:S(2)}) async-start(f32[8,168,128]{2,1,0:T(8,128)} %shard_map.96), calls=%async_computation | async-start | bytes 1376256 | tf_op jit(solution)/shard_map/all_to_all | solution.py:334
  22.9 0.0 copy-done.7
  22.9 0.0 copy-done.3
  22.9 0.0 copy-done.4
  22.9 1.5 %shard_map.97 = (bf16[1280,1344]{1,0:T(8,128)(2,1)S(1)}, bf16[1344,640]{1,0:T(8,128)(2,1)S(1)}, f32[1344,128]{1,0:T(8,128)S(1)}) custom-call(bf16[1296,640]{1,0:T(8,128)(2,1)S(1)} %bitcast.15, bf16[1296,640]{1,0:T(8,128)(2,1)S(1)} %bitcast.16, f32[1,1296]{1,0:T(1,128)S(1)} %reshape.34.growth_ref), custom_call_target="tpu_custom_call" | custom-call | flops 1000000 | bytes 1000000 | tf_op jit(solution)/shard_map/pallas_call | solution.py:339
  24.5 0.0 copy-start
  24.5 1.8 %copy-done = bf16[1280,1344]{1,0:T(8,128)(2,1)} copy-done((bf16[1280,1344]{1,0:T(8,128)(2,1)}, bf16[1280,1344]{1,0:T(8,128)(2,1)S(1)}, u32[]{:S(2)}) %copy-start) | copy-done | bytes 3440664
  26.3 0.0 copy-start.2
  26.3 1.2 %copy-done.2 = bf16[1344,640]{1,0:T(8,128)(2,1)} copy-done((bf16[1344,640]{1,0:T(8,128)(2,1)}, bf16[1344,640]{1,0:T(8,128)(2,1)S(1)}, u32[]{:S(2)}) %copy-start.2) | copy-done | bytes 1720344
  27.5 0.0 copy-start.5
  27.5 0.9 copy-done.5
  28.4 15.0 %all-to-all-done = f32[8,168,128]{2,1,0:T(8,128)} async-done(((f32[8,168,128]{2,1,0:T(8,128)}), f32[8,168,128]{2,1,0:T(8,128)}, u32[]{:S(2)}, u32[]{:S(2)}) %all-to-all-start) | async-done | bytes 688160 | tf_op jit(solution)/shard_map/all_to_all | solution.py:334
  43.3 0.0 copy-start.8
  43.3 0.0 copy-start.6
  43.3 7.2 %shard_map.98 = f32[1344,128]{1,0:T(8,128)} custom-call(f32[1344,128]{1,0:T(8,128)} %bitcast.packed_ref, bf16[1280,1344]{1,0:T(8,128)(2,1)} %copy-done, bf16[1344,640]{1,0:T(8,128)(2,1)} %copy-done.2, f32[1344,128]{1,0:T(8,128)} %copy-done.5), custom_call_target="tpu_custom_call" | custom-call | flops 1000000 | bytes 1000000 | tf_op jit(solution)/shard_map/pallas_call | solution.py:346
  50.6 3.6 %all-to-all-start.1 = ((f32[8,168,128]{2,1,0:T(8,128)}), f32[8,168,128]{2,1,0:T(8,128)S(1)}, u32[]{:S(2)}, u32[]{:S(2)}) async-start(f32[8,168,128]{2,1,0:T(8,128)} %bitcast.20), calls=%async_computation.1 | async-start | bytes 1376256 | tf_op jit(solution)/shard_map/all_to_all | solution.py:364
  54.2 0.0 copy-done.8
  54.2 0.1 copy.18.column_ref
  54.3 0.0 copy-done.6
  54.3 0.1 reshape.38
  54.4 0.1 copy.14
  54.5 0.1 copy.16.offsets_ref
  54.6 21.0 %all-to-all-done.1.slab_ref = f32[8,168,128]{2,1,0:T(8,128)S(1)} async-done(((f32[8,168,128]{2,1,0:T(8,128)}), f32[8,168,128]{2,1,0:T(8,128)S(1)}, u32[]{:S(2)}, u32[]{:S(2)}) %all-to-all-start.1) | async-done | bytes 688160 | tf_op jit(solution)/shard_map/all_to_all | solution.py:364
  75.6 1.0 shard_map.99
  76.6 24.2 %all_to_all.32 = f32[64,4,128]{2,1,0:T(4,128)S(1)} all-to-all(f32[64,4,128]{2,1,0:T(4,128)S(1)} %bitcast.17), channel_id=1, replica_groups=mesh['comp'=8,'pts'=64] {'pts'}, dimensions={0} | all-to-all | bytes 262144 | tf_op jit(solution)/shard_map/all_to_all | solution.py:370
  100.8 1.2 %shard_map.100 = f32[256,128]{1,0:T(8,128)} custom-call(s32[1,128]{1,0:T(1,128)S(1)} %broadcast_in_dim.10.block_ref, s32[64,1]{1,0:T(8,128)S(1)} %copy.18.column_ref, f32[256,128]{1,0:T(8,128)S(1)} %bitcast.19), custom_call_target="tpu_custom_call" | custom-call | flops 1000000 | bytes 1000000 | tf_op jit(solution)/shard_map/pallas_call | solution.py:372
  102.0 4.9 %all-to-all-start.3 = ((f32[64,4,128]{2,1,0:T(4,128)}), f32[64,4,128]{2,1,0:T(4,128)S(1)}, u32[]{:S(2)}, u32[]{:S(2)}) async-start(f32[64,4,128]{2,1,0:T(4,128)} %bitcast.9), calls=%async_computation.3 | async-start | bytes 262144 | tf_op jit(solution)/shard_map/all_to_all | solution.py:373
  106.9 0.1 copy.13
  107.1 1.0 copy.19
  108.1 9.1 %all-to-all-done.3 = f32[64,4,128]{2,1,0:T(4,128)S(1)} async-done(((f32[64,4,128]{2,1,0:T(4,128)}), f32[64,4,128]{2,1,0:T(4,128)S(1)}, u32[]{:S(2)}, u32[]{:S(2)}) %all-to-all-start.3) | async-done | bytes 131104 | tf_op jit(solution)/shard_map/all_to_all | solution.py:373
  117.2 1.0 shard_map.101
  (8 shorter events, 0.2 us)
Async XLA Ops:
  2.1 1.1 copy-start.1
  3.2 19.7 %copy-start.7 = (f32[1296]{0:T(1024)S(1)}, f32[1296]{0:T(1024)}, u32[]{:S(2)}) copy-start(f32[1296]{0:T(1024)} %param.10) | copy-start | bytes 15556
  3.2 19.7 %copy-start.3 = (bf16[640,1296]{0,1:T(8,128)(2,1)S(1)}, bf16[640,1296]{0,1:T(8,128)(2,1)}, u32[]{:S(2)}) copy-start(bf16[640,1296]{0,1:T(8,128)(2,1)} %param.11) | copy-start | bytes 4976644
  3.2 19.7 %copy-start.4 = (bf16[640,1296]{0,1:T(8,128)(2,1)S(1)}, bf16[640,1296]{0,1:T(8,128)(2,1)}, u32[]{:S(2)}) copy-start(bf16[640,1296]{0,1:T(8,128)(2,1)} %param.12) | copy-start | bytes 4976644
  3.3 10.3 %collective-permute-start = (f32[8,256]{1,0:T(8,128)S(1)}, f32[8,256]{1,0:T(8,128)S(1)}, u32[]{:S(2)}, u32[]{:S(2)}) collective-permute-start(f32[8,256]{1,0:T(8,128)S(1)} %get-tuple-element.7), channel_id=1, source_target_pairs={{0,1},{1,2},{2,3},{3,4},{4,5},{5,6},{6,7},{7,8},{8,9},{9,10},{10,1... | collective-permute-start | bytes 24584 | tf_op jit(solution)/shard_map/ppermute | solution.py:329
  9.0 5.5 %collective-permute-start.1 = (f32[8,256]{1,0:T(8,128)S(1)}, f32[8,256]{1,0:T(8,128)S(1)}, u32[]{:S(2)}, u32[]{:S(2)}) collective-permute-start(f32[8,256]{1,0:T(8,128)S(1)} %get-tuple-element.8), channel_id=1, source_target_pairs={{1,0},{2,1},{3,2},{4,3},{5,4},{6,5},{7,6},{8,7},{9,8},{10,9},{11,1... | collective-permute-start | bytes 24584 | tf_op jit(solution)/shard_map/ppermute | solution.py:330
  16.6 26.8 %all-to-all-start = ((f32[8,168,128]{2,1,0:T(8,128)}), f32[8,168,128]{2,1,0:T(8,128)}, u32[]{:S(2)}, u32[]{:S(2)}) async-start(f32[8,168,128]{2,1,0:T(8,128)} %shard_map.96), calls=%async_computation | async-start | bytes 1376256 | tf_op jit(solution)/shard_map/all_to_all | solution.py:334
  24.5 1.8 %copy-start = (bf16[1280,1344]{1,0:T(8,128)(2,1)}, bf16[1280,1344]{1,0:T(8,128)(2,1)S(1)}, u32[]{:S(2)}) copy-start(bf16[1280,1344]{1,0:T(8,128)(2,1)S(1)} %get-tuple-element.9.stacked_ref) | copy-start | bytes 10321924
  26.3 1.2 %copy-start.2 = (bf16[1344,640]{1,0:T(8,128)(2,1)}, bf16[1344,640]{1,0:T(8,128)(2,1)S(1)}, u32[]{:S(2)}) copy-start(bf16[1344,640]{1,0:T(8,128)(2,1)S(1)} %get-tuple-element.10.turned_ref) | copy-start | bytes 5160964
  27.5 0.9 copy-start.5
  43.3 10.8 %copy-start.8 = (s32[64]{0:T(128)S(1)}, s32[64]{0:T(128)}, u32[]{:S(2)}) copy-start(s32[64]{0:T(128)} %param.14) | copy-start | bytes 772
  43.3 10.9 %copy-start.6 = (s32[6144]{0:T(1024)S(1)}, s32[6144]{0:T(1024)}, u32[]{:S(2)}) copy-start(s32[6144]{0:T(1024)} %param.15) | copy-start | bytes 73732
  50.6 25.0 %all-to-all-start.1 = ((f32[8,168,128]{2,1,0:T(8,128)}), f32[8,168,128]{2,1,0:T(8,128)S(1)}, u32[]{:S(2)}, u32[]{:S(2)}) async-start(f32[8,168,128]{2,1,0:T(8,128)} %bitcast.20), calls=%async_computation.1 | async-start | bytes 1376256 | tf_op jit(solution)/shard_map/all_to_all | solution.py:364
  102.0 15.2 %all-to-all-start.3 = ((f32[64,4,128]{2,1,0:T(4,128)}), f32[64,4,128]{2,1,0:T(4,128)S(1)}, u32[]{:S(2)}, u32[]{:S(2)}) async-start(f32[64,4,128]{2,1,0:T(4,128)} %bitcast.9), calls=%async_computation.3 | async-start | bytes 262144 | tf_op jit(solution)/shard_map/all_to_all | solution.py:373

commit v5 on v4

--- a/solution.py
+++ b/solution.py
@@ -129,7 +129,11 @@
         copy.wait()
 
 
-def stack_body(a_ref, b_ref, growth_ref, both_ref, turned_ref, gain_ref, *, comps):
+def stack_body(a_ref, b_ref, growth_ref, *refs, comps):
+    tables = (len(refs) - 3) // 2
+    both_ref, turned_ref, gain_ref = refs[tables:tables + 3]
+    for source, target in zip(refs[:tables], refs[tables + 3:]):
+        target[...] = source[...]
     total, half = a_ref.shape
     rows = comps + 6
     groups = total // comps
@@ -156,7 +160,7 @@
     groups = padded // rows
     total = groups * comps
     half = both_ref.shape[0] // 2
-    loads = ((packed_ref, slab_ref), (gains_ref, gain_ref), (stacked_ref, both_ref), (turned_ref, turned_a_ref))
+    loads = ((packed_ref, slab_ref), (stacked_ref, both_ref), (turned_ref, turned_a_ref), (gains_ref, gain_ref))
     copies = [pltpu.make_async_copy(source, target, sems.at[i]) for i, (source, target) in enumerate(loads)]
     for copy in copies:
         copy.start()
@@ -324,7 +328,9 @@
     edge = jax.ShapeDtypeStruct((8, padded), F32)
     slab = jax.ShapeDtypeStruct((SLAB * n, LANES), F32)
 
-    side = jnp.concatenate([sea_mask.astype(F32), courant, jnp.zeros((points - comps,), F32)]).reshape(2, points)
+    zero = jnp.zeros((), F32)
+    side = lax.pad(sea_mask.astype(F32), zero, ((0, points, 0),)) + lax.pad(courant, zero, ((points, points - comps, 0),))
+    side = side.reshape(2, points)
     up, down = call(edges_body, (edge, edge), (VMEM, VMEM), (VMEM, VMEM))(spectrum, side)
     before = lax.ppermute(up, "pts", [(i, i + 1) for i in range(n - 1)])
     after = lax.ppermute(down, "pts", [(i + 1, i) for i in range(n - 1)])
@@ -333,16 +339,21 @@
     )(spectrum, side, before, after)
     slabs = lax.all_to_all(slabs, "comp", split_axis=0, concat_axis=0, tiled=True)
 
+    block = jnp.full((1, LANES), lax.axis_index("pts"), jnp.int32)
+    column = nest_counts.reshape(n, 1)
+    lines = jnp.repeat(jnp.pad(nest_offsets, (0, 4 * n)).reshape(-1, n), SLAB, axis=1)
     rows = groups * (comps + 6)
     half = quad_a.shape[0]
     wide = jax.ShapeDtypeStruct((rows, LANES), F32)
-    both, turned_a, gain = call(
+    tables = (block, column, lines)
+    both, turned_a, gain, block, column, lines = call(
         functools.partial(stack_body, comps=comps),
-        (jax.ShapeDtypeStruct((2 * half, rows), BF16), jax.ShapeDtypeStruct((rows, half), BF16), wide),
-        (VMEM, VMEM, VMEM),
-        (VMEM, VMEM, VMEM),
+        (jax.ShapeDtypeStruct((2 * half, rows), BF16), jax.ShapeDtypeStruct((rows, half), BF16), wide)
+        + tuple(jax.ShapeDtypeStruct(table.shape, table.dtype) for table in tables),
+        (VMEM,) * 6,
+        (VMEM,) * 6,
         vmem=40,
-    )(quad_a.T, quad_b.T, growth.reshape(1, total))
+    )(quad_a.T, quad_b.T, growth.reshape(1, total), *tables)
     result = call(
         functools.partial(steps_body, comps=comps),
         wide,
@@ -363,9 +374,6 @@
     result = result.reshape(packed.shape)
     result = lax.all_to_all(result, "comp", split_axis=0, concat_axis=0, tiled=True)
 
-    block = jnp.full((1, LANES), lax.axis_index("pts"), jnp.int32)
-    column = nest_counts.reshape(n, 1)
-    lines = jnp.repeat(jnp.pad(nest_offsets, (0, 4 * n)).reshape(-1, n), SLAB, axis=1)
     sent = call(gather_body, slab, (VMEM,) * 4)(block, column, result, lines)
     sent = lax.all_to_all(sent, "pts", split_axis=0, concat_axis=0, tiled=True)
     field = result[:, 0:comps].transpose(1, 0, 2).reshape(comps, points)

time: 119 us -> 119 us (level)
  blocking collectives: 24.2 us -> 49.1 us
  waiting for transfers between devices: 45.9 us -> 22.2 us
  starting transfers between devices: 25.1 us -> 21.5 us
  local copies, waits for them, and re-layouts: 7.33 us -> 8.78 us
    all_to_all x0 -> x1, blocking collectives: none -> 24.9 us  [per_device(): lax.all_to_all(result, 'comp', split_axis=0, concat_axis=0, tiled=True)]
    all_to_all x1 -> x0, waiting for transfers between devices: 21 us -> none  [per_device(): lax.all_to_all(result, 'comp', split_axis=0, concat_axis=0, tiled=True)]
    all_to_all x1 -> x0, starting transfers between devices: 3.56 us -> none  [per_device(): lax.all_to_all(result, 'comp', split_axis=0, concat_axis=0, tiled=True)]
    all_to_all x1, waiting for transfers between devices: 15 us -> 12.3 us  [per_device(): lax.all_to_all(slabs, 'comp', split_axis=0, concat_axis=0, tiled=True)]
    unnamed x20 -> x24, local copies, waits for them, and re-layouts: 5.99 us -> 6.63 us
  transfers between devices with their start and end apart: 5 -> 4, of which waited for: 4 -> 3; matrix products, arithmetic and copies ran while one was open for 1% -> 3% of each run, Pallas kernels for 1% -> 1%
where the time goes in v5:
time: 119 us; the launch traced here: 118 us
  blocking collectives  49.1 us (41%)
  waiting for transfers between devices  22.2 us (19%)
  starting transfers between devices  21.5 us (18%)
  Pallas kernels  14.2 us (12%)
  local copies, waits for them, and re-layouts  8.78 us (7%)
  other arithmetic  1.37 us (1%)
    all_to_all x1, blocking collectives, per_device(): lax.all_to_all(result, 'comp', split_axis=0, concat_axis=0, tiled=True)  24.9 us
    all_to_all x1, blocking collectives, per_device(): sent = lax.all_to_all(sent, 'pts', split_axis=0, concat_axis=0, tiled=True)  24.2 us
    all_to_all x1, waiting for transfers between devices, per_device(): lax.all_to_all(slabs, 'comp', split_axis=0, concat_axis=0, tiled=True)  12.3 us
    all_to_all x1, waiting for transfers between devices, per_device(): sent = lax.all_to_all(sent, 'pts', split_axis=0, concat_axis=0, tiled=True)  9.12 us
    pallas_call x1, Pallas kernels, per_device(): call(functools.partial(steps_body, comps=comps), wide, (HBM, HBM, HBM, HB...  7.19 us
    unnamed x24, local copies, waits for them, and re-layouts  6.63 us
    all_to_all x1, starting transfers between devices, per_device(): lax.all_to_all(slabs, 'comp', split_axis=0, concat_axis=0, tiled=True)  6.33 us
    ppermute x1, starting transfers between devices, per_device(): before = lax.ppermute(up, 'pts', [(i, i + 1) for i in range(n - 1)])  5.38 us
  transfers between devices with their start and end apart: 4, of which 3 were waited for; matrix products, arithmetic and copies ran while one was open for 3% of the time, Pallas kernels for 1%

profile of v5, /device:TPU:1, one launch (start us, length us, event | category | flops | bytes accessed | tf_op | source)
XLA Modules:
  0.0 118.1 jit_solution(7144124980930187228)
XLA Ops:
  0.6 0.7 convert_element_type.3
  1.3 0.7 pad_add_fusion
  2.0 0.0 copy-start.1
  2.0 1.1 copy-done.1
  3.1 0.0 copy-start.9
  3.1 0.0 copy-start.8
  3.1 0.0 copy-start.10
  3.1 0.1 shard_map.95
  3.2 5.4 %collective-permute-start = (f32[8,256]{1,0:T(8,128)S(1)}, f32[8,256]{1,0:T(8,128)S(1)}, u32[]{:S(2)}, u32[]{:S(2)}) collective-permute-start(f32[8,256]{1,0:T(8,128)S(1)} %get-tuple-element.10), channel_id=1, source_target_pairs={{0,1},{1,2},{2,3},{3,4},{4,5},{5,6},{6,7},{7,8},{8,9},{9,10},{10,1... | collective-permute-start | bytes 24584 | tf_op jit(solution)/shard_map/ppermute | solution.py:335
  8.6 0.0 copy-start.3
  8.6 0.0 copy-start.4
  8.7 4.9 %collective-permute-start.1 = (f32[8,256]{1,0:T(8,128)S(1)}, f32[8,256]{1,0:T(8,128)S(1)}, u32[]{:S(2)}, u32[]{:S(2)}) collective-permute-start(f32[8,256]{1,0:T(8,128)S(1)} %get-tuple-element.11), channel_id=1, source_target_pairs={{1,0},{2,1},{3,2},{4,3},{5,4},{6,5},{7,6},{8,7},{9,8},{10,9},{11,1... | collective-permute-start | bytes 24584 | tf_op jit(solution)/shard_map/ppermute | solution.py:336
  13.6 0.0 collective-permute-done.before_ref
  13.6 0.8 collective-permute-done.1.after_ref
  14.4 2.1 %shard_map.96 = f32[8,168,128]{2,1,0:T(8,128)} custom-call(f32[162,1024]{1,0:T(8,128)S(1)} %copy-done.1, f32[2,1024]{1,0:T(2,128)S(1)} %reshape.32.side_ref, f32[8,256]{1,0:T(8,128)S(1)} %collective-permute-done.before_ref, f32[8,256]{1,0:T(8,128)S(1)} %collective-permute-done.1.after_ref), custom_call_target="tpu_custom_call" | custom-call | flops 1000000 | bytes 1000000 | tf_op jit(solution)/shard_map/pallas_call | solution.py:337
  16.5 6.3 %all-to-all-start = ((f32[8,168,128]{2,1,0:T(8,128)}), f32[8,168,128]{2,1,0:T(8,128)}, u32[]{:S(2)}, u32[]{:S(2)}) async-start(f32[8,168,128]{2,1,0:T(8,128)} %shard_map.96), calls=%async_computation | async-start | bytes 1376256 | tf_op jit(solution)/shard_map/all_to_all | solution.py:340
  22.9 0.0 copy-done.9
  22.9 0.0 copy-done.8
  22.9 0.1 reshape.36
  23.0 0.1 copy.11
  23.1 0.0 copy-done.10
  23.1 0.1 copy.12.refs_1_
  23.2 0.7 broadcast_in_dim.7
  23.9 1.0 copy.13.refs_2_
  24.9 0.0 copy-done.3
  24.9 0.0 copy-done.4
  24.9 1.6 %shard_map.97 = (bf16[1280,1344]{1,0:T(8,128)(2,1)S(1)}, bf16[1344,640]{1,0:T(8,128)(2,1)S(1)}, f32[1344,128]{1,0:T(8,128)S(1)}, s32[1,128]{1,0:T(1,128)S(1)}, s...) custom-call(bf16[1296,640]{1,0:T(8,128)(2,1)S(1)} %bitcast.15, bf16[1296,640]{1,0:T(8,128)(2,1)S(1)} %bitcast.16, ...), custom_call_target="tpu_custom_call" | custom-call | flops 1000000 | bytes 1000000 | tf_op jit(solution)/shard_map/pallas_call | solution.py:349
  26.4 0.0 copy-start
  26.5 1.8 %copy-done = bf16[1280,1344]{1,0:T(8,128)(2,1)} copy-done((bf16[1280,1344]{1,0:T(8,128)(2,1)}, bf16[1280,1344]{1,0:T(8,128)(2,1)S(1)}, u32[]{:S(2)}) %copy-start) | copy-done | bytes 3440664
  28.2 0.0 copy-start.2
  28.2 1.2 %copy-done.2 = bf16[1344,640]{1,0:T(8,128)(2,1)} copy-done((bf16[1344,640]{1,0:T(8,128)(2,1)}, bf16[1344,640]{1,0:T(8,128)(2,1)S(1)}, u32[]{:S(2)}) %copy-start.2) | copy-done | bytes 1720344
  29.5 0.0 copy-start.5
  29.5 0.9 copy-done.5
  30.3 0.0 copy-start.6
  30.3 0.6 copy-done.6
  30.9 12.3 %all-to-all-done = f32[8,168,128]{2,1,0:T(8,128)} async-done(((f32[8,168,128]{2,1,0:T(8,128)}), f32[8,168,128]{2,1,0:T(8,128)}, u32[]{:S(2)}, u32[]{:S(2)}) %all-to-all-start) | async-done | bytes 688160 | tf_op jit(solution)/shard_map/all_to_all | solution.py:340
  43.3 0.0 copy-start.7
  43.3 7.2 %shard_map.98 = f32[1344,128]{1,0:T(8,128)} custom-call(f32[1344,128]{1,0:T(8,128)} %bitcast.packed_ref, bf16[1280,1344]{1,0:T(8,128)(2,1)} %copy-done, bf16[1344,640]{1,0:T(8,128)(2,1)} %copy-done.2, f32[1344,128]{1,0:T(8,128)} %copy-done.5), custom_call_target="tpu_custom_call" | custom-call | flops 1000000 | bytes 1000000 | tf_op jit(solution)/shard_map/pallas_call | solution.py:357
  50.5 24.9 %all_to_all.32.slab_ref = f32[8,168,128]{2,1,0:T(8,128)S(1)} all-to-all(f32[8,168,128]{2,1,0:T(8,128)} %bitcast.20), channel_id=1, replica_groups=mesh['comp'=8,'pts'=64] {'comp'}, dimensions={0} | all-to-all | bytes 1376256 | tf_op jit(solution)/shard_map/all_to_all | solution.py:375
  75.4 0.0 copy-done.7
  75.4 1.0 shard_map.99
  76.4 24.2 %all_to_all.33 = f32[64,4,128]{2,1,0:T(4,128)S(1)} all-to-all(f32[64,4,128]{2,1,0:T(4,128)S(1)} %bitcast.17), channel_id=1, replica_groups=mesh['comp'=8,'pts'=64] {'pts'}, dimensions={0} | all-to-all | bytes 262144 | tf_op jit(solution)/shard_map/all_to_all | solution.py:378
  100.6 1.2 %shard_map.100 = f32[256,128]{1,0:T(8,128)} custom-call(s32[1,128]{1,0:T(1,128)S(1)} %get-tuple-element.15.block_ref, s32[64,1]{1,0:T(8,128)S(1)} %get-tuple-element.16.column_ref, f32[256,128]{1,0:T(8,128)S(1)} %bitcast.19), custom_call_target="tpu_custom_call" | custom-call | flops 1000000 | bytes 1000000 | tf_op jit(solution)/shard_map/pallas_call | solution.py:380
  101.8 4.9 %all-to-all-start.3 = ((f32[64,4,128]{2,1,0:T(4,128)}), f32[64,4,128]{2,1,0:T(4,128)S(1)}, u32[]{:S(2)}, u32[]{:S(2)}) async-start(f32[64,4,128]{2,1,0:T(4,128)} %bitcast.9), calls=%async_computation.3 | async-start | bytes 262144 | tf_op jit(solution)/shard_map/all_to_all | solution.py:381
  106.8 0.1 copy.14
  107.0 1.0 copy.15
  107.9 9.1 %all-to-all-done.3 = f32[64,4,128]{2,1,0:T(4,128)S(1)} async-done(((f32[64,4,128]{2,1,0:T(4,128)}), f32[64,4,128]{2,1,0:T(4,128)S(1)}, u32[]{:S(2)}, u32[]{:S(2)}) %all-to-all-start.3) | async-done | bytes 131104 | tf_op jit(solution)/shard_map/all_to_all | solution.py:381
  117.1 1.0 shard_map.101
  (6 shorter events, 0.1 us)
Async XLA Ops:
  2.0 1.1 copy-start.1
  3.1 19.7 %copy-start.9 = (f32[1296]{0:T(1024)S(1)}, f32[1296]{0:T(1024)}, u32[]{:S(2)}) copy-start(f32[1296]{0:T(1024)} %param.10) | copy-start | bytes 15556
  3.1 19.8 %copy-start.8 = (s32[6144]{0:T(1024)S(1)}, s32[6144]{0:T(1024)}, u32[]{:S(2)}) copy-start(s32[6144]{0:T(1024)} %param.15) | copy-start | bytes 73732
  3.1 19.9 %copy-start.10 = (s32[64]{0:T(128)S(1)}, s32[64]{0:T(128)}, u32[]{:S(2)}) copy-start(s32[64]{0:T(128)} %param.14) | copy-start | bytes 772
  3.2 10.3 %collective-permute-start = (f32[8,256]{1,0:T(8,128)S(1)}, f32[8,256]{1,0:T(8,128)S(1)}, u32[]{:S(2)}, u32[]{:S(2)}) collective-permute-start(f32[8,256]{1,0:T(8,128)S(1)} %get-tuple-element.10), channel_id=1, source_target_pairs={{0,1},{1,2},{2,3},{3,4},{4,5},{5,6},{6,7},{7,8},{8,9},{9,10},{10,1... | collective-permute-start | bytes 24584 | tf_op jit(solution)/shard_map/ppermute | solution.py:335
  8.6 16.2 %copy-start.3 = (bf16[640,1296]{0,1:T(8,128)(2,1)S(1)}, bf16[640,1296]{0,1:T(8,128)(2,1)}, u32[]{:S(2)}) copy-start(bf16[640,1296]{0,1:T(8,128)(2,1)} %param.11) | copy-start | bytes 4976644
  8.6 16.2 %copy-start.4 = (bf16[640,1296]{0,1:T(8,128)(2,1)S(1)}, bf16[640,1296]{0,1:T(8,128)(2,1)}, u32[]{:S(2)}) copy-start(bf16[640,1296]{0,1:T(8,128)(2,1)} %param.12) | copy-start | bytes 4976644
  8.7 5.7 %collective-permute-start.1 = (f32[8,256]{1,0:T(8,128)S(1)}, f32[8,256]{1,0:T(8,128)S(1)}, u32[]{:S(2)}, u32[]{:S(2)}) collective-permute-start(f32[8,256]{1,0:T(8,128)S(1)} %get-tuple-element.11), channel_id=1, source_target_pairs={{1,0},{2,1},{3,2},{4,3},{5,4},{6,5},{7,6},{8,7},{9,8},{10,9},{11,1... | collective-permute-start | bytes 24584 | tf_op jit(solution)/shard_map/ppermute | solution.py:336
  16.5 26.8 %all-to-all-start = ((f32[8,168,128]{2,1,0:T(8,128)}), f32[8,168,128]{2,1,0:T(8,128)}, u32[]{:S(2)}, u32[]{:S(2)}) async-start(f32[8,168,128]{2,1,0:T(8,128)} %shard_map.96), calls=%async_computation | async-start | bytes 1376256 | tf_op jit(solution)/shard_map/all_to_all | solution.py:340
  26.4 1.8 %copy-start = (bf16[1280,1344]{1,0:T(8,128)(2,1)}, bf16[1280,1344]{1,0:T(8,128)(2,1)S(1)}, u32[]{:S(2)}) copy-start(bf16[1280,1344]{1,0:T(8,128)(2,1)S(1)} %get-tuple-element.12.stacked_ref) | copy-start | bytes 10321924
  28.2 1.2 %copy-start.2 = (bf16[1344,640]{1,0:T(8,128)(2,1)}, bf16[1344,640]{1,0:T(8,128)(2,1)S(1)}, u32[]{:S(2)}) copy-start(bf16[1344,640]{1,0:T(8,128)(2,1)S(1)} %get-tuple-element.13.turned_ref) | copy-start | bytes 5160964
  29.5 0.9 copy-start.5
  30.3 0.6 copy-start.6
  43.3 32.1 %copy-start.7 = (s32[100,256]{1,0:T(8,128)S(1)}, s32[100,256]{1,0:T(8,128)}, u32[]{:S(2)}) copy-start(s32[100,256]{1,0:T(8,128)} %copy-done.6) | copy-start | bytes 307204
  101.8 15.2 %all-to-all-start.3 = ((f32[64,4,128]{2,1,0:T(4,128)}), f32[64,4,128]{2,1,0:T(4,128)S(1)}, u32[]{:S(2)}, u32[]{:S(2)}) async-start(f32[64,4,128]{2,1,0:T(4,128)} %bitcast.9), calls=%async_computation.3 | async-start | bytes 262144 | tf_op jit(solution)/shard_map/all_to_all | solution.py:381

commit v6 on v4

--- a/solution.py
+++ b/solution.py
@@ -156,7 +156,7 @@
     groups = padded // rows
     total = groups * comps
     half = both_ref.shape[0] // 2
-    loads = ((packed_ref, slab_ref), (gains_ref, gain_ref), (stacked_ref, both_ref), (turned_ref, turned_a_ref))
+    loads = ((packed_ref, slab_ref), (stacked_ref, both_ref), (turned_ref, turned_a_ref), (gains_ref, gain_ref))
     copies = [pltpu.make_async_copy(source, target, sems.at[i]) for i, (source, target) in enumerate(loads)]
     for copy in copies:
         copy.start()
@@ -214,16 +214,20 @@
         copy.wait()
 
 
-def gather_body(block_ref, column_ref, slab_ref, offsets_ref, out_ref):
-    chunks = slab_ref.shape[0]
-    comps = slab_ref.shape[1] - 6
+def plan_body(block_ref, column_ref, offsets_ref, pick_ref, relay_ref, place_ref):
     n = column_ref.shape[0]
     rows = SLAB * n
     slots = NB_BLOCK // n
+    span = NB_BLOCK // 2
     block = block_ref[0:1, 0:1]
+    column = column_ref[...]
+
+    def ones(mask):
+        return mask.astype(F32).astype(BF16)
+
     device = iota((n, 1), 0)
-    start = jnp.sum(jnp.where(device < block, column_ref[...], 0), axis=0, keepdims=True)
-    count = jnp.sum(jnp.where(device == block, column_ref[...], 0), axis=0, keepdims=True)
+    start = jnp.sum(jnp.where(device < block, column, 0), axis=0, keepdims=True)
+    count = jnp.sum(jnp.where(device == block, column, 0), axis=0, keepdims=True)
     shift = lax.rem(start, jnp.int32(n))
     lane = iota((1, rows), 1)
     at = lane // SLAB
@@ -234,11 +238,35 @@
     table = offsets_ref[...]
     wanted = jnp.sum(jnp.where(iota(table.shape, 0) == line, table, 0), axis=0, keepdims=True)
     wanted = jnp.where(jnp.logical_and(slot < slots, base + n * slot < count), wanted, -1)
-    point = iota((LANES, rows), 0)
+    pick_ref[...] = ones(iota(pick_ref.shape, 0) == wanted)
+
+    wide = jnp.broadcast_to(column, (n, rows))
+    source = iota((n, rows), 0)
+    target = iota((n, rows), 1) // SLAB
+    starts = jnp.sum(jnp.where(source < target, wide, 0), axis=0, keepdims=True)
+    counts = jnp.sum(jnp.where(source == target, wide, 0), axis=0, keepdims=True)
+    position = lax.rem(block - starts + 128 * n, jnp.int32(n)) + n * slot
+    entry = jnp.where(jnp.logical_and(position < counts, slot < slots), starts + position, -(1 << 20))
+    row = iota((rows, 1), 0)
+    half = row % SLAB
+    place = row // SLAB
+    window = jnp.where(place < n // 2, span * place + counts[:, 0:1], span * (place - n // 2)) + n * half
+    size = jnp.where(half == 0, n, jnp.where(half == 1, span - n, 0))
+    inside = entry - window
+    relay_ref[...] = ones(jnp.logical_and(inside >= 0, inside < size))
+
+    own = jnp.where(block < n // 2, span * block + column[0:1, 0:1], span * (block - n // 2))
+    goal = lax.rem(place - own + 256 * n, jnp.int32(n)) + n * half
+    place_ref[...] = ones(jnp.logical_and(iota((rows, LANES), 1) == goal, half < 2))
+
+
+def gather_body(pick_ref, slab_ref, out_ref, *, slots):
+    chunks = slab_ref.shape[0]
+    comps = slab_ref.shape[1] - 6
+    rows = pick_ref.shape[1]
     picked = jnp.zeros((comps, rows), F32)
     for k in range(chunks):
-        chosen = (point + k * LANES == wanted).astype(F32).astype(BF16)
-        picked = picked + exact_dot(slab_ref[k, 0:comps, :], chosen, ((1,), (0,)))
+        picked = picked + exact_dot(slab_ref[k, 0:comps, :], pick_ref[k * LANES:(k + 1) * LANES, :], ((1,), (0,)))
     side = 2 * LANES
     turned = jnp.concatenate([picked, jnp.zeros((side - comps, rows), F32)], axis=0).T
     out_ref[...] = fold(turned, slots, comps - LANES)
@@ -271,45 +299,13 @@
     return jnp.concatenate([jnp.where(slot < slots, value, 0.0), side], axis=1)
 
 
-def relay_body(block_ref, column_ref, in_ref, out_ref, *, rest):
-    rows = in_ref.shape[0]
-    n = rows // SLAB
-    slots = NB_BLOCK // n
-    me = block_ref[0:1, 0:1]
-    wide = jnp.broadcast_to(column_ref[...], (n, rows))
-    source = iota((n, rows), 0)
-    target = iota((n, rows), 1) // SLAB
-    starts = jnp.sum(jnp.where(source < target, wide, 0), axis=0, keepdims=True)
-    counts = jnp.sum(jnp.where(source == target, wide, 0), axis=0, keepdims=True)
-    span = NB_BLOCK // 2
-    slot = iota((1, rows), 1) % SLAB
-    position = lax.rem(me - starts + 128 * n, jnp.int32(n)) + n * slot
-    valid = jnp.logical_and(position < counts, slot < slots)
-    entry = jnp.where(valid, starts + position, -(1 << 20))
-    place = iota((rows, 1), 0)
-    half = place % SLAB
-    place = place // SLAB
-    window = jnp.where(place < n // 2, span * place + counts[:, 0:1], span * (place - n // 2)) + n * half
-    size = jnp.where(half == 0, n, jnp.where(half == 1, span - n, 0))
-    inside = entry - window
-    chosen = jnp.logical_and(inside >= 0, inside < size).astype(F32).astype(BF16)
-    value = exact_pick(chosen, unfold(in_ref[...], slots, rest))
-    out_ref[...] = fold(value, 2, rest)
-
-
-def settle_body(block_ref, column_ref, in_ref, out_ref):
+def relay_body(chosen_ref, in_ref, out_ref, *, slots, rest):
+    out_ref[...] = fold(exact_pick(chosen_ref[...], unfold(in_ref[...], slots, rest)), 2, rest)
+
+
+def settle_body(chosen_ref, in_ref, out_ref):
     comps, span = out_ref.shape
-    rows = in_ref.shape[0]
-    n = rows // SLAB
-    block = block_ref[0:1, 0:1]
-    row = iota((rows, LANES), 0)
-    device = row // SLAB
-    half = row % SLAB
-    at = iota((rows, LANES), 1)
-    window = jnp.where(block < n // 2, span * block + column_ref[0:1, 0:1], span * (block - n // 2))
-    target = lax.rem(device - window + 256 * n, jnp.int32(n)) + n * half
-    chosen = jnp.logical_and(at == target, half < 2).astype(F32).astype(BF16)
-    value = exact_dot(unfold(in_ref[...], 2, comps - LANES).T, chosen, ((1,), (0,)))
+    value = exact_dot(unfold(in_ref[...], 2, comps - LANES).T, chosen_ref[...], ((1,), (0,)))
     out_ref[...] = value[0:comps, 0:span]
 
 
@@ -324,7 +320,9 @@
     edge = jax.ShapeDtypeStruct((8, padded), F32)
     slab = jax.ShapeDtypeStruct((SLAB * n, LANES), F32)
 
-    side = jnp.concatenate([sea_mask.astype(F32), courant, jnp.zeros((points - comps,), F32)]).reshape(2, points)
+    zero = jnp.zeros((), F32)
+    side = lax.pad(sea_mask, jnp.int32(0), ((0, points, 0),)).astype(F32) + lax.pad(courant, zero, ((points, points - comps, 0),))
+    side = side.reshape(2, points)
     up, down = call(edges_body, (edge, edge), (VMEM, VMEM), (VMEM, VMEM))(spectrum, side)
     before = lax.ppermute(up, "pts", [(i, i + 1) for i in range(n - 1)])
     after = lax.ppermute(down, "pts", [(i + 1, i) for i in range(n - 1)])
@@ -333,14 +331,23 @@
     )(spectrum, side, before, after)
     slabs = lax.all_to_all(slabs, "comp", split_axis=0, concat_axis=0, tiled=True)
 
+    block = jnp.full((1, LANES), lax.axis_index("pts"), jnp.int32)
+    column = nest_counts.reshape(n, 1)
+    lines = jnp.repeat(jnp.pad(nest_offsets, (0, 4 * n)).reshape(-1, n), SLAB, axis=1)
+    pick, relay, place = call(
+        plan_body,
+        tuple(jax.ShapeDtypeStruct(shape, BF16) for shape in ((points, SLAB * n), (SLAB * n, SLAB * n), (SLAB * n, LANES))),
+        (VMEM,) * 3,
+        (VMEM,) * 3,
+    )(block, column, lines)
     rows = groups * (comps + 6)
     half = quad_a.shape[0]
     wide = jax.ShapeDtypeStruct((rows, LANES), F32)
     both, turned_a, gain = call(
         functools.partial(stack_body, comps=comps),
         (jax.ShapeDtypeStruct((2 * half, rows), BF16), jax.ShapeDtypeStruct((rows, half), BF16), wide),
-        (VMEM, VMEM, VMEM),
-        (VMEM, VMEM, VMEM),
+        (VMEM,) * 3,
+        (VMEM,) * 3,
         vmem=40,
     )(quad_a.T, quad_b.T, growth.reshape(1, total))
     result = call(
@@ -363,15 +370,13 @@
     result = result.reshape(packed.shape)
     result = lax.all_to_all(result, "comp", split_axis=0, concat_axis=0, tiled=True)
 
-    block = jnp.full((1, LANES), lax.axis_index("pts"), jnp.int32)
-    column = nest_counts.reshape(n, 1)
-    lines = jnp.repeat(jnp.pad(nest_offsets, (0, 4 * n)).reshape(-1, n), SLAB, axis=1)
-    sent = call(gather_body, slab, (VMEM,) * 4)(block, column, result, lines)
+    slots = NB_BLOCK // n
+    sent = call(functools.partial(gather_body, slots=slots), slab, (VMEM,) * 2)(pick, result)
     sent = lax.all_to_all(sent, "pts", split_axis=0, concat_axis=0, tiled=True)
     field = result[:, 0:comps].transpose(1, 0, 2).reshape(comps, points)
-    sent = call(functools.partial(relay_body, rest=comps - LANES), slab, (VMEM,) * 3)(block, column, sent)
+    sent = call(functools.partial(relay_body, slots=slots, rest=comps - LANES), slab, (VMEM,) * 2)(relay, sent)
     sent = lax.all_to_all(sent, "pts", split_axis=0, concat_axis=0, tiled=True)
-    nest = call(settle_body, jax.ShapeDtypeStruct((comps, NB_BLOCK // 2), F32), (VMEM,) * 3)(block, column, sent)
+    nest = call(settle_body, jax.ShapeDtypeStruct((comps, NB_BLOCK // 2), F32), (VMEM,) * 2)(place, sent)
     return (field, nest)
 
 

time: 119 us -> 118 us (level)
    pallas_call x2 -> x3, Pallas kernels: 2.23 us -> 2.49 us  [the longest x1 1.11 us: per_device(): call(functools.partial(relay_body, slots=slots, rest=comps - LANES), slab...]
  transfers between devices with their start and end apart: 5 -> 5, of which waited for: 4 -> 4; matrix products, arithmetic and copies ran while one was open for 1% -> 1% of each run, Pallas kernels for 1% -> 2%
where the time goes in v6:
time: 118 us; the launch traced here: 117 us
  waiting for transfers between devices  45.3 us (38%)
  starting transfers between devices  25.1 us (21%)
  blocking collectives  24.2 us (21%)
  Pallas kernels  14.5 us (12%)
  local copies, waits for them, and re-layouts  6.6 us (6%)
    all_to_all x1, blocking collectives, per_device(): sent = lax.all_to_all(sent, 'pts', split_axis=0, concat_axis=0, tiled=True)  24.2 us
    all_to_all x1, waiting for transfers between devices, per_device(): lax.all_to_all(result, 'comp', split_axis=0, concat_axis=0, tiled=True)  20.5 us
    all_to_all x1, waiting for transfers between devices, per_device(): lax.all_to_all(slabs, 'comp', split_axis=0, concat_axis=0, tiled=True)  14.9 us
    all_to_all x1, waiting for transfers between devices, per_device(): sent = lax.all_to_all(sent, 'pts', split_axis=0, concat_axis=0, tiled=True)  9.12 us
    pallas_call x1, Pallas kernels, per_device(): call(functools.partial(steps_body, comps=comps), wide, (HBM, HBM, HBM, HB...  7.17 us
    all_to_all x1, starting transfers between devices, per_device(): lax.all_to_all(slabs, 'comp', split_axis=0, concat_axis=0, tiled=True)  6.33 us
    unnamed x20, local copies, waits for them, and re-layouts  6.01 us
    ppermute x1, starting transfers between devices, per_device(): before = lax.ppermute(up, 'pts', [(i, i + 1) for i in range(n - 1)])  5.65 us
  transfers between devices with their start and end apart: 5, of which 4 were waited for; matrix products, arithmetic and copies ran while one was open for 1% of the time, Pallas kernels for 2%

profile of v6, /device:TPU:1, one launch (start us, length us, event | category | flops | bytes accessed | tf_op | source)
XLA Modules:
  0.0 117.2 jit_solution(11313816984951828434)
XLA Ops:
  0.6 0.7 pad_add_fusion
  1.4 0.0 copy-start.1
  1.4 1.1 copy-done.1
  2.5 0.0 copy-start.7
  2.5 0.0 copy-start.3
  2.5 0.0 copy-start.4
  2.5 0.1 shard_map.95
  2.6 5.6 %collective-permute-start = (f32[8,256]{1,0:T(8,128)S(1)}, f32[8,256]{1,0:T(8,128)S(1)}, u32[]{:S(2)}, u32[]{:S(2)}) collective-permute-start(f32[8,256]{1,0:T(8,128)S(1)} %get-tuple-element.10), channel_id=1, source_target_pairs={{0,1},{1,2},{2,3},{3,4},{4,5},{5,6},{6,7},{7,8},{8,9},{9,10},{10,1... | collective-permute-start | bytes 24584 | tf_op jit(solution)/shard_map/ppermute | solution.py:327
  8.2 4.7 %collective-permute-start.1 = (f32[8,256]{1,0:T(8,128)S(1)}, f32[8,256]{1,0:T(8,128)S(1)}, u32[]{:S(2)}, u32[]{:S(2)}) collective-permute-start(f32[8,256]{1,0:T(8,128)S(1)} %get-tuple-element.11), channel_id=1, source_target_pairs={{1,0},{2,1},{3,2},{4,3},{5,4},{6,5},{7,6},{8,7},{9,8},{10,9},{11,1... | collective-permute-start | bytes 24584 | tf_op jit(solution)/shard_map/ppermute | solution.py:328
  12.9 0.0 collective-permute-done.before_ref
  12.9 0.8 collective-permute-done.1.after_ref
  13.7 2.1 %shard_map.96 = f32[8,168,128]{2,1,0:T(8,128)} custom-call(f32[162,1024]{1,0:T(8,128)S(1)} %copy-done.1, f32[2,1024]{1,0:T(2,128)S(1)} %reshape.32.side_ref, f32[8,256]{1,0:T(8,128)S(1)} %collective-permute-done.before_ref, f32[8,256]{1,0:T(8,128)S(1)} %collective-permute-done.1.after_ref), custom_call_target="tpu_custom_call" | custom-call | flops 1000000 | bytes 1000000 | tf_op jit(solution)/shard_map/pallas_call | solution.py:329
  15.8 6.3 %all-to-all-start = ((f32[8,168,128]{2,1,0:T(8,128)}), f32[8,168,128]{2,1,0:T(8,128)}, u32[]{:S(2)}, u32[]{:S(2)}) async-start(f32[8,168,128]{2,1,0:T(8,128)} %shard_map.96), calls=%async_computation | async-start | bytes 1376256 | tf_op jit(solution)/shard_map/all_to_all | solution.py:332
  22.2 0.0 copy-done.7
  22.2 0.0 copy-done.3
  22.2 0.0 copy-done.4
  22.2 1.6 %shard_map.97 = (bf16[1280,1344]{1,0:T(8,128)(2,1)S(1)}, bf16[1344,640]{1,0:T(8,128)(2,1)S(1)}, f32[1344,128]{1,0:T(8,128)S(1)}) custom-call(bf16[1296,640]{1,0:T(8,128)(2,1)S(1)} %bitcast.15, bf16[1296,640]{1,0:T(8,128)(2,1)S(1)} %bitcast.16, f32[1,1296]{1,0:T(1,128)S(1)} %reshape.34.growth_ref), custom_call_target="tpu_custom_call" | custom-call | flops 1000000 | bytes 1000000 | tf_op jit(solution)/shard_map/pallas_call | solution.py:346
  23.8 0.0 copy-start
  23.8 1.8 %copy-done = bf16[1280,1344]{1,0:T(8,128)(2,1)} copy-done((bf16[1280,1344]{1,0:T(8,128)(2,1)}, bf16[1280,1344]{1,0:T(8,128)(2,1)S(1)}, u32[]{:S(2)}) %copy-start) | copy-done | bytes 3440664
  25.6 0.0 copy-start.2
  25.6 1.2 %copy-done.2 = bf16[1344,640]{1,0:T(8,128)(2,1)} copy-done((bf16[1344,640]{1,0:T(8,128)(2,1)}, bf16[1344,640]{1,0:T(8,128)(2,1)S(1)}, u32[]{:S(2)}) %copy-start.2) | copy-done | bytes 1720344
  26.8 0.0 copy-start.5
  26.8 0.9 copy-done.5
  27.7 14.9 %all-to-all-done = f32[8,168,128]{2,1,0:T(8,128)} async-done(((f32[8,168,128]{2,1,0:T(8,128)}), f32[8,168,128]{2,1,0:T(8,128)}, u32[]{:S(2)}, u32[]{:S(2)}) %all-to-all-start) | async-done | bytes 688160 | tf_op jit(solution)/shard_map/all_to_all | solution.py:332
  42.6 0.0 copy-start.6
  42.6 7.2 %shard_map.98 = f32[1344,128]{1,0:T(8,128)} custom-call(f32[1344,128]{1,0:T(8,128)} %bitcast.packed_ref, bf16[1280,1344]{1,0:T(8,128)(2,1)} %copy-done, bf16[1344,640]{1,0:T(8,128)(2,1)} %copy-done.2, f32[1344,128]{1,0:T(8,128)} %copy-done.5), custom_call_target="tpu_custom_call" | custom-call | flops 1000000 | bytes 1000000 | tf_op jit(solution)/shard_map/pallas_call | solution.py:353
  49.8 0.0 copy-start.8
  49.8 3.6 %all-to-all-start.1 = ((f32[8,168,128]{2,1,0:T(8,128)}), f32[8,168,128]{2,1,0:T(8,128)S(1)}, u32[]{:S(2)}, u32[]{:S(2)}) async-start(f32[8,168,128]{2,1,0:T(8,128)} %bitcast.20), calls=%async_computation.1 | async-start | bytes 1376256 | tf_op jit(solution)/shard_map/all_to_all | solution.py:371
  53.4 0.0 copy-done.6
  53.4 0.1 reshape.38
  53.5 0.1 copy.12
  53.6 0.1 copy.14.offsets_ref
  53.7 0.0 copy-done.8
  53.7 0.1 copy.13.column_ref
  53.8 0.5 shard_map.99
  54.3 20.5 %all-to-all-done.1.slab_ref = f32[8,168,128]{2,1,0:T(8,128)S(1)} async-done(((f32[8,168,128]{2,1,0:T(8,128)}), f32[8,168,128]{2,1,0:T(8,128)S(1)}, u32[]{:S(2)}, u32[]{:S(2)}) %all-to-all-start.1) | async-done | bytes 688160 | tf_op jit(solution)/shard_map/all_to_all | solution.py:371
  74.8 0.9 shard_map.100
  75.7 24.2 %all_to_all.32 = f32[64,4,128]{2,1,0:T(4,128)S(1)} all-to-all(f32[64,4,128]{2,1,0:T(4,128)S(1)} %bitcast.19), channel_id=1, replica_groups=mesh['comp'=8,'pts'=64] {'pts'}, dimensions={0} | all-to-all | bytes 262144 | tf_op jit(solution)/shard_map/all_to_all | solution.py:375
  99.9 1.1 shard_map.101
  101.0 4.9 %all-to-all-start.3 = ((f32[64,4,128]{2,1,0:T(4,128)}), f32[64,4,128]{2,1,0:T(4,128)S(1)}, u32[]{:S(2)}, u32[]{:S(2)}) async-start(f32[64,4,128]{2,1,0:T(4,128)} %bitcast.9), calls=%async_computation.3 | async-start | bytes 262144 | tf_op jit(solution)/shard_map/all_to_all | solution.py:378
  105.9 0.1 copy.11
  106.1 1.0 copy.15
  107.1 9.1 %all-to-all-done.3 = f32[64,4,128]{2,1,0:T(4,128)S(1)} async-done(((f32[64,4,128]{2,1,0:T(4,128)}), f32[64,4,128]{2,1,0:T(4,128)S(1)}, u32[]{:S(2)}, u32[]{:S(2)}) %all-to-all-start.3) | async-done | bytes 131104 | tf_op jit(solution)/shard_map/all_to_all | solution.py:378
  116.2 1.0 shard_map.102
  (7 shorter events, 0.2 us)
Async XLA Ops:
  1.4 1.1 copy-start.1
  2.5 19.7 %copy-start.7 = (f32[1296]{0:T(1024)S(1)}, f32[1296]{0:T(1024)}, u32[]{:S(2)}) copy-start(f32[1296]{0:T(1024)} %param.10) | copy-start | bytes 15556
  2.5 19.7 %copy-start.3 = (bf16[640,1296]{0,1:T(8,128)(2,1)S(1)}, bf16[640,1296]{0,1:T(8,128)(2,1)}, u32[]{:S(2)}) copy-start(bf16[640,1296]{0,1:T(8,128)(2,1)} %param.11) | copy-start | bytes 4976644
  2.5 19.8 %copy-start.4 = (bf16[640,1296]{0,1:T(8,128)(2,1)S(1)}, bf16[640,1296]{0,1:T(8,128)(2,1)}, u32[]{:S(2)}) copy-start(bf16[640,1296]{0,1:T(8,128)(2,1)} %param.12) | copy-start | bytes 4976644
  2.6 10.3 %collective-permute-start = (f32[8,256]{1,0:T(8,128)S(1)}, f32[8,256]{1,0:T(8,128)S(1)}, u32[]{:S(2)}, u32[]{:S(2)}) collective-permute-start(f32[8,256]{1,0:T(8,128)S(1)} %get-tuple-element.10), channel_id=1, source_target_pairs={{0,1},{1,2},{2,3},{3,4},{4,5},{5,6},{6,7},{7,8},{8,9},{9,10},{10,1... | collective-permute-start | bytes 24584 | tf_op jit(solution)/shard_map/ppermute | solution.py:327
  8.2 5.5 %collective-permute-start.1 = (f32[8,256]{1,0:T(8,128)S(1)}, f32[8,256]{1,0:T(8,128)S(1)}, u32[]{:S(2)}, u32[]{:S(2)}) collective-permute-start(f32[8,256]{1,0:T(8,128)S(1)} %get-tuple-element.11), channel_id=1, source_target_pairs={{1,0},{2,1},{3,2},{4,3},{5,4},{6,5},{7,6},{8,7},{9,8},{10,9},{11,1... | collective-permute-start | bytes 24584 | tf_op jit(solution)/shard_map/ppermute | solution.py:328
  15.8 26.8 %all-to-all-start = ((f32[8,168,128]{2,1,0:T(8,128)}), f32[8,168,128]{2,1,0:T(8,128)}, u32[]{:S(2)}, u32[]{:S(2)}) async-start(f32[8,168,128]{2,1,0:T(8,128)} %shard_map.96), calls=%async_computation | async-start | bytes 1376256 | tf_op jit(solution)/shard_map/all_to_all | solution.py:332
  23.8 1.8 %copy-start = (bf16[1280,1344]{1,0:T(8,128)(2,1)}, bf16[1280,1344]{1,0:T(8,128)(2,1)S(1)}, u32[]{:S(2)}) copy-start(bf16[1280,1344]{1,0:T(8,128)(2,1)S(1)} %get-tuple-element.12.stacked_ref) | copy-start | bytes 10321924
  25.6 1.2 %copy-start.2 = (bf16[1344,640]{1,0:T(8,128)(2,1)}, bf16[1344,640]{1,0:T(8,128)(2,1)S(1)}, u32[]{:S(2)}) copy-start(bf16[1344,640]{1,0:T(8,128)(2,1)S(1)} %get-tuple-element.13.turned_ref) | copy-start | bytes 5160964
  26.8 0.9 copy-start.5
  42.6 10.8 %copy-start.6 = (s32[6144]{0:T(1024)S(1)}, s32[6144]{0:T(1024)}, u32[]{:S(2)}) copy-start(s32[6144]{0:T(1024)} %param.15) | copy-start | bytes 73732
  49.8 3.9 %copy-start.8 = (s32[64]{0:T(128)S(1)}, s32[64]{0:T(128)}, u32[]{:S(2)}) copy-start(s32[64]{0:T(128)} %param.14) | copy-start | bytes 772
  49.8 25.0 %all-to-all-start.1 = ((f32[8,168,128]{2,1,0:T(8,128)}), f32[8,168,128]{2,1,0:T(8,128)S(1)}, u32[]{:S(2)}, u32[]{:S(2)}) async-start(f32[8,168,128]{2,1,0:T(8,128)} %bitcast.20), calls=%async_computation.1 | async-start | bytes 1376256 | tf_op jit(solution)/shard_map/all_to_all | solution.py:371
  101.0 15.2 %all-to-all-start.3 = ((f32[64,4,128]{2,1,0:T(4,128)}), f32[64,4,128]{2,1,0:T(4,128)S(1)}, u32[]{:S(2)}, u32[]{:S(2)}) async-start(f32[64,4,128]{2,1,0:T(4,128)} %bitcast.9), calls=%async_computation.3 | async-start | bytes 262144 | tf_op jit(solution)/shard_map/all_to_all | solution.py:378

commit v7 on v6

--- a/solution.py
+++ b/solution.py
@@ -54,36 +54,44 @@
     return (high + middle) + low
 
 
-def edges_body(field_ref, side_ref, up_ref, down_ref):
+def edges_body(block_ref, field_ref, side_ref, pair_ref, next_ref):
     comps, points = field_ref.shape
-    padded = up_ref.shape[1]
-    for ref, start, order in ((up_ref, points - LANES, (LANES - 1, LANES - 2)), (down_ref, 0, (0, 1))):
+    padded = pair_ref.shape[1]
+    payloads = []
+    for start, order in ((points - LANES, (LANES - 1, LANES - 2)), (0, (0, 1))):
         tile = jnp.concatenate([field_ref[:, start:start + LANES], jnp.zeros((padded - comps, LANES), F32)], axis=0)
         turned = tile.T
-        for row, lane in enumerate(order):
-            ref[row:row + 1, :] = turned[lane:lane + 1, :]
         point = start + order[0]
-        ref[2:3, :] = jnp.broadcast_to(side_ref[0:1, point:point + 1], (1, padded))
-        ref[3:8, :] = jnp.zeros((5, padded), F32)
+        sea = jnp.broadcast_to(side_ref[0:1, point:point + 1], (1, padded))
+        payloads.append(jnp.concatenate([turned[lane:lane + 1, :] for lane in order] + [sea, jnp.zeros((5, padded), F32)], axis=0))
+    up, down = payloads
+    even = lax.rem(block_ref[0:1, 0:1], jnp.int32(2)) == 0
+    pair_ref[...] = jnp.where(even, up, down)
+    next_ref[...] = jnp.where(even, down, up)
 
 
 STEP = 40
 
 
-def pack_body(field_ref, side_ref, before_ref, after_ref, out_ref, slab_ref, sems):
+def rows_of(chosen, value):
+    high, middle, low = (lax.dot_general(chosen, term, (((1,), (1,)), ((), ())), preferred_element_type=F32) for term in split3(value))
+    return (high + middle) + low
+
+
+def pack_body(block_ref, field_ref, side_ref, pair_ref, next_ref, out_ref, slab_ref, sems):
     comps, points = field_ref.shape
     chunks = points // LANES
-    padded = before_ref.shape[1]
-    whole = comps // 8 * 8
-    rows = jnp.concatenate([before_ref[0:3, :], after_ref[0:3, :], side_ref[1:2, 0:padded], jnp.zeros((1, padded), F32)], axis=0)
-    columns = rows.T[:comps, :]
+    padded = pair_ref.shape[1]
+    even = lax.rem(block_ref[0:1, 0:1], jnp.int32(2)) == 0
+    before = jnp.where(even, next_ref[...], pair_ref[...])
+    after = jnp.where(even, pair_ref[...], next_ref[...])
+    courant_row = side_ref[1:2, 0:padded]
+    columns = jnp.concatenate([before[0:1], after[0:1], courant_row, jnp.zeros((5, padded), F32)], axis=0).T[:comps, :]
 
     def wide(at):
         return jnp.broadcast_to(columns[:, at:at + 1], (comps, LANES))
 
-    near_before, far_before, sea_before = wide(0), wide(1), wide(2)
-    near_after, far_after, sea_after = wide(3), wide(4), wide(5)
-    courant = wide(6)
+    near_before, near_after, courant = wide(0), wide(1), wide(2)
     speed = jnp.abs(courant)
     stay = 1.0 - speed
     forward = courant > 0
@@ -102,23 +110,32 @@
         slab_ref[k, 0:comps, :] = value
         moved.append(value)
 
-    first = jnp.broadcast_to(tiles[0][:, 0:1], (comps, LANES))
-    last = jnp.broadcast_to(tiles[chunks - 1][:, LANES - 1:LANES], (comps, LANES))
-    moved_before = (stay * near_before + speed * jnp.where(forward, far_before, first)) * sea_before
-    moved_after = (stay * near_after + speed * jnp.where(forward, last, far_after)) * sea_after
-    ghosts = courant
-    for k in range(chunks):
-        low = moved_before if k == 0 else pltpu.roll(moved[k - 1], k + 1, 1)
-        high = moved_after if k == chunks - 1 else pltpu.roll(moved[k + 1], chunks + k, 1)
-        ghosts = jnp.where(lane == k, low, jnp.where(lane == chunks + k, high, ghosts))
-    turned = jnp.concatenate([ghosts, jnp.zeros((padded - comps, LANES), F32)], axis=0).T
-    head = turned[0:3 * chunks, 0:LANES]
-    tail = turned[0:3 * chunks, LANES:2 * LANES]
-    mixed = tail[chunks:2 * chunks] + pltpu.roll(tail[0:chunks], STEP, 1) + pltpu.roll(tail[2 * chunks:3 * chunks], 2 * STEP, 1)
+    count = 2 * chunks
+    row = iota((count, LANES), 0)
+    at = iota((count, LANES), 1)
+
+    def picked(value, last_to, first_to):
+        mask = jnp.logical_or(jnp.logical_and(at == LANES - 1, row == last_to), jnp.logical_and(at == 0, row == first_to))
+        return rows_of(mask.astype(F32).astype(BF16), value)
+
+    ghosts = sum(picked(moved[k], k + 1 if k < chunks - 1 else -1, chunks + k - 1 if k > 0 else -1) for k in range(chunks))
+    outer = picked(tiles[0], -1, 0) + picked(tiles[chunks - 1], 1, -1)
+    gap = jnp.zeros((count, padded - comps), F32)
+    ghosts, outer = (jnp.concatenate([value, gap], axis=1) for value in (ghosts, outer))
+    speed_row = jnp.abs(courant_row)
+    stay_row = 1.0 - speed_row
+    forward_row = courant_row > 0
+    moved_before = (stay_row * before[0:1] + speed_row * jnp.where(forward_row, before[1:2], outer[0:1])) * before[2:3]
+    moved_after = (stay_row * after[0:1] + speed_row * jnp.where(forward_row, outer[1:2], after[1:2])) * after[2:3]
+    row = iota((count, padded), 0)
+    ghosts = jnp.where(row == 0, moved_before, jnp.where(row == count - 1, moved_after, ghosts))
+    head = ghosts[:, 0:LANES]
+    tail = ghosts[:, LANES:2 * LANES]
+    mixed = tail[chunks:count] + pltpu.roll(tail[0:chunks], STEP, 1) + pltpu.roll(courant_row[:, LANES:2 * LANES], 2 * STEP, 1)
     for k in range(chunks):
         slab_ref[k, comps:comps + 1, :] = head[chunks + k:chunks + k + 1]
         slab_ref[k, comps + 1:comps + 2, :] = head[k:k + 1]
-        slab_ref[k, comps + 2:comps + 3, :] = head[2 * chunks:2 * chunks + 1]
+        slab_ref[k, comps + 2:comps + 3, :] = courant_row[:, 0:LANES]
         slab_ref[k, comps + 3:comps + 4, :] = mixed[k:k + 1]
         slab_ref[k, comps + 4:comps + 5, :] = side_ref[0:1, k * LANES:(k + 1) * LANES]
         slab_ref[k, comps + 5:comps + 6, :] = jnp.zeros((1, LANES), F32)
@@ -323,15 +340,16 @@
     zero = jnp.zeros((), F32)
     side = lax.pad(sea_mask, jnp.int32(0), ((0, points, 0),)).astype(F32) + lax.pad(courant, zero, ((points, points - comps, 0),))
     side = side.reshape(2, points)
-    up, down = call(edges_body, (edge, edge), (VMEM, VMEM), (VMEM, VMEM))(spectrum, side)
-    before = lax.ppermute(up, "pts", [(i, i + 1) for i in range(n - 1)])
-    after = lax.ppermute(down, "pts", [(i + 1, i) for i in range(n - 1)])
+    block = jnp.full((1, LANES), lax.axis_index("pts"), jnp.int32)
+    swap, hop = call(edges_body, (edge, edge), (VMEM,) * 3, (VMEM, VMEM))(block, spectrum, side)
+    both_ways = [(i, i + 1) for i in range(n - 1)]
+    swap = lax.ppermute(swap, "pts", [pair for i, j in both_ways[0::2] for pair in ((i, j), (j, i))])
+    hop = lax.ppermute(hop, "pts", [pair for i, j in both_ways[1::2] for pair in ((i, j), (j, i))])
     slabs = call(
-        pack_body, packed, (VMEM,) * 4, HBM, scratch=(pltpu.VMEM(packed.shape, F32), pltpu.SemaphoreType.DMA((chunks,)))
-    )(spectrum, side, before, after)
+        pack_body, packed, (VMEM,) * 5, HBM, scratch=(pltpu.VMEM(packed.shape, F32), pltpu.SemaphoreType.DMA((chunks,)))
+    )(block, spectrum, side, swap, hop)
     slabs = lax.all_to_all(slabs, "comp", split_axis=0, concat_axis=0, tiled=True)
 
-    block = jnp.full((1, LANES), lax.axis_index("pts"), jnp.int32)
     column = nest_counts.reshape(n, 1)
     lines = jnp.repeat(jnp.pad(nest_offsets, (0, 4 * n)).reshape(-1, n), SLAB, axis=1)
     pick, relay, place = call(

time: 118 us -> 117 us (level)
  blocking collectives: 24.2 us -> 27.5 us
  waiting for transfers between devices: 45.3 us -> 43.1 us
  starting transfers between devices: 25.1 us -> 23.6 us
    all_to_all x1, blocking collectives: 24.2 us -> 27.5 us  [per_device(): sent = lax.all_to_all(sent, 'pts', split_axis=0, concat_axis=0, tiled=True)]
    all_to_all x1, waiting for transfers between devices: 14.9 us -> 12.5 us  [per_device(): lax.all_to_all(slabs, 'comp', split_axis=0, concat_axis=0, tiled=True)]
    ppermute x2, waiting for transfers between devices: 0.8 us -> 3.03 us  [the longest x1 3.03 us: per_device(): lax.ppermute(hop, 'pts', [pair for i, j in both_ways[1::2] for pair in ((...]
    all_to_all x1, starting transfers between devices: 6.33 us -> 4.22 us  [per_device(): lax.all_to_all(slabs, 'comp', split_axis=0, concat_axis=0, tiled=True)]
    all_to_all x1, waiting for transfers between devices: 20.5 us -> 18.5 us  [per_device(): lax.all_to_all(result, 'comp', split_axis=0, concat_axis=0, tiled=True)]
where the time goes in v7:
time: 117 us
  waiting for transfers between devices  43.1 us (37%)
  blocking collectives  27.5 us (24%)
  starting transfers between devices  23.6 us (20%)
  Pallas kernels  14.5 us (12%)
  local copies, waits for them, and re-layouts  6.6 us (6%)
    all_to_all x1, blocking collectives, per_device(): sent = lax.all_to_all(sent, 'pts', split_axis=0, concat_axis=0, tiled=True)  27.5 us
    all_to_all x1, waiting for transfers between devices, per_device(): lax.all_to_all(result, 'comp', split_axis=0, concat_axis=0, tiled=True)  18.5 us
    all_to_all x1, waiting for transfers between devices, per_device(): lax.all_to_all(slabs, 'comp', split_axis=0, concat_axis=0, tiled=True)  12.5 us
    all_to_all x1, waiting for transfers between devices, per_device(): sent = lax.all_to_all(sent, 'pts', split_axis=0, concat_axis=0, tiled=True)  9.12 us
    ppermute x1, starting transfers between devices, per_device(): lax.ppermute(swap, 'pts', [pair for i, j in both_ways[0::2] for pair in (...  9.01 us
    pallas_call x1, Pallas kernels, per_device(): call(functools.partial(steps_body, comps=comps), wide, (HBM, HBM, HBM, HB...  7.18 us
    unnamed x20, local copies, waits for them, and re-layouts  6.01 us
    all_to_all x1, starting transfers between devices, per_device(): sent = lax.all_to_all(sent, 'pts', split_axis=0, concat_axis=0, tiled=True)  4.88 us
  transfers between devices with their start and end apart: 5, of which 4 were waited for; matrix products, arithmetic and copies ran while one was open for 1% of the time, Pallas kernels for 2%

profile of v7, /device:TPU:1, one launch (start us, length us, event | category | flops | bytes accessed | tf_op | source)
XLA Modules:
  0.0 117.0 jit_solution(15188831377152915747)
XLA Ops:
  0.6 0.7 pad_add_fusion
  1.4 0.0 copy-start.1
  1.4 1.1 copy-done.1
  2.5 0.0 copy-start.7
  2.5 0.0 copy-start.3
  2.5 0.0 copy-start.4
  2.5 0.1 shard_map.95
  2.6 9.0 %collective-permute-start = (f32[8,256]{1,0:T(8,128)S(1)}, f32[8,256]{1,0:T(8,128)S(1)}, u32[]{:S(2)}, u32[]{:S(2)}) collective-permute-start(f32[8,256]{1,0:T(8,128)S(1)} %get-tuple-element.10), channel_id=1, source_target_pairs={{0,1},{1,0},{2,3},{3,2},{4,5},{5,4},{6,7},{7,6},{8,9},{9,8},{10,11... | collective-permute-start | bytes 24584 | tf_op jit(solution)/shard_map/ppermute | solution.py:346
  11.6 1.9 %collective-permute-start.1 = (f32[8,256]{1,0:T(8,128)S(1)}, f32[8,256]{1,0:T(8,128)S(1)}, u32[]{:S(2)}, u32[]{:S(2)}) collective-permute-start(f32[8,256]{1,0:T(8,128)S(1)} %get-tuple-element.11), channel_id=1, source_target_pairs={{1,2},{2,1},{3,4},{4,3},{5,6},{6,5},{7,8},{8,7},{9,10},{10,9},{11,... | collective-permute-start | bytes 24584 | tf_op jit(solution)/shard_map/ppermute | solution.py:347
  13.5 0.0 collective-permute-done.pair_ref
  13.6 3.0 %collective-permute-done.1.next_ref = f32[8,256]{1,0:T(8,128)S(1)} collective-permute-done((f32[8,256]{1,0:T(8,128)S(1)}, f32[8,256]{1,0:T(8,128)S(1)}, u32[]{:S(2)}, u32[]{:S(2)}) %collective-permute-start.1) | collective-permute-done | bytes 8224 | tf_op jit(solution)/shard_map/ppermute | solution.py:347
  16.6 2.2 %shard_map.96 = f32[8,168,128]{2,1,0:T(8,128)} custom-call(s32[1,128]{1,0:T(1,128)S(1)} %broadcast_in_dim.6.block_ref, f32[162,1024]{1,0:T(8,128)S(1)} %copy-done.1, f32[2,1024]{1,0:T(2,128)S(1)} %reshape.32.side_ref, f32[8,256]{1,0:T(8,128)S(1)} %collective-permute-done.pair_ref, f32[8,256]{1,0:T(8,128)S(1)} %collective-permute-done.1.next_ref), custom_call_target="tpu_custom_call" | custom-call | flops 1000000 | bytes 1000000 | tf_op jit(solution)/shard_map/pallas_call | solution.py:348
  18.8 4.2 %all-to-all-start = ((f32[8,168,128]{2,1,0:T(8,128)}), f32[8,168,128]{2,1,0:T(8,128)}, u32[]{:S(2)}, u32[]{:S(2)}) async-start(f32[8,168,128]{2,1,0:T(8,128)} %shard_map.96), calls=%async_computation | async-start | bytes 1376256 | tf_op jit(solution)/shard_map/all_to_all | solution.py:351
  23.0 0.0 copy-done.7
  23.0 0.0 copy-done.3
  23.0 0.0 copy-done.4
  23.0 1.6 %shard_map.97 = (bf16[1280,1344]{1,0:T(8,128)(2,1)S(1)}, bf16[1344,640]{1,0:T(8,128)(2,1)S(1)}, f32[1344,128]{1,0:T(8,128)S(1)}) custom-call(bf16[1296,640]{1,0:T(8,128)(2,1)S(1)} %bitcast.15, bf16[1296,640]{1,0:T(8,128)(2,1)S(1)} %bitcast.16, f32[1,1296]{1,0:T(1,128)S(1)} %reshape.34.growth_ref), custom_call_target="tpu_custom_call" | custom-call | flops 1000000 | bytes 1000000 | tf_op jit(solution)/shard_map/pallas_call | solution.py:364
  24.6 0.0 copy-start
  24.6 1.8 %copy-done = bf16[1280,1344]{1,0:T(8,128)(2,1)} copy-done((bf16[1280,1344]{1,0:T(8,128)(2,1)}, bf16[1280,1344]{1,0:T(8,128)(2,1)S(1)}, u32[]{:S(2)}) %copy-start) | copy-done | bytes 3440664
  26.4 0.0 copy-start.2
  26.4 1.2 %copy-done.2 = bf16[1344,640]{1,0:T(8,128)(2,1)} copy-done((bf16[1344,640]{1,0:T(8,128)(2,1)}, bf16[1344,640]{1,0:T(8,128)(2,1)S(1)}, u32[]{:S(2)}) %copy-start.2) | copy-done | bytes 1720344
  27.6 0.0 copy-start.5
  27.6 0.9 copy-done.5
  28.5 12.5 %all-to-all-done = f32[8,168,128]{2,1,0:T(8,128)} async-done(((f32[8,168,128]{2,1,0:T(8,128)}), f32[8,168,128]{2,1,0:T(8,128)}, u32[]{:S(2)}, u32[]{:S(2)}) %all-to-all-start) | async-done | bytes 688160 | tf_op jit(solution)/shard_map/all_to_all | solution.py:351
  41.0 0.0 copy-start.6
  41.0 7.2 %shard_map.98 = f32[1344,128]{1,0:T(8,128)} custom-call(f32[1344,128]{1,0:T(8,128)} %bitcast.packed_ref, bf16[1280,1344]{1,0:T(8,128)(2,1)} %copy-done, bf16[1344,640]{1,0:T(8,128)(2,1)} %copy-done.2, f32[1344,128]{1,0:T(8,128)} %copy-done.5), custom_call_target="tpu_custom_call" | custom-call | flops 1000000 | bytes 1000000 | tf_op jit(solution)/shard_map/pallas_call | solution.py:371
  48.1 0.0 copy-start.8
  48.2 3.6 %all-to-all-start.1 = ((f32[8,168,128]{2,1,0:T(8,128)}), f32[8,168,128]{2,1,0:T(8,128)S(1)}, u32[]{:S(2)}, u32[]{:S(2)}) async-start(f32[8,168,128]{2,1,0:T(8,128)} %bitcast.20), calls=%async_computation.1 | async-start | bytes 1376256 | tf_op jit(solution)/shard_map/all_to_all | solution.py:389
  51.7 0.0 copy-done.6
  51.7 0.1 reshape.38
  51.8 0.1 copy.12
  51.9 0.1 copy.14.offsets_ref
  52.0 0.0 copy-done.8
  52.0 0.1 copy.13.column_ref
  52.1 0.5 shard_map.99
  52.6 18.5 %all-to-all-done.1.slab_ref = f32[8,168,128]{2,1,0:T(8,128)S(1)} async-done(((f32[8,168,128]{2,1,0:T(8,128)}), f32[8,168,128]{2,1,0:T(8,128)S(1)}, u32[]{:S(2)}, u32[]{:S(2)}) %all-to-all-start.1) | async-done | bytes 688160 | tf_op jit(solution)/shard_map/all_to_all | solution.py:389
  71.1 0.9 shard_map.100
  72.1 27.5 %all_to_all.32 = f32[64,4,128]{2,1,0:T(4,128)S(1)} all-to-all(f32[64,4,128]{2,1,0:T(4,128)S(1)} %bitcast.19), channel_id=1, replica_groups=mesh['comp'=8,'pts'=64] {'pts'}, dimensions={0} | all-to-all | bytes 262144 | tf_op jit(solution)/shard_map/all_to_all | solution.py:393
  99.6 1.1 shard_map.101
  100.7 4.9 %all-to-all-start.3 = ((f32[64,4,128]{2,1,0:T(4,128)}), f32[64,4,128]{2,1,0:T(4,128)S(1)}, u32[]{:S(2)}, u32[]{:S(2)}) async-start(f32[64,4,128]{2,1,0:T(4,128)} %bitcast.9), calls=%async_computation.3 | async-start | bytes 262144 | tf_op jit(solution)/shard_map/all_to_all | solution.py:396
  105.7 0.1 copy.11
  105.8 1.0 copy.15
  106.8 9.1 %all-to-all-done.3 = f32[64,4,128]{2,1,0:T(4,128)S(1)} async-done(((f32[64,4,128]{2,1,0:T(4,128)}), f32[64,4,128]{2,1,0:T(4,128)S(1)}, u32[]{:S(2)}, u32[]{:S(2)}) %all-to-all-start.3) | async-done | bytes 131104 | tf_op jit(solution)/shard_map/all_to_all | solution.py:396
  115.9 1.0 shard_map.102
  (7 shorter events, 0.2 us)
Async XLA Ops:
  1.4 1.1 copy-start.1
  2.5 20.5 %copy-start.7 = (f32[1296]{0:T(1024)S(1)}, f32[1296]{0:T(1024)}, u32[]{:S(2)}) copy-start(f32[1296]{0:T(1024)} %param.10) | copy-start | bytes 15556
  2.5 20.6 %copy-start.3 = (bf16[640,1296]{0,1:T(8,128)(2,1)S(1)}, bf16[640,1296]{0,1:T(8,128)(2,1)}, u32[]{:S(2)}) copy-start(bf16[640,1296]{0,1:T(8,128)(2,1)} %param.11) | copy-start | bytes 4976644
  2.5 20.6 %copy-start.4 = (bf16[640,1296]{0,1:T(8,128)(2,1)S(1)}, bf16[640,1296]{0,1:T(8,128)(2,1)}, u32[]{:S(2)}) copy-start(bf16[640,1296]{0,1:T(8,128)(2,1)} %param.12) | copy-start | bytes 4976644
  2.6 11.0 %collective-permute-start = (f32[8,256]{1,0:T(8,128)S(1)}, f32[8,256]{1,0:T(8,128)S(1)}, u32[]{:S(2)}, u32[]{:S(2)}) collective-permute-start(f32[8,256]{1,0:T(8,128)S(1)} %get-tuple-element.10), channel_id=1, source_target_pairs={{0,1},{1,0},{2,3},{3,2},{4,5},{5,4},{6,7},{7,6},{8,9},{9,8},{10,11... | collective-permute-start | bytes 24584 | tf_op jit(solution)/shard_map/ppermute | solution.py:346
  11.6 5.0 %collective-permute-start.1 = (f32[8,256]{1,0:T(8,128)S(1)}, f32[8,256]{1,0:T(8,128)S(1)}, u32[]{:S(2)}, u32[]{:S(2)}) collective-permute-start(f32[8,256]{1,0:T(8,128)S(1)} %get-tuple-element.11), channel_id=1, source_target_pairs={{1,2},{2,1},{3,4},{4,3},{5,6},{6,5},{7,8},{8,7},{9,10},{10,9},{11,... | collective-permute-start | bytes 24584 | tf_op jit(solution)/shard_map/ppermute | solution.py:347
  18.8 22.2 %all-to-all-start = ((f32[8,168,128]{2,1,0:T(8,128)}), f32[8,168,128]{2,1,0:T(8,128)}, u32[]{:S(2)}, u32[]{:S(2)}) async-start(f32[8,168,128]{2,1,0:T(8,128)} %shard_map.96), calls=%async_computation | async-start | bytes 1376256 | tf_op jit(solution)/shard_map/all_to_all | solution.py:351
  24.6 1.8 %copy-start = (bf16[1280,1344]{1,0:T(8,128)(2,1)}, bf16[1280,1344]{1,0:T(8,128)(2,1)S(1)}, u32[]{:S(2)}) copy-start(bf16[1280,1344]{1,0:T(8,128)(2,1)S(1)} %get-tuple-element.12.stacked_ref) | copy-start | bytes 10321924
  26.4 1.2 %copy-start.2 = (bf16[1344,640]{1,0:T(8,128)(2,1)}, bf16[1344,640]{1,0:T(8,128)(2,1)S(1)}, u32[]{:S(2)}) copy-start(bf16[1344,640]{1,0:T(8,128)(2,1)S(1)} %get-tuple-element.13.turned_ref) | copy-start | bytes 5160964
  27.6 0.9 copy-start.5
  41.0 10.8 %copy-start.6 = (s32[6144]{0:T(1024)S(1)}, s32[6144]{0:T(1024)}, u32[]{:S(2)}) copy-start(s32[6144]{0:T(1024)} %param.15) | copy-start | bytes 73732
  48.1 3.9 %copy-start.8 = (s32[64]{0:T(128)S(1)}, s32[64]{0:T(128)}, u32[]{:S(2)}) copy-start(s32[64]{0:T(128)} %param.14) | copy-start | bytes 772
  48.2 23.0 %all-to-all-start.1 = ((f32[8,168,128]{2,1,0:T(8,128)}), f32[8,168,128]{2,1,0:T(8,128)S(1)}, u32[]{:S(2)}, u32[]{:S(2)}) async-start(f32[8,168,128]{2,1,0:T(8,128)} %bitcast.20), calls=%async_computation.1 | async-start | bytes 1376256 | tf_op jit(solution)/shard_map/all_to_all | solution.py:389
  100.7 15.2 %all-to-all-start.3 = ((f32[64,4,128]{2,1,0:T(4,128)}), f32[64,4,128]{2,1,0:T(4,128)S(1)}, u32[]{:S(2)}, u32[]{:S(2)}) async-start(f32[64,4,128]{2,1,0:T(4,128)} %bitcast.9), calls=%async_computation.3 | async-start | bytes 262144 | tf_op jit(solution)/shard_map/all_to_all | solution.py:396

commit v8 on v7

--- a/solution.py
+++ b/solution.py
@@ -175,9 +175,10 @@
     half = both_ref.shape[0] // 2
     loads = ((packed_ref, slab_ref), (stacked_ref, both_ref), (turned_ref, turned_a_ref), (gains_ref, gain_ref))
     copies = [pltpu.make_async_copy(source, target, sems.at[i]) for i, (source, target) in enumerate(loads)]
-    for copy in copies:
+    copies[0].start()
+    copies[0].wait()
+    for copy in copies[1:]:
         copy.start()
-    copies[0].wait()
     lane = iota((rows - LANES, LANES), 1)
     columns = jnp.concatenate([slab_ref[(g + 1) * rows - 8:(g + 1) * rows, :] for g in range(groups)] + [jnp.zeros((LANES - 8 * groups, LANES), F32)], axis=0).T
     for g in range(groups):

time: 117 us -> 118 us (level)
  no operation moved by 1% of the time
where the time goes in v8:
time: 118 us
  waiting for transfers between devices  43.1 us (37%)
  blocking collectives  27.5 us (23%)
  starting transfers between devices  23.6 us (20%)
  Pallas kernels  15.4 us (13%)
  local copies, waits for them, and re-layouts  6.6 us (6%)
    all_to_all x1, blocking collectives, per_device(): sent = lax.all_to_all(sent, 'pts', split_axis=0, concat_axis=0, tiled=True)  27.5 us
    all_to_all x1, waiting for transfers between devices, per_device(): lax.all_to_all(result, 'comp', split_axis=0, concat_axis=0, tiled=True)  18.5 us
    all_to_all x1, waiting for transfers between devices, per_device(): lax.all_to_all(slabs, 'comp', split_axis=0, concat_axis=0, tiled=True)  12.5 us
    all_to_all x1, waiting for transfers between devices, per_device(): sent = lax.all_to_all(sent, 'pts', split_axis=0, concat_axis=0, tiled=True)  9.12 us
    ppermute x1, starting transfers between devices, per_device(): lax.ppermute(swap, 'pts', [pair for i, j in both_ways[0::2] for pair in (...  9.01 us
    pallas_call x1, Pallas kernels, per_device(): call(functools.partial(steps_body, comps=comps), wide, (HBM, HBM, HBM, HB...  8.08 us
    unnamed x20, local copies, waits for them, and re-layouts  6.01 us
    all_to_all x1, starting transfers between devices, per_device(): sent = lax.all_to_all(sent, 'pts', split_axis=0, concat_axis=0, tiled=True)  4.88 us
  transfers between devices with their start and end apart: 5, of which 4 were waited for; matrix products, arithmetic and copies ran while one was open for 1% of the time, Pallas kernels for 2%

profile of v8, /device:TPU:1, one launch (start us, length us, event | category | flops | bytes accessed | tf_op | source)
XLA Modules:
  0.0 117.9 jit_solution(9040886768191145401)
XLA Ops:
  0.6 0.7 pad_add_fusion
  1.4 0.0 copy-start.1
  1.4 1.1 copy-done.1
  2.5 0.0 copy-start.7
  2.5 0.0 copy-start.3
  2.5 0.0 copy-start.4
  2.5 0.1 shard_map.95
  2.6 9.0 %collective-permute-start = (f32[8,256]{1,0:T(8,128)S(1)}, f32[8,256]{1,0:T(8,128)S(1)}, u32[]{:S(2)}, u32[]{:S(2)}) collective-permute-start(f32[8,256]{1,0:T(8,128)S(1)} %get-tuple-element.10), channel_id=1, source_target_pairs={{0,1},{1,0},{2,3},{3,2},{4,5},{5,4},{6,7},{7,6},{8,9},{9,8},{10,11... | collective-permute-start | bytes 24584 | tf_op jit(solution)/shard_map/ppermute | solution.py:347
  11.6 1.9 %collective-permute-start.1 = (f32[8,256]{1,0:T(8,128)S(1)}, f32[8,256]{1,0:T(8,128)S(1)}, u32[]{:S(2)}, u32[]{:S(2)}) collective-permute-start(f32[8,256]{1,0:T(8,128)S(1)} %get-tuple-element.11), channel_id=1, source_target_pairs={{1,2},{2,1},{3,4},{4,3},{5,6},{6,5},{7,8},{8,7},{9,10},{10,9},{11,... | collective-permute-start | bytes 24584 | tf_op jit(solution)/shard_map/ppermute | solution.py:348
  13.5 0.0 collective-permute-done.pair_ref
  13.6 3.0 %collective-permute-done.1.next_ref = f32[8,256]{1,0:T(8,128)S(1)} collective-permute-done((f32[8,256]{1,0:T(8,128)S(1)}, f32[8,256]{1,0:T(8,128)S(1)}, u32[]{:S(2)}, u32[]{:S(2)}) %collective-permute-start.1) | collective-permute-done | bytes 8224 | tf_op jit(solution)/shard_map/ppermute | solution.py:348
  16.6 2.2 %shard_map.96 = f32[8,168,128]{2,1,0:T(8,128)} custom-call(s32[1,128]{1,0:T(1,128)S(1)} %broadcast_in_dim.6.block_ref, f32[162,1024]{1,0:T(8,128)S(1)} %copy-done.1, f32[2,1024]{1,0:T(2,128)S(1)} %reshape.32.side_ref, f32[8,256]{1,0:T(8,128)S(1)} %collective-permute-done.pair_ref, f32[8,256]{1,0:T(8,128)S(1)} %collective-permute-done.1.next_ref), custom_call_target="tpu_custom_call" | custom-call | flops 1000000 | bytes 1000000 | tf_op jit(solution)/shard_map/pallas_call | solution.py:349
  18.8 4.2 %all-to-all-start = ((f32[8,168,128]{2,1,0:T(8,128)}), f32[8,168,128]{2,1,0:T(8,128)}, u32[]{:S(2)}, u32[]{:S(2)}) async-start(f32[8,168,128]{2,1,0:T(8,128)} %shard_map.96), calls=%async_computation | async-start | bytes 1376256 | tf_op jit(solution)/shard_map/all_to_all | solution.py:352
  23.0 0.0 copy-done.7
  23.0 0.0 copy-done.3
  23.0 0.0 copy-done.4
  23.0 1.6 %shard_map.97 = (bf16[1280,1344]{1,0:T(8,128)(2,1)S(1)}, bf16[1344,640]{1,0:T(8,128)(2,1)S(1)}, f32[1344,128]{1,0:T(8,128)S(1)}) custom-call(bf16[1296,640]{1,0:T(8,128)(2,1)S(1)} %bitcast.15, bf16[1296,640]{1,0:T(8,128)(2,1)S(1)} %bitcast.16, f32[1,1296]{1,0:T(1,128)S(1)} %reshape.34.growth_ref), custom_call_target="tpu_custom_call" | custom-call | flops 1000000 | bytes 1000000 | tf_op jit(solution)/shard_map/pallas_call | solution.py:365
  24.6 0.0 copy-start
  24.6 1.8 %copy-done = bf16[1280,1344]{1,0:T(8,128)(2,1)} copy-done((bf16[1280,1344]{1,0:T(8,128)(2,1)}, bf16[1280,1344]{1,0:T(8,128)(2,1)S(1)}, u32[]{:S(2)}) %copy-start) | copy-done | bytes 3440664
  26.4 0.0 copy-start.2
  26.4 1.2 %copy-done.2 = bf16[1344,640]{1,0:T(8,128)(2,1)} copy-done((bf16[1344,640]{1,0:T(8,128)(2,1)}, bf16[1344,640]{1,0:T(8,128)(2,1)S(1)}, u32[]{:S(2)}) %copy-start.2) | copy-done | bytes 1720344
  27.6 0.0 copy-start.5
  27.6 0.9 copy-done.5
  28.5 12.5 %all-to-all-done = f32[8,168,128]{2,1,0:T(8,128)} async-done(((f32[8,168,128]{2,1,0:T(8,128)}), f32[8,168,128]{2,1,0:T(8,128)}, u32[]{:S(2)}, u32[]{:S(2)}) %all-to-all-start) | async-done | bytes 688160 | tf_op jit(solution)/shard_map/all_to_all | solution.py:352
  41.0 0.0 copy-start.6
  41.0 8.1 %shard_map.98 = f32[1344,128]{1,0:T(8,128)} custom-call(f32[1344,128]{1,0:T(8,128)} %bitcast.packed_ref, bf16[1280,1344]{1,0:T(8,128)(2,1)} %copy-done, bf16[1344,640]{1,0:T(8,128)(2,1)} %copy-done.2, f32[1344,128]{1,0:T(8,128)} %copy-done.5), custom_call_target="tpu_custom_call" | custom-call | flops 1000000 | bytes 1000000 | tf_op jit(solution)/shard_map/pallas_call | solution.py:372
  49.0 0.0 copy-start.8
  49.1 3.6 %all-to-all-start.1 = ((f32[8,168,128]{2,1,0:T(8,128)}), f32[8,168,128]{2,1,0:T(8,128)S(1)}, u32[]{:S(2)}, u32[]{:S(2)}) async-start(f32[8,168,128]{2,1,0:T(8,128)} %bitcast.20), calls=%async_computation.1 | async-start | bytes 1376256 | tf_op jit(solution)/shard_map/all_to_all | solution.py:390
  52.6 0.0 copy-done.6
  52.6 0.1 reshape.38
  52.7 0.1 copy.12
  52.8 0.1 copy.14.offsets_ref
  52.9 0.0 copy-done.8
  52.9 0.1 copy.13.column_ref
  53.0 0.5 shard_map.99
  53.5 18.5 %all-to-all-done.1.slab_ref = f32[8,168,128]{2,1,0:T(8,128)S(1)} async-done(((f32[8,168,128]{2,1,0:T(8,128)}), f32[8,168,128]{2,1,0:T(8,128)S(1)}, u32[]{:S(2)}, u32[]{:S(2)}) %all-to-all-start.1) | async-done | bytes 688160 | tf_op jit(solution)/shard_map/all_to_all | solution.py:390
  72.0 0.9 shard_map.100
  73.0 27.5 %all_to_all.32 = f32[64,4,128]{2,1,0:T(4,128)S(1)} all-to-all(f32[64,4,128]{2,1,0:T(4,128)S(1)} %bitcast.19), channel_id=1, replica_groups=mesh['comp'=8,'pts'=64] {'pts'}, dimensions={0} | all-to-all | bytes 262144 | tf_op jit(solution)/shard_map/all_to_all | solution.py:394
  100.5 1.1 shard_map.101
  101.6 4.9 %all-to-all-start.3 = ((f32[64,4,128]{2,1,0:T(4,128)}), f32[64,4,128]{2,1,0:T(4,128)S(1)}, u32[]{:S(2)}, u32[]{:S(2)}) async-start(f32[64,4,128]{2,1,0:T(4,128)} %bitcast.9), calls=%async_computation.3 | async-start | bytes 262144 | tf_op jit(solution)/shard_map/all_to_all | solution.py:397
  106.6 0.1 copy.11
  106.8 1.0 copy.15
  107.7 9.1 %all-to-all-done.3 = f32[64,4,128]{2,1,0:T(4,128)S(1)} async-done(((f32[64,4,128]{2,1,0:T(4,128)}), f32[64,4,128]{2,1,0:T(4,128)S(1)}, u32[]{:S(2)}, u32[]{:S(2)}) %all-to-all-start.3) | async-done | bytes 131104 | tf_op jit(solution)/shard_map/all_to_all | solution.py:397
  116.8 1.0 shard_map.102
  (7 shorter events, 0.2 us)
Async XLA Ops:
  1.4 1.1 copy-start.1
  2.5 20.5 %copy-start.7 = (f32[1296]{0:T(1024)S(1)}, f32[1296]{0:T(1024)}, u32[]{:S(2)}) copy-start(f32[1296]{0:T(1024)} %param.10) | copy-start | bytes 15556
  2.5 20.6 %copy-start.3 = (bf16[640,1296]{0,1:T(8,128)(2,1)S(1)}, bf16[640,1296]{0,1:T(8,128)(2,1)}, u32[]{:S(2)}) copy-start(bf16[640,1296]{0,1:T(8,128)(2,1)} %param.11) | copy-start | bytes 4976644
  2.5 20.6 %copy-start.4 = (bf16[640,1296]{0,1:T(8,128)(2,1)S(1)}, bf16[640,1296]{0,1:T(8,128)(2,1)}, u32[]{:S(2)}) copy-start(bf16[640,1296]{0,1:T(8,128)(2,1)} %param.12) | copy-start | bytes 4976644
  2.6 11.0 %collective-permute-start = (f32[8,256]{1,0:T(8,128)S(1)}, f32[8,256]{1,0:T(8,128)S(1)}, u32[]{:S(2)}, u32[]{:S(2)}) collective-permute-start(f32[8,256]{1,0:T(8,128)S(1)} %get-tuple-element.10), channel_id=1, source_target_pairs={{0,1},{1,0},{2,3},{3,2},{4,5},{5,4},{6,7},{7,6},{8,9},{9,8},{10,11... | collective-permute-start | bytes 24584 | tf_op jit(solution)/shard_map/ppermute | solution.py:347
  11.6 5.0 %collective-permute-start.1 = (f32[8,256]{1,0:T(8,128)S(1)}, f32[8,256]{1,0:T(8,128)S(1)}, u32[]{:S(2)}, u32[]{:S(2)}) collective-permute-start(f32[8,256]{1,0:T(8,128)S(1)} %get-tuple-element.11), channel_id=1, source_target_pairs={{1,2},{2,1},{3,4},{4,3},{5,6},{6,5},{7,8},{8,7},{9,10},{10,9},{11,... | collective-permute-start | bytes 24584 | tf_op jit(solution)/shard_map/ppermute | solution.py:348
  18.8 22.2 %all-to-all-start = ((f32[8,168,128]{2,1,0:T(8,128)}), f32[8,168,128]{2,1,0:T(8,128)}, u32[]{:S(2)}, u32[]{:S(2)}) async-start(f32[8,168,128]{2,1,0:T(8,128)} %shard_map.96), calls=%async_computation | async-start | bytes 1376256 | tf_op jit(solution)/shard_map/all_to_all | solution.py:352
  24.6 1.8 %copy-start = (bf16[1280,1344]{1,0:T(8,128)(2,1)}, bf16[1280,1344]{1,0:T(8,128)(2,1)S(1)}, u32[]{:S(2)}) copy-start(bf16[1280,1344]{1,0:T(8,128)(2,1)S(1)} %get-tuple-element.12.stacked_ref) | copy-start | bytes 10321924
  26.4 1.2 %copy-start.2 = (bf16[1344,640]{1,0:T(8,128)(2,1)}, bf16[1344,640]{1,0:T(8,128)(2,1)S(1)}, u32[]{:S(2)}) copy-start(bf16[1344,640]{1,0:T(8,128)(2,1)S(1)} %get-tuple-element.13.turned_ref) | copy-start | bytes 5160964
  27.6 0.9 copy-start.5
  41.0 11.7 %copy-start.6 = (s32[6144]{0:T(1024)S(1)}, s32[6144]{0:T(1024)}, u32[]{:S(2)}) copy-start(s32[6144]{0:T(1024)} %param.15) | copy-start | bytes 73732
  49.0 3.9 %copy-start.8 = (s32[64]{0:T(128)S(1)}, s32[64]{0:T(128)}, u32[]{:S(2)}) copy-start(s32[64]{0:T(128)} %param.14) | copy-start | bytes 772
  49.1 23.0 %all-to-all-start.1 = ((f32[8,168,128]{2,1,0:T(8,128)}), f32[8,168,128]{2,1,0:T(8,128)S(1)}, u32[]{:S(2)}, u32[]{:S(2)}) async-start(f32[8,168,128]{2,1,0:T(8,128)} %bitcast.20), calls=%async_computation.1 | async-start | bytes 1376256 | tf_op jit(solution)/shard_map/all_to_all | solution.py:390
  101.6 15.2 %all-to-all-start.3 = ((f32[64,4,128]{2,1,0:T(4,128)}), f32[64,4,128]{2,1,0:T(4,128)S(1)}, u32[]{:S(2)}, u32[]{:S(2)}) async-start(f32[64,4,128]{2,1,0:T(4,128)} %bitcast.9), calls=%async_computation.3 | async-start | bytes 262144 | tf_op jit(solution)/shard_map/all_to_all | solution.py:397
